TPU v7x, 128 devices: a whole 4x4x4 slice. The times are simulated.
128 devices in a mesh: tm: 2 (over core), rows: 64 (over z, x, y).
Axes of the slice: x: 4, y: 4, z: 4, core: 2. Of those that a mesh axis runs over, the one named last changes fastest.
Arguments:
- feat: bfloat16 [4, 128, 240, 512], P('tm', 'rows'), may hold values from -24 to 24
- norm1_gain: float32 [512], replicated, may hold values from 0.5 to 1.5
- norm1_bias: float32 [512], replicated, may hold values from -3 to 3
- conv_weight: bfloat16 [3, 3, 3, 512, 512], replicated, may hold values from -0.0546875 to 0.0546875
- conv_bias: float32 [512], replicated, may hold values from -3 to 3
- norm2_gain: float32 [512], replicated, may hold values from 0.5 to 1.5
- norm2_bias: float32 [512], replicated, may hold values from -3 to 3
- w_query: bfloat16 [512, 512], replicated, may hold values from -0.44194174 to 0.44194174
- w_key: bfloat16 [512, 512], replicated, may hold values from -1.5467961 to 1.5467961
- w_value: bfloat16 [512, 512], replicated, may hold values from -0.25 to 0.25
- w_out: bfloat16 [512, 512], replicated, may hold values from -0.25 to 0.25
- out_bias: float32 [512], replicated, may hold values from -3 to 3
Outputs:
- block_out: bfloat16 [4, 128, 240, 512], P('tm', 'rows')
All inputs are finite; a program needn't handle non-finite values.
Results may differ from a plain program's by a relative error of at most 0.0062.
The roundings to bfloat16 on the way count: a program that leaves them out, or rounds other values in their place, can miss the bound.
Values may be sent and summed in bfloat16 or wider, within the bound.
No kernel may reach another device: no remote copies, remote signals or barrier semaphores. Data moves between devices by JAX's collectives and lax.ppermute only.
A program may use at most 128 MiB of HBM per device.

v0:
```python
import math

import jax
import jax.numpy as jnp
from jax import lax
from jax.sharding import PartitionSpec as P

GROUPS = 32
RADIUS = 4


EPS = 1e-06


def from_behind(array, axis, by):
    peers = lax.axis_size(axis)
    pairs = [(i, i + by) for i in range(peers) if 0 <= i + by < peers]
    return lax.ppermute(array, axis, pairs)


def padded_2(cells, sides, width):
    for axis, dim in sides:
        count = lax.axis_size(axis)
        ends = count - 1
        head = lax.slice_in_dim(cells, 0, width, axis=dim)
        tail = lax.slice_in_dim(cells, cells.shape[dim] - width, cells.shape[dim], axis=dim)
        cells = jnp.concatenate(
            [
                lax.ppermute(tail, axis, [(i, (i + 1) % count) for i in range(ends)]),
                cells,
                lax.ppermute(head, axis, [((i + 1) % count, i) for i in range(ends)]),
            ],
            axis=dim,
        )
    return cells


def group_norm(values, gain, shift, count):
    chans = values.shape[-1]
    grouped = values.reshape(values.shape[:-1] + (GROUPS, chans // GROUPS))
    local_sum = jnp.sum(grouped, axis=(0, 1, 2, 4))
    mean = lax.psum(local_sum, ("tm", "rows")) / count
    centered = grouped - mean[:, None]
    spread = lax.psum(jnp.sum(centered * centered, axis=(0, 1, 2, 4)), ("tm", "rows")) / count
    normed = centered * lax.rsqrt(spread + EPS)[:, None]
    return normed.reshape(values.shape) * gain + shift


def conv_taps(padded, weight, frames, height, width):
    chans = padded.shape[-1]
    total = jnp.zeros((frames * height * width, weight.shape[-1]), jnp.float32)
    for step_t in range(3):
        for step_h in range(3):
            slab = padded[step_t : step_t + frames, step_h : step_h + height]
            stacked = jnp.concatenate(
                [slab[:, :, step_w : step_w + width] for step_w in range(3)], axis=-1
            )
            total = total + jnp.dot(
                stacked.reshape(-1, 3 * chans),
                weight[step_t, step_h].reshape(3 * chans, -1),
                preferred_element_type=jnp.float32,
            )
    return total.reshape(frames, height, width, -1)


def project(flat, weight):
    return jnp.dot(flat, weight, preferred_element_type=jnp.float32).astype(jnp.bfloat16)


def shards(
    feat,
    norm1_gain,
    norm1_bias,
    conv_weight,
    conv_bias,
    norm2_gain,
    norm2_bias,
    w_query,
    w_key,
    w_value,
    w_out,
    out_bias,
):
    frames, stripe_rows, width, chans = feat.shape
    stripes = lax.axis_size("rows")
    count = lax.axis_size("tm") * stripes * frames * stripe_rows * width * (chans // GROUPS)
    act = jax.nn.silu(group_norm(feat.astype(jnp.float32), norm1_gain, norm1_bias, count)).astype(
        jnp.bfloat16
    )
    earlier = from_behind(act, "tm", 1)
    opening = jnp.broadcast_to(act[:1], earlier.shape)
    earlier = jnp.where(lax.axis_index("tm") == 0, opening, earlier)
    timed = jnp.concatenate([earlier, act], axis=0)
    rimmed = padded_2(timed, (("rows", 1),), 1)
    padded = jnp.pad(rimmed, ((0, 0), (0, 0), (1, 1), (0, 0)))
    conv = conv_taps(padded, conv_weight, frames, stripe_rows, width) + conv_bias
    resid = (feat.astype(jnp.float32) + conv).astype(jnp.bfloat16)
    normed = group_norm(resid.astype(jnp.float32), norm2_gain, norm2_bias, count).astype(
        jnp.bfloat16
    )
    flat = normed.reshape(-1, chans)
    query = project(flat, w_query).reshape(frames, -1, chans)
    reach = RADIUS * stripe_rows
    paired = jnp.stack([project(flat, w_key), project(flat, w_value)]).reshape(
        2, frames, stripe_rows, width, chans
    )
    pieces = []
    for offset in range(-RADIUS, RADIUS + 1):
        if offset == 0:
            pieces.append(paired)
        else:
            pieces.append(from_behind(paired, "rows", -offset))
    wide = jnp.concatenate(pieces, axis=2)
    keys = wide[0].reshape(frames, -1, chans)
    values = wide[1].reshape(frames, -1, chans)
    span = 2 * reach + stripe_rows
    place = lax.axis_index("rows") * stripe_rows - reach + jnp.arange(span, dtype=jnp.int32)
    valid = jnp.repeat((place >= 0) & (place < stripes * stripe_rows), width)
    scale = 1.0 / math.sqrt(chans)
    scores = jnp.einsum("fqc,fkc->fqk", query, keys, preferred_element_type=jnp.float32) * scale
    scores = jnp.where(valid[None, None, :], scores, jnp.float32(-1e30))
    top = jnp.max(scores, axis=-1, keepdims=True)
    expo = jnp.exp(scores - top)
    total = jnp.sum(expo, axis=-1, keepdims=True)
    mixed = jnp.einsum(
        "fqk,fkc->fqc", expo.astype(jnp.bfloat16), values, preferred_element_type=jnp.float32
    )
    attn = (mixed / total).astype(jnp.bfloat16).reshape(-1, chans)
    output = jnp.dot(attn, w_out, preferred_element_type=jnp.float32).reshape(
        frames, stripe_rows, width, chans
    )
    return (resid.astype(jnp.float32) + out_bias + output).astype(jnp.bfloat16)


def solution(mesh):
    return jax.shard_map(
        shards,
        mesh=mesh,
        in_specs=(
            P("tm", "rows", None, None),
            P(),
            P(),
            P(),
            P(),
            P(),
            P(),
            P(),
            P(),
            P(),
            P(),
            P(),
        ),
        out_specs=P("tm", "rows", None, None),
        check_vma=False,
    )
```

profile of v0, /device:TPU:33, one launch (start us, length us, event | category | flops | bytes accessed | tf_op | source)
XLA Modules:
  0.0 672.4 jit_solution(8682278299150185639)
XLA Ops:
  0.0 1.5 convert_reduce_fusion.1
  1.7 65.9 %psum.28 = f32[32]{0:T(128)S(1)} all-reduce(f32[32]{0:T(128)S(1)} %reduce_sum.59), channel_id=1, replica_groups=mesh['tm'=2,'rows'=64] {'tm','rows'}, use_global_device_ids=true, to_apply=%region_2.0 | all-reduce | flops 32 | bytes 256 | tf_op jit(solution)/shard_map/psum | solution.py:42
  67.7 1.5 fusion.23
  69.4 63.8 %psum.29 = f32[32]{0:T(128)S(1)} all-reduce(f32[32]{0:T(128)S(1)} %reduce_sum.62), channel_id=1, replica_groups=mesh['tm'=2,'rows'=64] {'tm','rows'}, use_global_device_ids=true, to_apply=%region_5.6 | all-reduce | flops 32 | bytes 256 | tf_op jit(solution)/shard_map/psum | solution.py:44
  133.4 1.9 fusion.31
  135.3 1.3 collective-permute-start
  136.7 3.1 collective-permute-done
  140.1 1.9 collective-permute-start.1
  142.0 7.8 %collective-permute-start.2 = (bf16[4,1,240,512]{3,2,1,0:T(8,128)(2,1)S(1)}, bf16[4,1,240,512]{3,2,1,0:T(8,128)(2,1)S(1)}, u32[]{:S(2)}, u32[]{:S(2)}) collective-permute-start(bf16[4,1,240,512]{3,2,1,0:T(8,128)(2,1)S(1)} %get-tuple-element.45), channel_id=1, source_target_pairs={{1,0},{2,1},{3,2},{4,3},{5,4},{6,5},{7,6},{8,7},{9,8},{10,9},{11,1... | collective-permute-start | bytes 2949128 | tf_op jit(solution)/shard_map/ppermute | solution.py:31
  149.8 9.3 %fusion.44 = (bf16[1,1,3,512,512]{4,3,2,1,0:T(8,128)(2,1)S(1)}, bf16[1,1,3,512,512]{4,3,2,1,0:T(8,128)(2,1)}, bf16[1,1,3,512,512]{4,3,2,1,0:T(8,128)(2,1)}, bf16...) fusion(bf16[3,3,3,512,512]{4,3,2,1,0:T(8,128)(2,1)} %param.15), kind=kLoop, calls=%fused_computation.89 | loop fusion | bytes 28311552 | tf_op jit(solution)/shard_map/slice | solution.py:60
  159.0 10.4 %collective-permute-done.1 = bf16[4,1,240,512]{3,2,1,0:T(8,128)(2,1)S(1)} collective-permute-done((bf16[4,1,240,512]{3,2,1,0:T(8,128)(2,1)S(1)}, bf16[4,1,240,512]{3,2,1,0:T(8,128)(2,1)S(1)}, u32[]{:S(2)}, u32[]{:S(2)}) %collective-permute-start.1) | collective-permute-done | bytes 983072 | tf_op jit(solution)/shard_map/ppermute | solution.py:29
  169.4 0.9 collective-permute-done.2
  170.3 2.1 select_maximum_fusion
  172.3 6.3 fusion.45
  178.6 0.6 pad_maximum_fusion.3
  179.8 0.9 copy-done.10
  182.0 1.0 copy-done.21
  183.0 1.7 fusion.48
  184.7 1.7 fusion.50
  186.8 0.5 pad_maximum_fusion.5
  187.3 0.9 copy-done.19
  188.2 1.7 fusion.51
  189.9 1.7 fusion.53
  191.6 0.4 pad_maximum_fusion.7
  192.0 1.0 copy-done.17
  193.0 1.7 fusion.54
  194.7 0.9 pad_maximum_fusion.2
  195.6 0.5 copy-done.16
  196.1 1.7 fusion.49
  197.8 1.7 fusion.52
  199.5 1.7 fusion.55
  201.2 2.5 add_add_fusion
  204.3 66.9 %psum.30 = f32[32]{0:T(128)S(1)} all-reduce(f32[32]{0:T(128)S(1)} %reduce_sum.81), channel_id=1, replica_groups=mesh['tm'=2,'rows'=64] {'tm','rows'}, use_global_device_ids=true, to_apply=%region_8.9 | all-reduce | flops 32 | bytes 256 | tf_op jit(solution)/shard_map/psum | solution.py:42
  272.0 62.4 %psum.31 = f32[32]{0:T(128)S(1)} all-reduce(f32[32]{0:T(128)S(1)} %reduce_sum.84), channel_id=1, replica_groups=mesh['tm'=2,'rows'=64] {'tm','rows'}, use_global_device_ids=true, to_apply=%region_11.12 | all-reduce | flops 32 | bytes 256 | tf_op jit(solution)/shard_map/psum | solution.py:44
  334.9 0.7 convolution_convert_fusion.1
  335.6 1.7 convolution_convert_fusion
  337.3 1.5 pad_maximum_fusion.10
  338.8 2.4 collective-permute-start.3
  341.3 3.1 collective-permute-start.4
  344.3 3.2 collective-permute-start.5
  347.5 1.9 collective-permute-start.6
  349.4 7.6 %collective-permute-start.7 = (bf16[2,2,2,240,512]{4,3,2,1,0:T(8,128)(2,1)}, bf16[2,2,2,240,512]{4,3,2,1,0:T(8,128)(2,1)}, u32[]{:S(2)}, u32[]{:S(2)}) collective-permute-start(bf16[2,2,2,240,512]{4,3,2,1,0:T(8,128)(2,1)} %pad_maximum_fusion.10), channel_id=1, source_target_pairs={{1,0},{2,1},{3,2},{4,3},{5,4},{6,5},{7,6},{8,7},{9,8},{10,9},{11,1... | collective-permute-start | bytes 5898248 | tf_op jit(solution)/shard_map/ppermute | solution.py:18
  357.0 29.8 %collective-permute-done.3 = bf16[2,2,2,240,512]{4,3,2,1,0:T(8,128)(2,1)} collective-permute-done((bf16[2,2,2,240,512]{4,3,2,1,0:T(8,128)(2,1)}, bf16[2,2,2,240,512]{4,3,2,1,0:T(8,128)(2,1)}, u32[]{:S(2)}, u32[]{:S(2)}) %collective-permute-start.3) | collective-permute-done | bytes 1966112 | tf_op jit(solution)/shard_map/ppermute | solution.py:18
  386.9 2.9 collective-permute-start.8
  389.7 122.3 %collective-permute-done.4 = bf16[2,2,2,240,512]{4,3,2,1,0:T(8,128)(2,1)} collective-permute-done((bf16[2,2,2,240,512]{4,3,2,1,0:T(8,128)(2,1)}, bf16[2,2,2,240,512]{4,3,2,1,0:T(8,128)(2,1)}, u32[]{:S(2)}, u32[]{:S(2)}) %collective-permute-start.4) | collective-permute-done | bytes 1966112 | tf_op jit(solution)/shard_map/ppermute | solution.py:18
  512.0 1.9 collective-permute-start.9
  513.9 1.9 collective-permute-start.10
  516.0 2.7 convolution_convert_fusion.2
  518.8 1.7 constant_dynamic-update-slice_fusion.8
  520.4 1.7 constant_dynamic-update-slice_fusion.7
  522.1 1.7 constant_dynamic-update-slice_fusion.6
  523.8 13.2 %collective-permute-done.6 = bf16[2,2,2,240,512]{4,3,2,1,0:T(8,128)(2,1)} collective-permute-done((bf16[2,2,2,240,512]{4,3,2,1,0:T(8,128)(2,1)}, bf16[2,2,2,240,512]{4,3,2,1,0:T(8,128)(2,1)}, u32[]{:S(2)}, u32[]{:S(2)}) %collective-permute-start.6) | collective-permute-done | bytes 1966112 | tf_op jit(solution)/shard_map/ppermute | solution.py:18
  537.0 1.7 constant_dynamic-update-slice_fusion.5
  538.8 1.7 constant_dynamic-update-slice_fusion.3
  540.5 1.7 constant_dynamic-update-slice_fusion.2
  542.2 49.7 %collective-permute-done.9 = bf16[2,2,2,240,512]{4,3,2,1,0:T(8,128)(2,1)} collective-permute-done((bf16[2,2,2,240,512]{4,3,2,1,0:T(8,128)(2,1)}, bf16[2,2,2,240,512]{4,3,2,1,0:T(8,128)(2,1)}, u32[]{:S(2)}, u32[]{:S(2)}) %collective-permute-start.9) | collective-permute-done | bytes 1966112 | tf_op jit(solution)/shard_map/ppermute | solution.py:18
  591.9 1.7 constant_dynamic-update-slice_fusion.1
  593.6 40.5 %collective-permute-done.10 = bf16[2,2,2,240,512]{4,3,2,1,0:T(8,128)(2,1)} collective-permute-done((bf16[2,2,2,240,512]{4,3,2,1,0:T(8,128)(2,1)}, bf16[2,2,2,240,512]{4,3,2,1,0:T(8,128)(2,1)}, u32[]{:S(2)}, u32[]{:S(2)}) %collective-permute-start.10) | collective-permute-done | bytes 1966112 | tf_op jit(solution)/shard_map/ppermute | solution.py:18
  634.1 1.7 constant_dynamic-update-slice_fusion
  635.7 4.3 fusion.43
  640.1 10.2 %fusion = (f32[2,480]{1,0:T(2,128)S(1)}, f32[2,480,4320]{2,1,0:T(8,128)}) fusion(pred[4320]{0:T(1024)(128)(4,1)S(1)} %broadcast_in_dim.35, bf16[2,480,512]{2,1,0:T(8,128)(2,1)} %bitcast.89, bf16[2,4320,512]{2,1,0:T(8,128)(2,1)S(1)} %bitcast.63), kind=kOutput, calls=%fused_computation.2 | convolution fusion | flops 4259173376 | bytes 26427360 | tf_op jit(solution)/shard_map/fqc,fkc->fqk/dot_general | solution.py:120
  650.2 9.5 %fusion.1 = f32[2,480]{1,0:T(2,128)S(1)} fusion(f32[2,480,4320]{2,1,0:T(8,128)} %get-tuple-element.50, f32[2,480]{1,0:T(2,128)S(1)} %get-tuple-element.49, pred[4320]{0:T(1024)(128)(4,1)S(1)} %broadcast_in_dim.35), kind=kLoop, calls=%fused_computation.3 | loop fusion | flops 16587840 | bytes 16600800 | tf_op jit(solution)/shard_map/reduce_sum | solution.py:124
  659.7 11.0 %divide_convert_fusion = bf16[2,480,512]{2,1,0:T(8,128)(2,1)S(1)} fusion(bf16[2,4320,512]{2,1,0:T(8,128)(2,1)} %bitcast.62, f32[2,480,4320]{2,1,0:T(8,128)} %get-tuple-element.50, f32[2,480]{1,0:T(2,128)S(1)} %get-tuple-element.49, pred[4320]{0:T(1024)(128)(4,1)S(1)} %broadcast_in_dim.35, f32[2,480]{1,0:T(2,128)S(1)} %fusion.1), kind=kOutput, calls=%fused_computation.62 | convolution fusion | flops 4264304640 | bytes 26431200 | tf_op jit(solution)/shard_map/fqk,fkc->fqc/dot_general | solution.py:125
  670.8 1.6 fusion.34
  (89 shorter events, 5.4 us)
Async XLA Ops:
  0.0 334.9 %copy-start = (bf16[512,512]{1,0:T(8,128)(2,1)S(1)}, bf16[512,512]{1,0:T(8,128)(2,1)}, u32[]{:S(2)}) copy-start(bf16[512,512]{1,0:T(8,128)(2,1)} %param.20) | copy-start | bytes 1572868
  135.3 4.5 collective-permute-start
  140.1 29.3 %collective-permute-start.1 = (bf16[4,1,240,512]{3,2,1,0:T(8,128)(2,1)S(1)}, bf16[4,1,240,512]{3,2,1,0:T(8,128)(2,1)S(1)}, u32[]{:S(2)}, u32[]{:S(2)}) collective-permute-start(bf16[4,1,240,512]{3,2,1,0:T(8,128)(2,1)S(1)} %get-tuple-element.44), channel_id=1, source_target_pairs={{0,1},{1,2},{2,3},{3,4},{4,5},{5,6},{6,7},{7,8},{8,9},{9,10},{10,1... | collective-permute-start | bytes 2949128 | tf_op jit(solution)/shard_map/ppermute | solution.py:29
  142.0 28.3 %collective-permute-start.2 = (bf16[4,1,240,512]{3,2,1,0:T(8,128)(2,1)S(1)}, bf16[4,1,240,512]{3,2,1,0:T(8,128)(2,1)S(1)}, u32[]{:S(2)}, u32[]{:S(2)}) collective-permute-start(bf16[4,1,240,512]{3,2,1,0:T(8,128)(2,1)S(1)} %get-tuple-element.45), channel_id=1, source_target_pairs={{1,0},{2,1},{3,2},{4,3},{5,4},{6,5},{7,6},{8,7},{9,8},{10,9},{11,1... | collective-permute-start | bytes 2949128 | tf_op jit(solution)/shard_map/ppermute | solution.py:31
  179.5 1.2 copy-start.10
  179.5 1.5 copy-start.11
  179.5 1.8 copy-start.12
  179.5 2.1 copy-start.13
  181.6 1.4 copy-start.21
  183.0 1.7 copy-start.20
  184.7 1.7 copy-start.6
  184.7 1.7 copy-start.7
  184.7 1.8 copy-start.8
  184.7 2.1 copy-start.9
  186.8 1.4 copy-start.19
  188.2 1.7 copy-start.18
  189.9 1.7 copy-start.5
  191.6 1.4 copy-start.17
  194.7 1.4 copy-start.16
  196.1 1.7 copy-start.15
  197.8 1.7 copy-start.14
  201.2 2.5 copy-start.2
  201.2 2.5 copy-start.24
  203.7 130.8 %copy-start.25 = (f32[512]{0:T(512)S(1)}, f32[512]{0:T(512)}, u32[]{:S(2)}) copy-start(f32[512]{0:T(512)} %param.18) | copy-start | bytes 6148
  203.7 130.8 %copy-start.26 = (f32[512]{0:T(512)S(1)}, f32[512]{0:T(512)}, u32[]{:S(2)}) copy-start(f32[512]{0:T(512)} %param.17) | copy-start | bytes 6148
  204.1 131.5 %copy-start.3 = (bf16[2,2,240,512]{3,2,1,0:T(8,128)(2,1)}, bf16[2,2,240,512]{3,2,1,0:T(8,128)(2,1)S(1)}, u32[]{:S(2)}) copy-start(bf16[2,2,240,512]{3,2,1,0:T(8,128)(2,1)S(1)} %get-tuple-element.6) | copy-start | bytes 2949124
  334.9 2.4 copy-start.22
  337.3 178.7 %copy-start.23 = (bf16[2,2,240,512]{3,2,1,0:T(8,128)(2,1)S(1)}, bf16[2,2,240,512]{3,2,1,0:T(8,128)(2,1)}, u32[]{:S(2)}) copy-start(bf16[2,2,240,512]{3,2,1,0:T(8,128)(2,1)} %copy-done.22) | copy-start | bytes 2949124
  338.8 48.0 %collective-permute-start.3 = (bf16[2,2,2,240,512]{4,3,2,1,0:T(8,128)(2,1)}, bf16[2,2,2,240,512]{4,3,2,1,0:T(8,128)(2,1)}, u32[]{:S(2)}, u32[]{:S(2)}) collective-permute-start(bf16[2,2,2,240,512]{4,3,2,1,0:T(8,128)(2,1)} %pad_maximum_fusion.10), channel_id=1, source_target_pairs={{0,4},{1,5},{2,6},{3,7},{4,8},{5,9},{6,10},{7,11},{8,12},{9,13},{1... | collective-permute-start | bytes 5898248 | tf_op jit(solution)/shard_map/ppermute | solution.py:18
  341.3 170.7 %collective-permute-start.4 = (bf16[2,2,2,240,512]{4,3,2,1,0:T(8,128)(2,1)}, bf16[2,2,2,240,512]{4,3,2,1,0:T(8,128)(2,1)}, u32[]{:S(2)}, u32[]{:S(2)}) collective-permute-start(bf16[2,2,2,240,512]{4,3,2,1,0:T(8,128)(2,1)} %pad_maximum_fusion.10), channel_id=1, source_target_pairs={{0,3},{1,4},{2,5},{3,6},{4,7},{5,8},{6,9},{7,10},{8,11},{9,12},{10... | collective-permute-start | bytes 5898248 | tf_op jit(solution)/shard_map/ppermute | solution.py:18
  344.3 169.6 %collective-permute-start.5 = (bf16[2,2,2,240,512]{4,3,2,1,0:T(8,128)(2,1)}, bf16[2,2,2,240,512]{4,3,2,1,0:T(8,128)(2,1)}, u32[]{:S(2)}, u32[]{:S(2)}) collective-permute-start(bf16[2,2,2,240,512]{4,3,2,1,0:T(8,128)(2,1)} %pad_maximum_fusion.10), channel_id=1, source_target_pairs={{0,2},{1,3},{2,4},{3,5},{4,6},{5,7},{6,8},{7,9},{8,10},{9,11},{10,... | collective-permute-start | bytes 5898248 | tf_op jit(solution)/shard_map/ppermute | solution.py:18
  347.5 189.5 %collective-permute-start.6 = (bf16[2,2,2,240,512]{4,3,2,1,0:T(8,128)(2,1)}, bf16[2,2,2,240,512]{4,3,2,1,0:T(8,128)(2,1)}, u32[]{:S(2)}, u32[]{:S(2)}) collective-permute-start(bf16[2,2,2,240,512]{4,3,2,1,0:T(8,128)(2,1)} %pad_maximum_fusion.10), channel_id=1, source_target_pairs={{0,1},{1,2},{2,3},{3,4},{4,5},{5,6},{6,7},{7,8},{8,9},{9,10},{10,1... | collective-permute-start | bytes 5898248 | tf_op jit(solution)/shard_map/ppermute | solution.py:18
  349.4 189.4 %collective-permute-start.7 = (bf16[2,2,2,240,512]{4,3,2,1,0:T(8,128)(2,1)}, bf16[2,2,2,240,512]{4,3,2,1,0:T(8,128)(2,1)}, u32[]{:S(2)}, u32[]{:S(2)}) collective-permute-start(bf16[2,2,2,240,512]{4,3,2,1,0:T(8,128)(2,1)} %pad_maximum_fusion.10), channel_id=1, source_target_pairs={{1,0},{2,1},{3,2},{4,3},{5,4},{6,5},{7,6},{8,7},{9,8},{10,9},{11,1... | collective-permute-start | bytes 5898248 | tf_op jit(solution)/shard_map/ppermute | solution.py:18
  386.9 153.7 %collective-permute-start.8 = (bf16[2,2,2,240,512]{4,3,2,1,0:T(8,128)(2,1)}, bf16[2,2,2,240,512]{4,3,2,1,0:T(8,128)(2,1)}, u32[]{:S(2)}, u32[]{:S(2)}) collective-permute-start(bf16[2,2,2,240,512]{4,3,2,1,0:T(8,128)(2,1)} %pad_maximum_fusion.10), channel_id=1, source_target_pairs={{2,0},{3,1},{4,2},{5,3},{6,4},{7,5},{8,6},{9,7},{10,8},{11,9},{12,... | collective-permute-start | bytes 5898248 | tf_op jit(solution)/shard_map/ppermute | solution.py:18
  512.0 80.0 %collective-permute-start.9 = (bf16[2,2,2,240,512]{4,3,2,1,0:T(8,128)(2,1)}, bf16[2,2,2,240,512]{4,3,2,1,0:T(8,128)(2,1)}, u32[]{:S(2)}, u32[]{:S(2)}) collective-permute-start(bf16[2,2,2,240,512]{4,3,2,1,0:T(8,128)(2,1)} %pad_maximum_fusion.10), channel_id=1, source_target_pairs={{3,0},{4,1},{5,2},{6,3},{7,4},{8,5},{9,6},{10,7},{11,8},{12,9},{13... | collective-permute-start | bytes 5898248 | tf_op jit(solution)/shard_map/ppermute | solution.py:18
  513.9 120.2 %collective-permute-start.10 = (bf16[2,2,2,240,512]{4,3,2,1,0:T(8,128)(2,1)}, bf16[2,2,2,240,512]{4,3,2,1,0:T(8,128)(2,1)}, u32[]{:S(2)}, u32[]{:S(2)}) collective-permute-start(bf16[2,2,2,240,512]{4,3,2,1,0:T(8,128)(2,1)} %pad_maximum_fusion.10), channel_id=1, source_target_pairs={{4,0},{5,1},{6,2},{7,3},{8,4},{9,5},{10,6},{11,7},{12,8},{13,9},{1... | collective-permute-start | bytes 5898248 | tf_op jit(solution)/shard_map/ppermute | solution.py:18
  659.7 11.1 %copy-start.4 = (bf16[2,2,240,512]{3,2,1,0:T(8,128)(2,1)S(1)}, bf16[2,2,240,512]{3,2,1,0:T(8,128)(2,1)}, u32[]{:S(2)}) copy-start(bf16[2,2,240,512]{3,2,1,0:T(8,128)(2,1)} %copy-done.3) | copy-start | bytes 2949124
  659.7 11.1 %copy-start.27 = (bf16[512,512]{1,0:T(8,128)(2,1)S(1)}, bf16[512,512]{1,0:T(8,128)(2,1)}, u32[]{:S(2)}) copy-start(bf16[512,512]{1,0:T(8,128)(2,1)} %param.22) | copy-start | bytes 1572868
  659.7 11.1 %copy-start.28 = (f32[512]{0:T(512)S(1)}, f32[512]{0:T(512)}, u32[]{:S(2)}) copy-start(f32[512]{0:T(512)} %param.23) | copy-start | bytes 6148
  659.7 12.7 %copy-start.1 = (bf16[512,512]{1,0:T(8,128)(2,1)S(1)}, bf16[512,512]{1,0:T(8,128)(2,1)}, u32[]{:S(2)}) copy-start(bf16[512,512]{1,0:T(8,128)(2,1)} %param.20) | copy-start | bytes 1572868
where the time goes:
time: 682 us; the launch traced here: 672 us
  waiting for transfers between devices  270 us (40%)
  blocking collectives  259 us (38%)
  matrix products  43.8 us (6%)
  local copies, waits for them, and re-layouts  40.4 us (6%)
  starting transfers between devices  35.9 us (5%)
  other arithmetic  22.8 us (3%)
    ppermute x9, waiting for transfers between devices, from_behind(): return lax.ppermute(array, axis, pairs)  259 us
    psum x2, blocking collectives, group_norm(): mean = lax.psum(local_sum, ('tm', 'rows')) / count  133 us
    psum x2, blocking collectives, group_norm(): lax.psum(jnp.sum(centered * centered, axis=(0, 1, 2, 4)), ('tm', 'rows'))  126 us
    ppermute x9, starting transfers between devices, from_behind(): return lax.ppermute(array, axis, pairs)  26.2 us
    unnamed x65, local copies, waits for them, and re-layouts  17.3 us
    dot_general x9, matrix products, conv_taps(): jnp.dot(stacked.reshape(-1, 3 * chans), weight[step_t, step_h].reshape(3...  15.9 us
  transfers between devices with their start and end apart: 11, of which 8 were waited for; matrix products, arithmetic and copies ran while one was open for 4% of the time, Pallas kernels for 0%

commit v1 on v0

v1 whole, which is shorter than its diff:
```python
import functools
import math

import jax
import jax.numpy as jnp
import numpy as np
from jax import lax
from jax.experimental import pallas as pl
from jax.experimental.pallas import tpu as pltpu
from jax.sharding import Mesh, PartitionSpec as P

GROUPS = 32
EPS = 1e-06
AXES = ("tm", "z", "x", "y")
NZ, NX, NY = 4, 4, 4
LOG2E = 1.4426950408889634
VMEM_LIMIT = 60 * 1024 * 1024
BF = jnp.bfloat16
F32 = jnp.float32


def lin(t, z, x, y):
    return ((t * NZ + z) * NX + x) * NY + y


def pairs_of(move):
    found = []
    for t in range(2):
        for z in range(NZ):
            for x in range(NX):
                for y in range(NY):
                    dest = move(t, z, x, y)
                    if dest is not None:
                        found.append((lin(t, z, x, y), lin(*dest)))
    return found


def send(value, move):
    return lax.ppermute(value, AXES, pairs_of(move))


def rows_by(step):
    def move(t, z, x, y):
        row = (z * NX + x) * NY + y + step
        if 0 <= row < NZ * NX * NY:
            return (t, row // (NX * NY), (row // NY) % NX, row % NY)
        return None

    return move


def blocks_by(step):
    def move(t, z, x, y):
        block = z * NX + x + step
        if 0 <= block < NZ * NX:
            return (t, block // NX, block % NX, y)
        return None

    return move


def turned(axis, step):
    def move(t, z, x, y):
        if axis == "tm":
            return (1 - t, z, x, y)
        if axis == "z":
            return (t, (z + step) % NZ, x, y)
        if axis == "x":
            return (t, z, (x + step) % NX, y)
        return (t, z, x, (y + step) % NY)

    return move


def to_frames(order):
    def move(t, z, x, y):
        return (y // 2, z, x, 2 * t + ((y + order) & 1))

    return move


def to_stripes(order):
    forward = to_frames(order)
    back = {}
    for t in range(2):
        for y in range(NY):
            dest = forward(t, 0, 0, y)
            back[(dest[0], dest[3])] = (t, y)

    def move(t, z, x, y):
        there = back[(t, y)]
        return (there[0], z, x, there[1])

    return move


def merge(parts):
    count = len(parts)
    mean = sum(p[0] for p in parts) / count
    spread = sum(p[1] for p in parts) / count
    away = sum((p[0] - mean) * (p[0] - mean) for p in parts) / count
    return jnp.stack([mean, spread + away])


def global_stats(stats):
    stats = merge([stats, send(stats, turned("tm", 1))])
    for axis in ("z", "x", "y"):
        stats = merge([stats] + [send(stats, turned(axis, k)) for k in (1, 2, 3)])
    return stats


def group_mean(row):
    chans = row.shape[-1]
    size = chans // GROUPS
    lane = lax.broadcasted_iota(jnp.int32, row.shape, 1)
    step = 1
    while step < size:
        low = (lane & step) == 0
        row = row + jnp.where(
            low, pltpu.roll(row, chans - step, 1), pltpu.roll(row, step, 1)
        )
        step *= 2
    return row / size


def local_stats(blocks, stat_ref):
    chans = stat_ref.shape[-1]
    cells = sum(b.shape[0] for b in [f() for f in blocks])
    total = sum(jnp.sum(f().astype(F32), axis=0, keepdims=True) for f in blocks)
    mean = group_mean(jnp.broadcast_to(total / cells, (8, chans)))
    center = mean[0:1]
    square = 0.0
    for f in blocks:
        away = f().astype(F32) - center
        square = square + jnp.sum(away * away, axis=0, keepdims=True)
    spread = group_mean(jnp.broadcast_to(square / cells, (8, chans)))
    stat_ref[0:1, :] = center
    stat_ref[1:2, :] = spread[0:1]


def edge_kernel(feat_ref, stat_ref, top_ref, low_ref):
    frames = feat_ref.shape[0]
    for f in range(frames):
        top_ref[f] = feat_ref[f, 0]
        low_ref[f] = feat_ref[f, 1]
    local_stats(
        [functools.partial(lambda f, h: feat_ref[f, h], f, h) for f in range(frames) for h in range(2)],
        stat_ref,
    )


def affine(stat_ref, gain_ref, bias_ref):
    scale = lax.rsqrt(stat_ref[1:2, :] + EPS) * gain_ref[...]
    return scale, bias_ref[...] - stat_ref[0:1, :] * scale


def conv_kernel(
    flags,
    stat_ref,
    gain_ref,
    bias_ref,
    own_ref,
    up_ref,
    down_ref,
    past_ref,
    past_up_ref,
    past_down_ref,
    weight_ref,
    conv_bias_ref,
    out0_ref,
    out1_ref,
    out_stat_ref,
    act_ref,
    acc_ref,
):
    step = pl.program_id(0)
    width, chans = own_ref.shape[2], own_ref.shape[3]
    later, parity, has_up, has_down = flags[0], flags[1], flags[2], flags[3]

    @pl.when(step == 0)
    def _():
        scale, shift = affine(stat_ref, gain_ref, bias_ref)
        row_id = lax.broadcasted_iota(jnp.int32, (width, chans), 0)

        def put(frame, row, value, keep):
            pre = value.astype(F32) * scale + shift
            act = pre / (1.0 + jnp.exp(-pre))
            if keep is not None:
                act = jnp.where(keep > 0, act, 0.0)
            left = jnp.where(row_id == 0, 0.0, pltpu.roll(act, 1, 0))
            right = jnp.where(row_id == width - 1, 0.0, pltpu.roll(act, width - 1, 0))
            act_ref[frame, row, :, 0:chans] = left.astype(BF)
            act_ref[frame, row, :, chans : 2 * chans] = act.astype(BF)
            act_ref[frame, row, :, 2 * chans : 3 * chans] = right.astype(BF)

        for f in range(2):
            put(2 + f, 0, up_ref[f], has_up)
            put(2 + f, 1, own_ref[f, 0], None)
            put(2 + f, 2, own_ref[f, 1], None)
            put(2 + f, 3, down_ref[f], has_down)

        @pl.when(later == 1)
        def _():
            for f in range(2):
                put(f, 0, past_up_ref[f], has_up)
                put(f, 1, past_ref[f, 0], None)
                put(f, 2, past_ref[f, 1], None)
                put(f, 3, past_down_ref[f], has_down)

        @pl.when(later == 0)
        def _():
            for f in range(2):
                for row in range(4):
                    act_ref[f, row] = act_ref[2, row]

    tap_t, tap_h = step // 3, step % 3
    slab = act_ref[pl.ds(tap_t, 2), pl.ds(tap_h, 2)].reshape(4 * width, 3 * chans)
    part = jnp.dot(slab, weight_ref[0], preferred_element_type=F32)

    @pl.when(step == 0)
    def _():
        acc_ref[...] = part.reshape(acc_ref.shape)

    @pl.when(step > 0)
    def _():
        acc_ref[...] += part.reshape(acc_ref.shape)

    @pl.when(step == 8)
    def _():
        outs = (out0_ref, out1_ref)
        for p in range(2):
            frame = (parity + p) & 1
            for h in range(2):
                value = own_ref[frame, h].astype(F32) + (acc_ref[frame, h] + conv_bias_ref[...])
                outs[p][h * width : (h + 1) * width, :] = value.astype(BF)
        local_stats(
            [
                functools.partial(lambda p, h: outs[p][h * width : (h + 1) * width, :], p, h)
                for p in range(2)
                for h in range(2)
            ],
            out_stat_ref,
        )


KEYS = 4352
PAD = 32
SPLITS = (1280, 1024, 1024, 1024)


def attend_kernel(
    flags,
    stat_ref,
    gain_ref,
    bias_ref,
    own0_ref,
    own1_ref,
    swap0_ref,
    swap1_ref,
    relay0_ref,
    relay1_ref,
    prev0_ref,
    prev1_ref,
    next0_ref,
    next1_ref,
    wq_ref,
    wk_ref,
    wv_ref,
    wo_ref,
    out_bias_ref,
    out0_ref,
    out1_ref,
    key_ref,
    mask_ref,
):
    cells, chans = own0_ref.shape
    low, prev_ok, next_ok, relay_ok = flags[0], flags[1], flags[2], flags[3]
    scale, shift = affine(stat_ref, gain_ref, bias_ref)

    def put(place, ref):
        start = place * cells
        if not isinstance(place, int):
            start = pl.multiple_of(start, 16)
        key_ref[pl.ds(start, cells), :] = (ref[...].astype(F32) * scale + shift).astype(BF)

    high = 1 - low
    put(1, own0_ref)
    put(2, own1_ref)
    put(3, swap0_ref)
    put(4, swap1_ref)
    put(5, relay0_ref)
    put(6, relay1_ref)
    put(7 * low, prev0_ref)
    put(7 * high, prev1_ref)
    put(8 + high, next1_ref)
    put(8 + low, next0_ref)

    place = lax.broadcasted_iota(jnp.int32, (1, KEYS), 1)
    for upper in range(2):
        row = place + upper * (cells - PAD)
        stripe_ok = jnp.where(
            (row < cells) | ((row >= 7 * cells) & (row < 8 * cells)),
            prev_ok,
            jnp.where(row >= 8 * cells, next_ok, jnp.where((row >= 5 * cells) & (row < 7 * cells), relay_ok, 1)),
        )
        inside = (row < 9 * cells) if upper == 0 else (row >= cells)
        mask_ref[upper : upper + 1, :] = jnp.where(inside & (stripe_ok > 0), 0.0, -1e30)

    factor = LOG2E / math.sqrt(chans)
    for p, (own_ref, out_ref) in enumerate(((own0_ref, out0_ref), (own1_ref, out1_ref))):
        upper = low ^ p
        normed = key_ref[(1 + p) * cells : (2 + p) * cells, :]
        query = jnp.dot(normed, wq_ref[...], preferred_element_type=F32).astype(BF)
        query = lax.dot_general(
            query, wk_ref[...], (((1,), (1,)), ((), ())), preferred_element_type=F32
        )
        query = (query * factor).astype(BF)
        top = jnp.full((cells, 1), -jnp.inf, F32)
        total = jnp.zeros((cells, 1), F32)
        acc = jnp.zeros((cells, chans), F32)
        start = 0
        for size in SPLITS:
            begin = pl.multiple_of(upper * (cells - PAD) + start, 16)
            block = key_ref[pl.ds(begin, size), :]
            score = lax.dot_general(
                query, block, (((1,), (1,)), ((), ())), preferred_element_type=F32
            )
            score = score + mask_ref[pl.ds(upper, 1), start : start + size]
            new_top = jnp.maximum(top, jnp.max(score, axis=-1, keepdims=True))
            weight = jnp.exp2(score - new_top)
            fade = jnp.exp2(top - new_top)
            total = total * fade + jnp.sum(weight, axis=-1, keepdims=True)
            acc = acc * fade + jnp.dot(weight.astype(BF), block, preferred_element_type=F32)
            top = new_top
            start += size
        mixed = (acc / total).astype(BF)
        attn = jnp.dot(mixed, wv_ref[...], preferred_element_type=F32).astype(BF)
        result = jnp.dot(attn, wo_ref[...], preferred_element_type=F32)
        out_ref[...] = (own_ref[...].astype(F32) + out_bias_ref[...] + result).astype(BF)


def whole():
    return pl.BlockSpec(memory_space=pltpu.VMEM)


def flag_spec():
    return pl.BlockSpec(memory_space=pltpu.SMEM)


def params():
    return pltpu.CompilerParams(vmem_limit_bytes=VMEM_LIMIT)


def shards(
    feat,
    norm1_gain,
    norm1_bias,
    conv_weight,
    conv_bias,
    norm2_gain,
    norm2_bias,
    w_query,
    w_key,
    w_value,
    w_out,
    out_bias,
):
    frames, rows, width, chans = feat.shape
    t, z, x, y = (lax.axis_index(a) for a in AXES)
    block = z * NX + x
    stripe = block * NY + y
    i32 = lambda *v: jnp.stack([jnp.asarray(a, jnp.int32) for a in v])
    line = lambda v: v.reshape(1, chans)

    edge = jax.ShapeDtypeStruct((frames, width, chans), BF)
    stat_shape = jax.ShapeDtypeStruct((2, chans), F32)
    stats, top, low = pl.pallas_call(
        edge_kernel,
        out_shape=(stat_shape, edge, edge),
        in_specs=[whole()],
        out_specs=(whole(), whole(), whole()),
        compiler_params=params(),
        name="edges",
    )(feat)
    up = send(low, rows_by(1))
    down = send(top, rows_by(-1))
    past = send(feat, turned("tm", 1))
    past_up = send(up, turned("tm", 1))
    past_down = send(down, turned("tm", 1))
    stats = global_stats(stats)

    flags = i32(t, y & 1, stripe > 0, stripe < NZ * NX * NY - 1)
    full = lambda a: pl.BlockSpec(a.shape, lambda i, *_: (0,) * a.ndim)
    cells = rows * width
    piece = jax.ShapeDtypeStruct((cells, chans), BF)
    args = (stats, line(norm1_gain), line(norm1_bias), feat, up, down, past, past_up, past_down)
    own0, own1, stats2 = pl.pallas_call(
        conv_kernel,
        out_shape=(piece, piece, stat_shape),
        grid_spec=pltpu.PrefetchScalarGridSpec(
            num_scalar_prefetch=1,
            grid=(9,),
            in_specs=[full(a) for a in args]
            + [
                pl.BlockSpec((1, 3 * chans, chans), lambda i, *_: (i, 0, 0)),
                pl.BlockSpec((1, chans), lambda i, *_: (0, 0)),
            ],
            out_specs=(full(piece), full(piece), full(stat_shape)),
            scratch_shapes=[
                pltpu.VMEM((4, 4, width, 3 * chans), BF),
                pltpu.VMEM((frames, rows, width, chans), F32),
            ],
        ),
        compiler_params=params(),
        name="conv",
    )(flags, *args, conv_weight.reshape(9, 3 * chans, chans), line(conv_bias))

    mine0 = send(own0, to_frames(0))
    mine1 = send(own1, to_frames(1))
    prev0 = send(mine0, blocks_by(1))
    next0 = send(mine0, blocks_by(-1))
    prev1 = send(mine1, blocks_by(1))
    next1 = send(mine1, blocks_by(-1))
    swap0 = send(mine0, turned("tm", 1))
    swap1 = send(mine1, turned("tm", 1))
    relay0 = send(jnp.where(t == 1, prev0, next0), turned("tm", 1))
    relay1 = send(jnp.where(t == 1, prev1, next1), turned("tm", 1))
    stats2 = global_stats(stats2)

    prev_ok = block > 0
    next_ok = block < NZ * NX - 1
    flags2 = i32(y & 1, prev_ok, next_ok, jnp.where(t == 0, prev_ok, next_ok))
    out0, out1 = pl.pallas_call(
        attend_kernel,
        out_shape=(piece, piece),
        in_specs=[flag_spec()] + [whole()] * 18,
        out_specs=(whole(), whole()),
        scratch_shapes=[
            pltpu.VMEM((10 * cells, chans), BF),
            pltpu.VMEM((2, KEYS), F32),
        ],
        compiler_params=params(),
        name="attend",
    )(
        flags2,
        stats2,
        line(norm2_gain),
        line(norm2_bias),
        mine0,
        mine1,
        swap0,
        swap1,
        relay0,
        relay1,
        prev0,
        prev1,
        next0,
        next1,
        w_query,
        w_key,
        w_value,
        w_out,
        line(out_bias),
    )
    back0 = send(out0, to_stripes(0))
    back1 = send(out1, to_stripes(1))
    odd = (y & 1) == 1
    output = jnp.stack([jnp.where(odd, back1, back0), jnp.where(odd, back0, back1)])
    return output.reshape(feat.shape)


def solution(mesh):
    fine = Mesh(mesh.devices.reshape(2, NZ, NX, NY), AXES)
    place = P("tm", ("z", "x", "y"), None, None)
    return jax.shard_map(
        shards,
        mesh=fine,
        in_specs=(place,) + (P(),) * 11,
        out_specs=place,
        check_vma=False,
    )
```

time: 682 us -> 167 us (0.24); the launches traced: 672 us -> 165 us
  blocking collectives: 259 us -> 0 us
  waiting for transfers between devices: 270 us -> 59.7 us
  Pallas kernels: 0 us -> 48.8 us
  matrix products: 43.8 us -> 0 us
  local copies, waits for them, and re-layouts: 40.4 us -> 1.24 us
  other arithmetic: 22.8 us -> 5.32 us
  starting transfers between devices: 35.9 us -> 49.4 us
    psum x4 -> x0, blocking collectives: 259 us -> none  [the longest x2 133 us: group_norm(): mean = lax.psum(local_sum, ('tm', 'rows')) / count]
    ppermute x11 -> x37, waiting for transfers between devices: 270 us -> 59.7 us  [send(): return lax.ppermute(value, AXES, pairs_of(move))]
    pallas_call x0 -> x3, Pallas kernels: none -> 48.8 us  [the longest x1 26.8 us: shards(): pl.pallas_call(conv_kernel, out_shape=(piece, piece, stat_shape), grid_sp...]
    dot_general x15 -> x0, matrix products: 43.8 us -> none  [the longest x9 15.9 us: conv_taps(): jnp.dot(stacked.reshape(-1, 3 * chans), weight[step_t, step_h].reshape(3...]
    slice x5 -> x0, local copies, waits for them, and re-layouts: 20.3 us -> none  [the longest x1 9.25 us: conv_taps(): weight[step_t, step_h].reshape(3 * chans, -1)]
    unnamed x65 -> x20, local copies, waits for them, and re-layouts: 17.3 us -> 1.24 us
    reduce_sum x9 -> x0, other arithmetic: 13.7 us -> none  [the longest x1 9.45 us: shards(): total = jnp.sum(expo, axis=-1, keepdims=True)]
    ppermute x11 -> x37, starting transfers between devices: 35.9 us -> 49.4 us  [send(): return lax.ppermute(value, AXES, pairs_of(move))]
  transfers between devices with their start and end apart: 11 -> 37, of which waited for: 8 -> 13; matrix products, arithmetic and copies ran while one was open for 4% -> 2% of each run, Pallas kernels for 0% -> 0%
where the time goes in v1:
time: 167 us; the launch traced here: 165 us
  waiting for transfers between devices  59.7 us (36%)
  starting transfers between devices  49.4 us (30%)
  Pallas kernels  48.8 us (29%)
  other arithmetic  5.32 us (3%)
    ppermute x37, waiting for transfers between devices, send(): return lax.ppermute(value, AXES, pairs_of(move))  59.7 us
    ppermute x37, starting transfers between devices, send(): return lax.ppermute(value, AXES, pairs_of(move))  49.4 us
    pallas_call x1, Pallas kernels, shards(): pl.pallas_call(conv_kernel, out_shape=(piece, piece, stat_shape), grid_sp...  26.8 us
    pallas_call x1, Pallas kernels, shards(): pl.pallas_call(attend_kernel, out_shape=(piece, piece), in_specs=[flag_sp...  18.8 us
  transfers between devices with their start and end apart: 37, of which 13 were waited for; matrix products, arithmetic and copies ran while one was open for 2% of the time, Pallas kernels for 0%

profile of v1, /device:TPU:33, one launch (start us, length us, event | category | flops | bytes accessed | tf_op | source)
XLA Modules:
  0.0 164.9 jit_solution(13444917015744131990)
XLA Ops:
  0.0 3.1 %edges.1 = (f32[2,512]{1,0:T(2,128)}, bf16[2,240,512]{2,1,0:T(8,128)(2,1)}, bf16[2,240,512]{2,1,0:T(8,128)(2,1)}) custom-call(bf16[2,2,240,512]{3,2,1,0:T(8,128)(2,1)} %own_ref.1), custom_call_target="tpu_custom_call" | custom-call | tf_op jit(solution)/shard_map/edges/pallas_call | solution.py:377
  3.1 0.7 collective-permute-start
  3.8 1.0 collective-permute-done
  4.9 0.8 fusion.8
  5.6 0.1 collective-permute-start.3
  5.7 2.8 %collective-permute-start.2 = (f32[2,512]{1,0:T(2,128)S(1)}, f32[2,512]{1,0:T(2,128)S(1)}, u32[]{:S(2)}, u32[]{:S(2)}) collective-permute-start(f32[2,512]{1,0:T(2,128)S(1)} %pad_maximum_fusion.1), channel_id=1, source_target_pairs={{0,32},{1,33},{2,34},{3,35},{4,36},{5,37},{6,38},{7,39},{8,40},{9,... | collective-permute-start | bytes 12296 | tf_op jit(solution)/shard_map/ppermute | solution.py:39
  8.5 1.9 %collective-permute-start.1 = (f32[2,512]{1,0:T(2,128)S(1)}, f32[2,512]{1,0:T(2,128)S(1)}, u32[]{:S(2)}, u32[]{:S(2)}) collective-permute-start(f32[2,512]{1,0:T(2,128)S(1)} %pad_maximum_fusion.1), channel_id=1, source_target_pairs={{0,16},{1,17},{2,18},{3,19},{4,20},{5,21},{6,22},{7,23},{8,24},{9,... | collective-permute-start | bytes 12296 | tf_op jit(solution)/shard_map/ppermute | solution.py:39
  10.5 1.2 collective-permute-start.12
  11.7 3.2 %collective-permute-start.10 = (bf16[2,240,512]{2,1,0:T(8,128)(2,1)}, bf16[2,240,512]{2,1,0:T(8,128)(2,1)S(1)}, u32[]{:S(2)}, u32[]{:S(2)}) collective-permute-start(bf16[2,240,512]{2,1,0:T(8,128)(2,1)} %get-tuple-element.14), channel_id=1, source_target_pairs={{0,1},{1,2},{2,3},{3,4},{4,5},{5,6},{6,7},{7,8},{8,9},{9,10},{10,1... | collective-permute-start | bytes 1474568 | tf_op jit(solution)/shard_map/ppermute | solution.py:39
  14.9 6.3 %collective-permute-start.11 = (bf16[2,240,512]{2,1,0:T(8,128)(2,1)}, bf16[2,240,512]{2,1,0:T(8,128)(2,1)S(1)}, u32[]{:S(2)}, u32[]{:S(2)}) collective-permute-start(bf16[2,240,512]{2,1,0:T(8,128)(2,1)} %get-tuple-element.15), channel_id=1, source_target_pairs={{1,0},{2,1},{3,2},{4,3},{5,4},{6,5},{7,6},{8,7},{9,8},{10,9},{11,1... | collective-permute-start | bytes 1474568 | tf_op jit(solution)/shard_map/ppermute | solution.py:39
  21.3 0.4 collective-permute-start.6
  21.7 0.5 collective-permute-start.5
  22.2 9.5 %collective-permute-done.6 = f32[2,512]{1,0:T(2,128)S(1)} collective-permute-done((f32[2,512]{1,0:T(2,128)S(1)}, f32[2,512]{1,0:T(2,128)S(1)}, u32[]{:S(2)}, u32[]{:S(2)}) %collective-permute-start.6) | collective-permute-done | bytes 4128 | tf_op jit(solution)/shard_map/ppermute | solution.py:39
  31.7 0.8 collective-permute-start.4
  32.6 3.4 %collective-permute-done.4 = f32[2,512]{1,0:T(2,128)S(1)} collective-permute-done((f32[2,512]{1,0:T(2,128)S(1)}, f32[2,512]{1,0:T(2,128)S(1)}, u32[]{:S(2)}, u32[]{:S(2)}) %collective-permute-start.4) | collective-permute-done | bytes 4128 | tf_op jit(solution)/shard_map/ppermute | solution.py:39
  36.0 2.3 %collective-permute-start.13 = (bf16[2,240,512]{2,1,0:T(8,128)(2,1)S(1)}, bf16[2,240,512]{2,1,0:T(8,128)(2,1)S(1)}, u32[]{:S(2)}, u32[]{:S(2)}) collective-permute-start(bf16[2,240,512]{2,1,0:T(8,128)(2,1)S(1)} %collective-permute-done.10.up_ref), channel_id=1, source_target_pairs={{0,64},{1,65},{2,66},{3,67},{4,68},{5,69},{6,70},{7,71},{8,72},{9,... | collective-permute-start | bytes 1474568 | tf_op jit(solution)/shard_map/ppermute | solution.py:39
  38.4 0.1 collective-permute-start.14
  38.5 0.1 collective-permute-start.9
  38.6 0.1 collective-permute-start.8
  38.7 2.3 %collective-permute-done.9 = f32[2,512]{1,0:T(2,128)S(1)} collective-permute-done((f32[2,512]{1,0:T(2,128)S(1)}, f32[2,512]{1,0:T(2,128)S(1)}, u32[]{:S(2)}, u32[]{:S(2)}) %collective-permute-start.9) | collective-permute-done | bytes 4128 | tf_op jit(solution)/shard_map/ppermute | solution.py:39
  41.0 0.6 pad_add_fusion.1.flags
  41.6 1.0 collective-permute-done.8
  42.6 2.1 %collective-permute-done.7 = f32[2,512]{1,0:T(2,128)S(1)} collective-permute-done((f32[2,512]{1,0:T(2,128)S(1)}, f32[2,512]{1,0:T(2,128)S(1)}, u32[]{:S(2)}, u32[]{:S(2)}) %collective-permute-start.7) | collective-permute-done | bytes 4128 | tf_op jit(solution)/shard_map/ppermute | solution.py:39
  44.7 0.6 pad_maximum_fusion.4.stat_ref
  45.3 0.0 copy-start.4
  45.4 0.7 copy-done.7
  46.1 0.2 copy-done.8
  46.3 0.3 copy-done.4
  46.6 26.8 %conv.1 = (bf16[480,512]{1,0:T(8,128)(2,1)}, bf16[480,512]{1,0:T(8,128)(2,1)}, f32[2,512]{1,0:T(2,128)}) custom-call(s32[4]{0:T(128)} %pad_add_fusion.1.flags, f32[2,512]{1,0:T(2,128)} %pad_maximum_fusion.4.stat_ref, f32[1,512]{1,0:T(1,128)} %bitcast.19, f32[1,512]{1,0:T(1,128)} %bitcast.20, bf16[2,2,240,512]{3,2,1,0:T(8,128)(2,1)} %own_ref.1, ...), custom_call_target="tpu_custom_call" | custom-call | tf_op jit(solution)/shard_map/conv/pallas_call | solution.py:397
  73.4 1.9 %collective-permute-start.25 = (bf16[480,512]{1,0:T(8,128)(2,1)}, bf16[480,512]{1,0:T(8,128)(2,1)S(1)}, u32[]{:S(2)}, u32[]{:S(2)}) collective-permute-start(bf16[480,512]{1,0:T(8,128)(2,1)} %get-tuple-element.17), channel_id=1, source_target_pairs={{0,0},{1,1},{2,64},{3,65},{4,4},{5,5},{6,68},{7,69},{8,8},{9,9},{1... | collective-permute-start | bytes 1474568 | tf_op jit(solution)/shard_map/ppermute | solution.py:39
  75.3 0.8 collective-permute-start.15
  76.2 1.3 collective-permute-start.26
  77.5 0.8 fusion.9
  78.3 0.1 collective-permute-start.18
  78.4 1.6 collective-permute-start.17
  80.0 0.8 collective-permute-start.16
  80.7 9.8 %collective-permute-done.25.own0_ref = bf16[480,512]{1,0:T(8,128)(2,1)S(1)} collective-permute-done((bf16[480,512]{1,0:T(8,128)(2,1)}, bf16[480,512]{1,0:T(8,128)(2,1)S(1)}, u32[]{:S(2)}, u32[]{:S(2)}) %collective-permute-start.25) | collective-permute-done | bytes 491552 | tf_op jit(solution)/shard_map/ppermute | solution.py:39
  90.6 1.9 %collective-permute-start.30 = (bf16[480,512]{1,0:T(8,128)(2,1)S(1)}, bf16[480,512]{1,0:T(8,128)(2,1)S(1)}, u32[]{:S(2)}, u32[]{:S(2)}) collective-permute-start(bf16[480,512]{1,0:T(8,128)(2,1)S(1)} %collective-permute-done.25.own0_ref), channel_id=1, source_target_pairs={{4,0},{5,1},{6,2},{7,3},{8,4},{9,5},{10,6},{11,7},{12,8},{13,9},{1... | collective-permute-start | bytes 1474568 | tf_op jit(solution)/shard_map/ppermute | solution.py:39
  92.5 3.4 %collective-permute-start.29 = (bf16[480,512]{1,0:T(8,128)(2,1)S(1)}, bf16[480,512]{1,0:T(8,128)(2,1)S(1)}, u32[]{:S(2)}, u32[]{:S(2)}) collective-permute-start(bf16[480,512]{1,0:T(8,128)(2,1)S(1)} %collective-permute-done.25.own0_ref), channel_id=1, source_target_pairs={{0,4},{1,5},{2,6},{3,7},{4,8},{5,9},{6,10},{7,11},{8,12},{9,13},{1... | collective-permute-start | bytes 1474568 | tf_op jit(solution)/shard_map/ppermute | solution.py:39
  95.9 4.1 %collective-permute-start.21 = (f32[2,512]{1,0:T(2,128)S(1)}, f32[2,512]{1,0:T(2,128)S(1)}, u32[]{:S(2)}, u32[]{:S(2)}) collective-permute-start(f32[2,512]{1,0:T(2,128)S(1)} %pad_maximum_fusion.6), channel_id=1, source_target_pairs={{0,12},{1,13},{2,14},{3,15},{4,0},{5,1},{6,2},{7,3},{8,4},{9,5},{1... | collective-permute-start | bytes 12296 | tf_op jit(solution)/shard_map/ppermute | solution.py:39
  100.1 1.9 %collective-permute-start.33 = (bf16[480,512]{1,0:T(8,128)(2,1)}, bf16[480,512]{1,0:T(8,128)(2,1)S(1)}, u32[]{:S(2)}, u32[]{:S(2)}) collective-permute-start(bf16[480,512]{1,0:T(8,128)(2,1)} %collective-permute-done.26.own1_ref), channel_id=1, source_target_pairs={{4,0},{5,1},{6,2},{7,3},{8,4},{9,5},{10,6},{11,7},{12,8},{13,9},{1... | collective-permute-start | bytes 1474568 | tf_op jit(solution)/shard_map/ppermute | solution.py:39
  102.0 1.9 %collective-permute-done.21 = f32[2,512]{1,0:T(2,128)S(1)} collective-permute-done((f32[2,512]{1,0:T(2,128)S(1)}, f32[2,512]{1,0:T(2,128)S(1)}, u32[]{:S(2)}, u32[]{:S(2)}) %collective-permute-start.21) | collective-permute-done | bytes 4128 | tf_op jit(solution)/shard_map/ppermute | solution.py:39
  103.9 1.9 %collective-permute-start.32 = (bf16[480,512]{1,0:T(8,128)(2,1)}, bf16[480,512]{1,0:T(8,128)(2,1)S(1)}, u32[]{:S(2)}, u32[]{:S(2)}) collective-permute-start(bf16[480,512]{1,0:T(8,128)(2,1)} %collective-permute-done.26.own1_ref), channel_id=1, source_target_pairs={{0,4},{1,5},{2,6},{3,7},{4,8},{5,9},{6,10},{7,11},{8,12},{9,13},{1... | collective-permute-start | bytes 1474568 | tf_op jit(solution)/shard_map/ppermute | solution.py:39
  105.8 0.9 collective-permute-start.19
  106.6 10.3 %collective-permute-done.19 = f32[2,512]{1,0:T(2,128)S(1)} collective-permute-done((f32[2,512]{1,0:T(2,128)S(1)}, f32[2,512]{1,0:T(2,128)S(1)}, u32[]{:S(2)}, u32[]{:S(2)}) %collective-permute-start.19) | collective-permute-done | bytes 4128 | tf_op jit(solution)/shard_map/ppermute | solution.py:39
  116.9 0.1 collective-permute-start.27
  117.1 0.5 collective-permute-start.28
  117.5 0.1 broadcast_select_fusion.1
  117.6 0.2 collective-permute-start.31
  117.8 0.1 broadcast_select_fusion
  117.9 0.5 collective-permute-start.34
  118.4 0.1 collective-permute-start.24
  118.5 2.4 %collective-permute-done.24 = f32[2,512]{1,0:T(2,128)S(1)} collective-permute-done((f32[2,512]{1,0:T(2,128)S(1)}, f32[2,512]{1,0:T(2,128)S(1)}, u32[]{:S(2)}, u32[]{:S(2)}) %collective-permute-start.24) | collective-permute-done | bytes 4128 | tf_op jit(solution)/shard_map/ppermute | solution.py:39
  120.9 1.2 collective-permute-start.23
  122.2 2.7 %collective-permute-done.23 = f32[2,512]{1,0:T(2,128)S(1)} collective-permute-done((f32[2,512]{1,0:T(2,128)S(1)}, f32[2,512]{1,0:T(2,128)S(1)}, u32[]{:S(2)}, u32[]{:S(2)}) %collective-permute-start.23) | collective-permute-done | bytes 4128 | tf_op jit(solution)/shard_map/ppermute | solution.py:39
  124.9 0.6 pad_add_fusion.flags
  125.5 3.1 %collective-permute-done.22 = f32[2,512]{1,0:T(2,128)S(1)} collective-permute-done((f32[2,512]{1,0:T(2,128)S(1)}, f32[2,512]{1,0:T(2,128)S(1)}, u32[]{:S(2)}, u32[]{:S(2)}) %collective-permute-start.22) | collective-permute-done | bytes 4128 | tf_op jit(solution)/shard_map/ppermute | solution.py:39
  128.6 0.6 pad_maximum_fusion.8.stat_ref
  129.2 18.8 %attend.1 = (bf16[480,512]{1,0:T(8,128)(2,1)}, bf16[480,512]{1,0:T(8,128)(2,1)}) custom-call(s32[4]{0:T(128)} %pad_add_fusion.flags, f32[2,512]{1,0:T(2,128)} %pad_maximum_fusion.8.stat_ref, f32[1,512]{1,0:T(1,128)} %bitcast.22, f32[1,512]{1,0:T(1,128)} %bitcast.23, bf16[480,512]{1,0:T(8,128)(2,1)} %copy-done.9, ...), custom_call_target="tpu_custom_call" | custom-call | tf_op jit(solution)/shard_map/attend/pallas_call | solution.py:433
  148.1 3.7 %collective-permute-start.35 = (bf16[480,512]{1,0:T(8,128)(2,1)}, bf16[480,512]{1,0:T(8,128)(2,1)S(1)}, u32[]{:S(2)}, u32[]{:S(2)}) collective-permute-start(bf16[480,512]{1,0:T(8,128)(2,1)} %get-tuple-element.19), channel_id=1, source_target_pairs={{0,1},{1,0},{2,65},{3,64},{4,5},{5,4},{6,69},{7,68},{8,9},{9,8},{1... | collective-permute-start | bytes 1474568 | tf_op jit(solution)/shard_map/ppermute | solution.py:39
  151.8 1.9 %collective-permute-start.36 = (bf16[480,512]{1,0:T(8,128)(2,1)}, bf16[480,512]{1,0:T(8,128)(2,1)S(1)}, u32[]{:S(2)}, u32[]{:S(2)}) collective-permute-start(bf16[480,512]{1,0:T(8,128)(2,1)} %get-tuple-element.20), channel_id=1, source_target_pairs={{0,0},{1,1},{2,64},{3,65},{4,4},{5,5},{6,68},{7,69},{8,8},{9,9},{1... | collective-permute-start | bytes 1474568 | tf_op jit(solution)/shard_map/ppermute | solution.py:39
  153.7 10.0 %collective-permute-done.35 = bf16[480,512]{1,0:T(8,128)(2,1)S(1)} collective-permute-done((bf16[480,512]{1,0:T(8,128)(2,1)}, bf16[480,512]{1,0:T(8,128)(2,1)S(1)}, u32[]{:S(2)}, u32[]{:S(2)}) %collective-permute-start.35) | collective-permute-done | bytes 491552 | tf_op jit(solution)/shard_map/ppermute | solution.py:39
  163.8 0.1 broadcast_select_fusion.3
  163.9 1.0 pad_maximum_fusion
  (55 shorter events, 0.3 us)
Async XLA Ops:
  3.1 1.7 %collective-permute-start = (f32[2,512]{1,0:T(2,128)}, f32[2,512]{1,0:T(2,128)S(1)}, u32[]{:S(2)}, u32[]{:S(2)}) collective-permute-start(f32[2,512]{1,0:T(2,128)} %get-tuple-element.13), channel_id=1, source_target_pairs={{0,64},{1,65},{2,66},{3,67},{4,68},{5,69},{6,70},{7,71},{8,72},{9,... | collective-permute-start | bytes 12296 | tf_op jit(solution)/shard_map/ppermute | solution.py:39
  5.6 9.2 %collective-permute-start.3 = (f32[2,512]{1,0:T(2,128)S(1)}, f32[2,512]{1,0:T(2,128)S(1)}, u32[]{:S(2)}, u32[]{:S(2)}) collective-permute-start(f32[2,512]{1,0:T(2,128)S(1)} %pad_maximum_fusion.1), channel_id=1, source_target_pairs={{0,48},{1,49},{2,50},{3,51},{4,52},{5,53},{6,54},{7,55},{8,56},{9,... | collective-permute-start | bytes 12296 | tf_op jit(solution)/shard_map/ppermute | solution.py:39
  5.7 15.5 %collective-permute-start.2 = (f32[2,512]{1,0:T(2,128)S(1)}, f32[2,512]{1,0:T(2,128)S(1)}, u32[]{:S(2)}, u32[]{:S(2)}) collective-permute-start(f32[2,512]{1,0:T(2,128)S(1)} %pad_maximum_fusion.1), channel_id=1, source_target_pairs={{0,32},{1,33},{2,34},{3,35},{4,36},{5,37},{6,38},{7,39},{8,40},{9,... | collective-permute-start | bytes 12296 | tf_op jit(solution)/shard_map/ppermute | solution.py:39
  8.5 12.7 %collective-permute-start.1 = (f32[2,512]{1,0:T(2,128)S(1)}, f32[2,512]{1,0:T(2,128)S(1)}, u32[]{:S(2)}, u32[]{:S(2)}) collective-permute-start(f32[2,512]{1,0:T(2,128)S(1)} %pad_maximum_fusion.1), channel_id=1, source_target_pairs={{0,16},{1,17},{2,18},{3,19},{4,20},{5,21},{6,22},{7,23},{8,24},{9,... | collective-permute-start | bytes 12296 | tf_op jit(solution)/shard_map/ppermute | solution.py:39
  10.5 34.8 %collective-permute-start.12 = (bf16[2,2,240,512]{3,2,1,0:T(8,128)(2,1)}, bf16[2,2,240,512]{3,2,1,0:T(8,128)(2,1)S(1)}, u32[]{:S(2)}, u32[]{:S(2)}) collective-permute-start(bf16[2,2,240,512]{3,2,1,0:T(8,128)(2,1)} %own_ref.1), channel_id=1, source_target_pairs={{0,64},{1,65},{2,66},{3,67},{4,68},{5,69},{6,70},{7,71},{8,72},{9,... | collective-permute-start | bytes 2949128 | tf_op jit(solution)/shard_map/ppermute | solution.py:39
  11.7 24.4 %collective-permute-start.10 = (bf16[2,240,512]{2,1,0:T(8,128)(2,1)}, bf16[2,240,512]{2,1,0:T(8,128)(2,1)S(1)}, u32[]{:S(2)}, u32[]{:S(2)}) collective-permute-start(bf16[2,240,512]{2,1,0:T(8,128)(2,1)} %get-tuple-element.14), channel_id=1, source_target_pairs={{0,1},{1,2},{2,3},{3,4},{4,5},{5,6},{6,7},{7,8},{8,9},{9,10},{10,1... | collective-permute-start | bytes 1474568 | tf_op jit(solution)/shard_map/ppermute | solution.py:39
  14.9 23.5 %collective-permute-start.11 = (bf16[2,240,512]{2,1,0:T(8,128)(2,1)}, bf16[2,240,512]{2,1,0:T(8,128)(2,1)S(1)}, u32[]{:S(2)}, u32[]{:S(2)}) collective-permute-start(bf16[2,240,512]{2,1,0:T(8,128)(2,1)} %get-tuple-element.15), channel_id=1, source_target_pairs={{1,0},{2,1},{3,2},{4,3},{5,4},{6,5},{7,6},{8,7},{9,8},{10,9},{11,1... | collective-permute-start | bytes 1474568 | tf_op jit(solution)/shard_map/ppermute | solution.py:39
  21.3 10.5 %collective-permute-start.6 = (f32[2,512]{1,0:T(2,128)S(1)}, f32[2,512]{1,0:T(2,128)S(1)}, u32[]{:S(2)}, u32[]{:S(2)}) collective-permute-start(f32[2,512]{1,0:T(2,128)S(1)} %pad_maximum_fusion.2), channel_id=1, source_target_pairs={{0,12},{1,13},{2,14},{3,15},{4,0},{5,1},{6,2},{7,3},{8,4},{9,5},{1... | collective-permute-start | bytes 12296 | tf_op jit(solution)/shard_map/ppermute | solution.py:39
  21.7 10.9 %collective-permute-start.5 = (f32[2,512]{1,0:T(2,128)S(1)}, f32[2,512]{1,0:T(2,128)S(1)}, u32[]{:S(2)}, u32[]{:S(2)}) collective-permute-start(f32[2,512]{1,0:T(2,128)S(1)} %pad_maximum_fusion.2), channel_id=1, source_target_pairs={{0,8},{1,9},{2,10},{3,11},{4,12},{5,13},{6,14},{7,15},{8,0},{9,1},... | collective-permute-start | bytes 12296 | tf_op jit(solution)/shard_map/ppermute | solution.py:39
  31.7 4.3 %collective-permute-start.4 = (f32[2,512]{1,0:T(2,128)S(1)}, f32[2,512]{1,0:T(2,128)S(1)}, u32[]{:S(2)}, u32[]{:S(2)}) collective-permute-start(f32[2,512]{1,0:T(2,128)S(1)} %pad_maximum_fusion.2), channel_id=1, source_target_pairs={{0,4},{1,5},{2,6},{3,7},{4,8},{5,9},{6,10},{7,11},{8,12},{9,13},{1... | collective-permute-start | bytes 12296 | tf_op jit(solution)/shard_map/ppermute | solution.py:39
  36.0 9.3 %copy-start.5 = (bf16[2,240,512]{2,1,0:T(8,128)(2,1)}, bf16[2,240,512]{2,1,0:T(8,128)(2,1)S(1)}, u32[]{:S(2)}) copy-start(bf16[2,240,512]{2,1,0:T(8,128)(2,1)S(1)} %collective-permute-done.10.up_ref) | copy-start | bytes 1474564
  36.0 9.3 %collective-permute-start.13 = (bf16[2,240,512]{2,1,0:T(8,128)(2,1)S(1)}, bf16[2,240,512]{2,1,0:T(8,128)(2,1)S(1)}, u32[]{:S(2)}, u32[]{:S(2)}) collective-permute-start(bf16[2,240,512]{2,1,0:T(8,128)(2,1)S(1)} %collective-permute-done.10.up_ref), channel_id=1, source_target_pairs={{0,64},{1,65},{2,66},{3,67},{4,68},{5,69},{6,70},{7,71},{8,72},{9,... | collective-permute-start | bytes 1474568 | tf_op jit(solution)/shard_map/ppermute | solution.py:39
  38.4 7.0 %copy-start.6 = (bf16[2,240,512]{2,1,0:T(8,128)(2,1)}, bf16[2,240,512]{2,1,0:T(8,128)(2,1)S(1)}, u32[]{:S(2)}) copy-start(bf16[2,240,512]{2,1,0:T(8,128)(2,1)S(1)} %collective-permute-done.11.down_ref) | copy-start | bytes 1474564
  38.4 6.9 %collective-permute-start.14 = (bf16[2,240,512]{2,1,0:T(8,128)(2,1)S(1)}, bf16[2,240,512]{2,1,0:T(8,128)(2,1)S(1)}, u32[]{:S(2)}, u32[]{:S(2)}) collective-permute-start(bf16[2,240,512]{2,1,0:T(8,128)(2,1)S(1)} %collective-permute-done.11.down_ref), channel_id=1, source_target_pairs={{0,64},{1,65},{2,66},{3,67},{4,68},{5,69},{6,70},{7,71},{8,72},{9,... | collective-permute-start | bytes 1474568 | tf_op jit(solution)/shard_map/ppermute | solution.py:39
  38.5 2.5 %collective-permute-start.9 = (f32[2,512]{1,0:T(2,128)S(1)}, f32[2,512]{1,0:T(2,128)S(1)}, u32[]{:S(2)}, u32[]{:S(2)}) collective-permute-start(f32[2,512]{1,0:T(2,128)S(1)} %pad_maximum_fusion.3), channel_id=1, source_target_pairs={{0,3},{1,0},{2,1},{3,2},{4,7},{5,4},{6,5},{7,6},{8,11},{9,8},{10,9... | collective-permute-start | bytes 12296 | tf_op jit(solution)/shard_map/ppermute | solution.py:39
  38.6 4.0 %collective-permute-start.8 = (f32[2,512]{1,0:T(2,128)S(1)}, f32[2,512]{1,0:T(2,128)S(1)}, u32[]{:S(2)}, u32[]{:S(2)}) collective-permute-start(f32[2,512]{1,0:T(2,128)S(1)} %pad_maximum_fusion.3), channel_id=1, source_target_pairs={{0,2},{1,3},{2,0},{3,1},{4,6},{5,7},{6,4},{7,5},{8,10},{9,11},{10,... | collective-permute-start | bytes 12296 | tf_op jit(solution)/shard_map/ppermute | solution.py:39
  41.0 3.7 %collective-permute-start.7 = (f32[2,512]{1,0:T(2,128)S(1)}, f32[2,512]{1,0:T(2,128)S(1)}, u32[]{:S(2)}, u32[]{:S(2)}) collective-permute-start(f32[2,512]{1,0:T(2,128)S(1)} %pad_maximum_fusion.3), channel_id=1, source_target_pairs={{0,1},{1,2},{2,3},{3,0},{4,5},{5,6},{6,7},{7,4},{8,9},{9,10},{10,1... | collective-permute-start | bytes 12296 | tf_op jit(solution)/shard_map/ppermute | solution.py:39
  45.3 0.8 copy-start.7
  45.3 0.9 copy-start.8
  45.3 1.2 copy-start.4
  73.4 17.1 %collective-permute-start.25 = (bf16[480,512]{1,0:T(8,128)(2,1)}, bf16[480,512]{1,0:T(8,128)(2,1)S(1)}, u32[]{:S(2)}, u32[]{:S(2)}) collective-permute-start(bf16[480,512]{1,0:T(8,128)(2,1)} %get-tuple-element.17), channel_id=1, source_target_pairs={{0,0},{1,1},{2,64},{3,65},{4,4},{5,5},{6,68},{7,69},{8,8},{9,9},{1... | collective-permute-start | bytes 1474568 | tf_op jit(solution)/shard_map/ppermute | solution.py:39
  75.3 2.1 %collective-permute-start.15 = (f32[2,512]{1,0:T(2,128)}, f32[2,512]{1,0:T(2,128)S(1)}, u32[]{:S(2)}, u32[]{:S(2)}) collective-permute-start(f32[2,512]{1,0:T(2,128)} %get-tuple-element.16), channel_id=1, source_target_pairs={{0,64},{1,65},{2,66},{3,67},{4,68},{5,69},{6,70},{7,71},{8,72},{9,... | collective-permute-start | bytes 12296 | tf_op jit(solution)/shard_map/ppermute | solution.py:39
  76.2 23.9 %collective-permute-start.26 = (bf16[480,512]{1,0:T(8,128)(2,1)}, bf16[480,512]{1,0:T(8,128)(2,1)}, u32[]{:S(2)}, u32[]{:S(2)}) collective-permute-start(bf16[480,512]{1,0:T(8,128)(2,1)} %get-tuple-element.18), channel_id=1, source_target_pairs={{0,1},{1,0},{2,65},{3,64},{4,5},{5,4},{6,69},{7,68},{8,9},{9,8},{1... | collective-permute-start | bytes 1474568 | tf_op jit(solution)/shard_map/ppermute | solution.py:39
  78.3 14.2 %collective-permute-start.18 = (f32[2,512]{1,0:T(2,128)S(1)}, f32[2,512]{1,0:T(2,128)S(1)}, u32[]{:S(2)}, u32[]{:S(2)}) collective-permute-start(f32[2,512]{1,0:T(2,128)S(1)} %pad_maximum_fusion.5), channel_id=1, source_target_pairs={{0,48},{1,49},{2,50},{3,51},{4,52},{5,53},{6,54},{7,55},{8,56},{9,... | collective-permute-start | bytes 12296 | tf_op jit(solution)/shard_map/ppermute | solution.py:39
  78.4 17.5 %collective-permute-start.17 = (f32[2,512]{1,0:T(2,128)S(1)}, f32[2,512]{1,0:T(2,128)S(1)}, u32[]{:S(2)}, u32[]{:S(2)}) collective-permute-start(f32[2,512]{1,0:T(2,128)S(1)} %pad_maximum_fusion.5), channel_id=1, source_target_pairs={{0,32},{1,33},{2,34},{3,35},{4,36},{5,37},{6,38},{7,39},{8,40},{9,... | collective-permute-start | bytes 12296 | tf_op jit(solution)/shard_map/ppermute | solution.py:39
  80.0 15.9 %collective-permute-start.16 = (f32[2,512]{1,0:T(2,128)S(1)}, f32[2,512]{1,0:T(2,128)S(1)}, u32[]{:S(2)}, u32[]{:S(2)}) collective-permute-start(f32[2,512]{1,0:T(2,128)S(1)} %pad_maximum_fusion.5), channel_id=1, source_target_pairs={{0,16},{1,17},{2,18},{3,19},{4,20},{5,21},{6,22},{7,23},{8,24},{9,... | collective-permute-start | bytes 12296 | tf_op jit(solution)/shard_map/ppermute | solution.py:39
  90.6 38.6 %copy-start.9 = (bf16[480,512]{1,0:T(8,128)(2,1)}, bf16[480,512]{1,0:T(8,128)(2,1)S(1)}, u32[]{:S(2)}) copy-start(bf16[480,512]{1,0:T(8,128)(2,1)S(1)} %collective-permute-done.25.own0_ref) | copy-start | bytes 1474564
  90.6 26.5 %collective-permute-start.30 = (bf16[480,512]{1,0:T(8,128)(2,1)S(1)}, bf16[480,512]{1,0:T(8,128)(2,1)S(1)}, u32[]{:S(2)}, u32[]{:S(2)}) collective-permute-start(bf16[480,512]{1,0:T(8,128)(2,1)S(1)} %collective-permute-done.25.own0_ref), channel_id=1, source_target_pairs={{4,0},{5,1},{6,2},{7,3},{8,4},{9,5},{10,6},{11,7},{12,8},{13,9},{1... | collective-permute-start | bytes 1474568 | tf_op jit(solution)/shard_map/ppermute | solution.py:39
  92.5 25.0 %collective-permute-start.29 = (bf16[480,512]{1,0:T(8,128)(2,1)S(1)}, bf16[480,512]{1,0:T(8,128)(2,1)S(1)}, u32[]{:S(2)}, u32[]{:S(2)}) collective-permute-start(bf16[480,512]{1,0:T(8,128)(2,1)S(1)} %collective-permute-done.25.own0_ref), channel_id=1, source_target_pairs={{0,4},{1,5},{2,6},{3,7},{4,8},{5,9},{6,10},{7,11},{8,12},{9,13},{1... | collective-permute-start | bytes 1474568 | tf_op jit(solution)/shard_map/ppermute | solution.py:39
  95.9 7.9 %collective-permute-start.21 = (f32[2,512]{1,0:T(2,128)S(1)}, f32[2,512]{1,0:T(2,128)S(1)}, u32[]{:S(2)}, u32[]{:S(2)}) collective-permute-start(f32[2,512]{1,0:T(2,128)S(1)} %pad_maximum_fusion.6), channel_id=1, source_target_pairs={{0,12},{1,13},{2,14},{3,15},{4,0},{5,1},{6,2},{7,3},{8,4},{9,5},{1... | collective-permute-start | bytes 12296 | tf_op jit(solution)/shard_map/ppermute | solution.py:39
  100.1 5.7 %collective-permute-start.20 = (f32[2,512]{1,0:T(2,128)S(1)}, f32[2,512]{1,0:T(2,128)S(1)}, u32[]{:S(2)}, u32[]{:S(2)}) collective-permute-start(f32[2,512]{1,0:T(2,128)S(1)} %pad_maximum_fusion.6), channel_id=1, source_target_pairs={{0,8},{1,9},{2,10},{3,11},{4,12},{5,13},{6,14},{7,15},{8,0},{9,1},... | collective-permute-start | bytes 12296 | tf_op jit(solution)/shard_map/ppermute | solution.py:39
  100.1 17.7 %collective-permute-start.33 = (bf16[480,512]{1,0:T(8,128)(2,1)}, bf16[480,512]{1,0:T(8,128)(2,1)S(1)}, u32[]{:S(2)}, u32[]{:S(2)}) collective-permute-start(bf16[480,512]{1,0:T(8,128)(2,1)} %collective-permute-done.26.own1_ref), channel_id=1, source_target_pairs={{4,0},{5,1},{6,2},{7,3},{8,4},{9,5},{10,6},{11,7},{12,8},{13,9},{1... | collective-permute-start | bytes 1474568 | tf_op jit(solution)/shard_map/ppermute | solution.py:39
  103.9 13.9 %collective-permute-start.32 = (bf16[480,512]{1,0:T(8,128)(2,1)}, bf16[480,512]{1,0:T(8,128)(2,1)S(1)}, u32[]{:S(2)}, u32[]{:S(2)}) collective-permute-start(bf16[480,512]{1,0:T(8,128)(2,1)} %collective-permute-done.26.own1_ref), channel_id=1, source_target_pairs={{0,4},{1,5},{2,6},{3,7},{4,8},{5,9},{6,10},{7,11},{8,12},{9,13},{1... | collective-permute-start | bytes 1474568 | tf_op jit(solution)/shard_map/ppermute | solution.py:39
  105.8 11.1 %collective-permute-start.19 = (f32[2,512]{1,0:T(2,128)S(1)}, f32[2,512]{1,0:T(2,128)S(1)}, u32[]{:S(2)}, u32[]{:S(2)}) collective-permute-start(f32[2,512]{1,0:T(2,128)S(1)} %pad_maximum_fusion.6), channel_id=1, source_target_pairs={{0,4},{1,5},{2,6},{3,7},{4,8},{5,9},{6,10},{7,11},{8,12},{9,13},{1... | collective-permute-start | bytes 12296 | tf_op jit(solution)/shard_map/ppermute | solution.py:39
  116.9 12.2 %collective-permute-start.27 = (bf16[480,512]{1,0:T(8,128)(2,1)S(1)}, bf16[480,512]{1,0:T(8,128)(2,1)}, u32[]{:S(2)}, u32[]{:S(2)}) collective-permute-start(bf16[480,512]{1,0:T(8,128)(2,1)S(1)} %collective-permute-done.25.own0_ref), channel_id=1, source_target_pairs={{0,64},{1,65},{2,66},{3,67},{4,68},{5,69},{6,70},{7,71},{8,72},{9,... | collective-permute-start | bytes 1474568 | tf_op jit(solution)/shard_map/ppermute | solution.py:39
  117.0 12.2 %copy-start = (bf16[480,512]{1,0:T(8,128)(2,1)}, bf16[480,512]{1,0:T(8,128)(2,1)S(1)}, u32[]{:S(2)}) copy-start(bf16[480,512]{1,0:T(8,128)(2,1)S(1)} %collective-permute-done.30.next0_ref) | copy-start | bytes 1474564
  117.1 12.1 %collective-permute-start.28 = (bf16[480,512]{1,0:T(8,128)(2,1)}, bf16[480,512]{1,0:T(8,128)(2,1)}, u32[]{:S(2)}, u32[]{:S(2)}) collective-permute-start(bf16[480,512]{1,0:T(8,128)(2,1)} %collective-permute-done.26.own1_ref), channel_id=1, source_target_pairs={{0,64},{1,65},{2,66},{3,67},{4,68},{5,69},{6,70},{7,71},{8,72},{9,... | collective-permute-start | bytes 1474568 | tf_op jit(solution)/shard_map/ppermute | solution.py:39
  117.5 11.7 %copy-start.1 = (bf16[480,512]{1,0:T(8,128)(2,1)}, bf16[480,512]{1,0:T(8,128)(2,1)S(1)}, u32[]{:S(2)}) copy-start(bf16[480,512]{1,0:T(8,128)(2,1)S(1)} %collective-permute-done.29.prev0_ref) | copy-start | bytes 1474564
  117.6 11.6 %collective-permute-start.31 = (bf16[480,512]{1,0:T(8,128)(2,1)S(1)}, bf16[480,512]{1,0:T(8,128)(2,1)}, u32[]{:S(2)}, u32[]{:S(2)}) collective-permute-start(bf16[480,512]{1,0:T(8,128)(2,1)S(1)} %broadcast_select_fusion.1), channel_id=1, source_target_pairs={{0,64},{1,65},{2,66},{3,67},{4,68},{5,69},{6,70},{7,71},{8,72},{9,... | collective-permute-start | bytes 1474568 | tf_op jit(solution)/shard_map/ppermute | solution.py:39
  117.8 11.4 %copy-start.2 = (bf16[480,512]{1,0:T(8,128)(2,1)}, bf16[480,512]{1,0:T(8,128)(2,1)S(1)}, u32[]{:S(2)}) copy-start(bf16[480,512]{1,0:T(8,128)(2,1)S(1)} %collective-permute-done.33.next1_ref) | copy-start | bytes 1474564
  117.8 11.4 %copy-start.3 = (bf16[480,512]{1,0:T(8,128)(2,1)}, bf16[480,512]{1,0:T(8,128)(2,1)S(1)}, u32[]{:S(2)}) copy-start(bf16[480,512]{1,0:T(8,128)(2,1)S(1)} %collective-permute-done.32.prev1_ref) | copy-start | bytes 1474564
  117.9 11.3 %collective-permute-start.34 = (bf16[480,512]{1,0:T(8,128)(2,1)S(1)}, bf16[480,512]{1,0:T(8,128)(2,1)}, u32[]{:S(2)}, u32[]{:S(2)}) collective-permute-start(bf16[480,512]{1,0:T(8,128)(2,1)S(1)} %broadcast_select_fusion), channel_id=1, source_target_pairs={{0,64},{1,65},{2,66},{3,67},{4,68},{5,69},{6,70},{7,71},{8,72},{9,... | collective-permute-start | bytes 1474568 | tf_op jit(solution)/shard_map/ppermute | solution.py:39
  118.4 2.5 %collective-permute-start.24 = (f32[2,512]{1,0:T(2,128)S(1)}, f32[2,512]{1,0:T(2,128)S(1)}, u32[]{:S(2)}, u32[]{:S(2)}) collective-permute-start(f32[2,512]{1,0:T(2,128)S(1)} %pad_maximum_fusion.7), channel_id=1, source_target_pairs={{0,3},{1,0},{2,1},{3,2},{4,7},{5,4},{6,5},{7,6},{8,11},{9,8},{10,9... | collective-permute-start | bytes 12296 | tf_op jit(solution)/shard_map/ppermute | solution.py:39
  120.9 4.0 %collective-permute-start.23 = (f32[2,512]{1,0:T(2,128)S(1)}, f32[2,512]{1,0:T(2,128)S(1)}, u32[]{:S(2)}, u32[]{:S(2)}) collective-permute-start(f32[2,512]{1,0:T(2,128)S(1)} %pad_maximum_fusion.7), channel_id=1, source_target_pairs={{0,2},{1,3},{2,0},{3,1},{4,6},{5,7},{6,4},{7,5},{8,10},{9,11},{10,... | collective-permute-start | bytes 12296 | tf_op jit(solution)/shard_map/ppermute | solution.py:39
  124.9 3.7 %collective-permute-start.22 = (f32[2,512]{1,0:T(2,128)S(1)}, f32[2,512]{1,0:T(2,128)S(1)}, u32[]{:S(2)}, u32[]{:S(2)}) collective-permute-start(f32[2,512]{1,0:T(2,128)S(1)} %pad_maximum_fusion.7), channel_id=1, source_target_pairs={{0,1},{1,2},{2,3},{3,0},{4,5},{5,6},{6,7},{7,4},{8,9},{9,10},{10,1... | collective-permute-start | bytes 12296 | tf_op jit(solution)/shard_map/ppermute | solution.py:39
  148.1 15.7 %collective-permute-start.35 = (bf16[480,512]{1,0:T(8,128)(2,1)}, bf16[480,512]{1,0:T(8,128)(2,1)S(1)}, u32[]{:S(2)}, u32[]{:S(2)}) collective-permute-start(bf16[480,512]{1,0:T(8,128)(2,1)} %get-tuple-element.19), channel_id=1, source_target_pairs={{0,1},{1,0},{2,65},{3,64},{4,5},{5,4},{6,69},{7,68},{8,9},{9,8},{1... | collective-permute-start | bytes 1474568 | tf_op jit(solution)/shard_map/ppermute | solution.py:39
  151.8 12.0 %collective-permute-start.36 = (bf16[480,512]{1,0:T(8,128)(2,1)}, bf16[480,512]{1,0:T(8,128)(2,1)S(1)}, u32[]{:S(2)}, u32[]{:S(2)}) collective-permute-start(bf16[480,512]{1,0:T(8,128)(2,1)} %get-tuple-element.20), channel_id=1, source_target_pairs={{0,0},{1,1},{2,64},{3,65},{4,4},{5,5},{6,68},{7,69},{8,8},{9,9},{1... | collective-permute-start | bytes 1474568 | tf_op jit(solution)/shard_map/ppermute | solution.py:39

commit v2 on v1

v2 whole, which is shorter than its diff:
```python
import functools
import math

import jax
import jax.numpy as jnp
import numpy as np
from jax import lax
from jax.experimental import pallas as pl
from jax.experimental.pallas import tpu as pltpu
from jax.sharding import Mesh, PartitionSpec as P

GROUPS = 32
EPS = 1e-06
AXES = ("tm", "z", "x", "y")
NZ, NX, NY = 4, 4, 4
LOG2E = 1.4426950408889634
CONV = 40
OWN = 24
TAIL = 24
BF = jnp.bfloat16
F32 = jnp.float32


def lin(t, z, x, y):
    return ((t * NZ + z) * NX + x) * NY + y


def pairs_of(move):
    found = []
    for t in range(2):
        for z in range(NZ):
            for x in range(NX):
                for y in range(NY):
                    dest = move(t, z, x, y)
                    if dest is not None:
                        found.append((lin(t, z, x, y), lin(*dest)))
    return found


def send(value, move):
    return lax.ppermute(value, AXES, pairs_of(move))


def edges_out(t, z, x, y):
    row = (z * NX + x) * NY + y + (1 - 2 * t)
    if 0 <= row < NZ * NX * NY:
        return (t, row // (NX * NY), (row // NY) % NX, row % NY)
    return None


def blocks_out(t, z, x, y):
    block = z * NX + x + (1 - 2 * t)
    if 0 <= block < NZ * NX:
        return (t, block // NX, block % NX, y)
    return None


def turned(axis, step):
    def move(t, z, x, y):
        if axis == "tm":
            return (1 - t, z, x, y)
        if axis == "z":
            return (t, (z + step) % NZ, x, y)
        if axis == "x":
            return (t, z, (x + step) % NX, y)
        return (t, z, x, (y + step) % NY)

    return move


def to_frames(order):
    def move(t, z, x, y):
        return (y // 2, z, x, 2 * t + ((y + order) & 1))

    return move


def to_stripes(order):
    forward = to_frames(order)
    back = {}
    for t in range(2):
        for y in range(NY):
            dest = forward(t, 0, 0, y)
            back[(dest[0], dest[3])] = (t, y)

    def move(t, z, x, y):
        there = back[(t, y)]
        return (there[0], z, x, there[1])

    return move


def merge(parts):
    count = len(parts)
    mid = sum(parts) / count
    away = [p[0:1] - mid[0:1] for p in parts]
    extra = sum(a * a for a in away) / count
    row = lax.broadcasted_iota(jnp.int32, mid.shape, 0)
    return mid + jnp.where(row == 1, jnp.broadcast_to(extra, mid.shape), 0.0)


def gathered(stats, axis):
    steps = (1,) if axis == "tm" else (1, 2, 3)
    return [stats] + [send(stats, turned(axis, k)) for k in steps]


def over(stats, axis):
    return merge(gathered(stats, axis))


def after(value, *first):
    return lax.optimization_barrier((value,) + first)[0]


def group_mean(row):
    chans = row.shape[-1]
    size = chans // GROUPS
    lane = lax.broadcasted_iota(jnp.int32, row.shape, 1)
    step = 1
    while step < size:
        low = (lane & step) == 0
        row = row + jnp.where(
            low, pltpu.roll(row, chans - step, 1), pltpu.roll(row, step, 1)
        )
        step *= 2
    return row / size


def local_stats(blocks, stat_ref):
    chans = stat_ref.shape[-1]
    cells = sum(b.shape[0] for b in [f() for f in blocks])
    total = sum(jnp.sum(f().astype(F32), axis=0, keepdims=True) for f in blocks)
    mean = group_mean(jnp.broadcast_to(total / cells, (8, chans)))
    center = mean[0:1]
    square = 0.0
    for f in blocks:
        away = f().astype(F32) - center
        square = square + jnp.sum(away * away, axis=0, keepdims=True)
    spread = group_mean(jnp.broadcast_to(square / cells, (8, chans)))
    stat_ref[0:1, :] = center
    stat_ref[1:2, :] = spread[0:1]


def edge_kernel(flags, feat_ref, other_ref, stat_ref, edge_ref):
    frames = feat_ref.shape[0]
    core = flags[0]
    row = 1 - core
    for f in range(frames):
        edge_ref[frames * core + f] = feat_ref[f, row]
        edge_ref[frames * (1 - core) + f] = other_ref[f, row]
    local_stats(
        [
            functools.partial(lambda ref, f, h: ref[f, h], ref, f, h)
            for ref in (feat_ref, other_ref)
            for f in range(frames)
            for h in range(2)
        ],
        stat_ref,
    )


def affine(stat_ref, gain_ref, bias_ref):
    scale = lax.rsqrt(stat_ref[1:2, :] + EPS) * gain_ref[...]
    return scale, bias_ref[...] - stat_ref[0:1, :] * scale


def conv_kernel(
    flags,
    stat_ref,
    gain_ref,
    bias_ref,
    own_ref,
    past_ref,
    edge_ref,
    cross_ref,
    weight_ref,
    conv_bias_ref,
    out0_ref,
    out1_ref,
    act_ref,
    acc_ref,
    tap_ref,
    sems,
):
    width, chans = own_ref.shape[2], own_ref.shape[3]
    later, parity = flags[0] == 1, flags[1]
    keep = {0: jnp.where(flags[2] > 0, 1.0, 0.0), 3: jnp.where(flags[3] > 0, 1.0, 0.0)}
    copies = [
        pltpu.make_async_copy(weight_ref.at[i], tap_ref.at[i], sems.at[i]) for i in range(9)
    ]
    for copy in copies:
        copy.start()
    scale, shift = affine(stat_ref, gain_ref, bias_ref)
    half_scale, half_shift = scale * 0.5, shift * 0.5
    zero = jnp.zeros((1, chans), BF)

    def put(frame, row):
        if row in keep:
            at = jnp.maximum(2 * flags[0] - 2 + frame, 0)
            mine, theirs = edge_ref[at], cross_ref[at]
            raw = jnp.where(later, theirs, mine) if row == 0 else jnp.where(later, mine, theirs)
        elif frame >= 2:
            raw = own_ref[frame - 2, row - 1]
        else:
            raw = jnp.where(later, past_ref[frame, row - 1], own_ref[0, row - 1])
        raw = raw.astype(F32)
        half = raw * half_scale + half_shift
        act = half + half * jnp.tanh(half)
        if row in keep:
            act = act * keep[row]
        act = act.astype(BF)
        act_ref[frame, row, :, 0:chans] = jnp.concatenate([zero, act[: width - 1]], axis=0)
        act_ref[frame, row, :, chans : 2 * chans] = act
        act_ref[frame, row, :, 2 * chans : 3 * chans] = jnp.concatenate([act[1:], zero], axis=0)

    ready = set()
    for i in range(9):
        tap_t, tap_h = i // 3, i % 3
        for frame in (tap_t, tap_t + 1):
            for row in (tap_h, tap_h + 1):
                if (frame, row) not in ready:
                    ready.add((frame, row))
                    put(frame, row)
        copies[i].wait()
        slab = act_ref[tap_t : tap_t + 2, tap_h : tap_h + 2].reshape(4 * width, 3 * chans)
        part = jnp.dot(slab, tap_ref[i], preferred_element_type=F32).reshape(acc_ref.shape)
        if i == 0:
            acc_ref[...] = part
        else:
            acc_ref[...] += part

    outs = (out0_ref, out1_ref)
    for p in range(2):
        frame = (parity + p) & 1
        for h in range(2):
            value = own_ref[frame, h].astype(F32) + (acc_ref[frame, h] + conv_bias_ref[...])
            outs[p][h * width : (h + 1) * width, :] = value.astype(BF)


def stat_kernel(first_ref, second_ref, stat_ref):
    half = first_ref.shape[0] // 2
    local_stats(
        [
            functools.partial(lambda ref, h: ref[h * half : (h + 1) * half, :], ref, h)
            for ref in (first_ref, second_ref)
            for h in range(2)
        ],
        stat_ref,
    )


def dot_t(a, b):
    return lax.dot_general(a, b, (((1,), (1,)), ((), ())), preferred_element_type=F32)


def gather(query, block, mask, state):
    score = dot_t(query, block)
    if mask is not None:
        score = score + mask
    top = jnp.max(score, axis=-1, keepdims=True)
    if state is not None:
        top = jnp.maximum(state[0], top)
    weight = jnp.exp2(score - top)
    total = jnp.sum(weight, axis=-1, keepdims=True)
    acc = jnp.dot(weight.astype(BF), block, preferred_element_type=F32)
    if state is not None:
        fade = jnp.exp2(state[0] - top)
        total = state[1] * fade + total
        acc = state[2] * fade + acc
    return top, total, acc


def keep_state(state, acc_ref, sum_ref):
    top, total, acc = state
    acc_ref[...] = acc
    lane = lax.broadcasted_iota(jnp.int32, sum_ref.shape, 1)
    sum_ref[...] = jnp.where(lane == 0, top, total)


def load_state(acc_ref, sum_ref):
    return sum_ref[:, 0:1], sum_ref[:, 1:2], acc_ref[...]


def reach_mask(flags, order, far_side, row, start, cells):
    core, low = flags[0], flags[1]
    side = core ^ far_side
    fine = jnp.where(side == 0, flags[4], flags[5])
    mask = 0.0
    for p in range(2):
        key_upper, query_upper = low ^ p, low ^ order
        seen = jnp.where(side == 0, key_upper >= query_upper, key_upper <= query_upper)
        here = (row >= start + p * cells) & (row < start + (p + 1) * cells)
        mask = mask + jnp.where(here & jnp.logical_not(seen & (fine > 0)), -1e30, 0.0)
    return mask


OWN_KEYS = 2944


def own_kernel(
    flags,
    stat_ref,
    gain_ref,
    bias_ref,
    mine_ref,
    swap_ref,
    near_ref,
    wq_ref,
    wk_ref,
    query0_ref,
    query1_ref,
    acc0_ref,
    acc1_ref,
    sum0_ref,
    sum1_ref,
    key_ref,
):
    cells, chans = query0_ref.shape
    scale, shift = affine(stat_ref, gain_ref, bias_ref)
    for i, ref in enumerate((mine_ref, swap_ref, near_ref)):
        raw = ref[...].astype(F32)
        key_ref[2 * i * cells : 2 * (i + 1) * cells, :] = (raw * scale + shift).astype(BF)
    key_ref[6 * cells : OWN_KEYS, :] = jnp.zeros((OWN_KEYS - 6 * cells, chans), BF)
    factor = LOG2E / math.sqrt(chans)
    queries = (query0_ref, query1_ref)
    for p in range(2):
        normed = key_ref[p * cells : (p + 1) * cells, :]
        query = jnp.dot(normed, wq_ref[...], preferred_element_type=F32).astype(BF)
        queries[p][...] = (dot_t(query, wk_ref[...]) * factor).astype(BF)
    row = lax.broadcasted_iota(jnp.int32, (1, OWN_KEYS), 1)
    for p, (acc_ref, sum_ref) in enumerate(((acc0_ref, sum0_ref), (acc1_ref, sum1_ref))):
        mask = reach_mask(flags, p, 0, row, 4 * cells, cells)
        mask = mask + jnp.where(row >= 6 * cells, -1e30, 0.0)
        keep_state(gather(queries[p][...], key_ref[...], mask, None), acc_ref, sum_ref)


def tail_kernel(
    order,
    flags,
    stat_ref,
    gain_ref,
    bias_ref,
    far_ref,
    relay_ref,
    query_ref,
    acc_ref,
    sum_ref,
    own_ref,
    wv_ref,
    wo_ref,
    out_bias_ref,
    out_ref,
    key_ref,
):
    cells = out_ref.shape[0]
    scale, shift = affine(stat_ref, gain_ref, bias_ref)
    for i, ref in enumerate((far_ref, relay_ref)):
        raw = ref[...].astype(F32)
        key_ref[2 * i * cells : 2 * (i + 1) * cells, :] = (raw * scale + shift).astype(BF)
    row = lax.broadcasted_iota(jnp.int32, (1, 4 * cells), 1)
    mask = reach_mask(flags, order, 1, row, 2 * cells, cells)
    far_ok = jnp.where(flags[0] == 0, flags[4], flags[5])
    mask = mask + jnp.where((row < 2 * cells) & (far_ok == 0), -1e30, 0.0)
    state = load_state(acc_ref, sum_ref)
    _, total, acc = gather(query_ref[...], key_ref[...], mask, state)
    mixed = (acc / total).astype(BF)
    attn = jnp.dot(mixed, wv_ref[...], preferred_element_type=F32).astype(BF)
    result = jnp.dot(attn, wo_ref[...], preferred_element_type=F32)
    own = own_ref[...].astype(F32)
    out_ref[...] = (own + out_bias_ref[...] + result).astype(BF)


def place_kernel(flags, back0_ref, back1_ref, out_ref):
    odd = flags[1]
    out_ref[odd] = back0_ref[...]
    out_ref[1 - odd] = back1_ref[...]


def whole():
    return pl.BlockSpec(memory_space=pltpu.VMEM)


def remote():
    return pl.BlockSpec(memory_space=pl.ANY)


def cost(flops, moved):
    return pl.CostEstimate(flops=int(flops), bytes_accessed=int(moved), transcendentals=0)


def flag_spec():
    return pl.BlockSpec(memory_space=pltpu.SMEM)


def params(mib):
    return pltpu.CompilerParams(vmem_limit_bytes=mib * 1024 * 1024)


def shards(
    feat,
    norm1_gain,
    norm1_bias,
    conv_weight,
    conv_bias,
    norm2_gain,
    norm2_bias,
    w_query,
    w_key,
    w_value,
    w_out,
    out_bias,
):
    frames, rows, width, chans = feat.shape
    t, z, x, y = (lax.axis_index(a) for a in AXES)
    block = z * NX + x
    stripe = block * NY + y
    i32 = lambda *v: jnp.stack([jnp.asarray(a, jnp.int32) for a in v])
    line = lambda v: v.reshape(1, chans)

    stat_shape = jax.ShapeDtypeStruct((2, chans), F32)
    flags = i32(t, y & 1, stripe > 0, stripe < NZ * NX * NY - 1, block > 0, block < NZ * NX - 1)
    swap = turned("tm", 1)
    other = send(feat, swap)
    stats, edge = pl.pallas_call(
        edge_kernel,
        out_shape=(stat_shape, jax.ShapeDtypeStruct((2 * frames, width, chans), BF)),
        in_specs=[flag_spec(), whole(), whole()],
        out_specs=(whole(), whole()),
        compiler_params=params(16),
        name="edges",
    )(flags, feat, other)
    parts = gathered(stats, "y")
    edge = send(after(edge, parts[1]), edges_out)
    stats = over(over(merge(parts), "z"), "x")
    cross = send(after(edge, stats), swap)

    cells = rows * width
    piece = jax.ShapeDtypeStruct((cells, chans), BF)
    own0, own1 = pl.pallas_call(
        conv_kernel,
        out_shape=(piece, piece),
        in_specs=[flag_spec()] + [whole()] * 7 + [remote(), whole()],
        out_specs=(whole(),) * 2,
        scratch_shapes=[
            pltpu.VMEM((4, 4, width, 3 * chans), BF),
            pltpu.VMEM((frames, rows, width, chans), F32),
            pltpu.VMEM((9, 3 * chans, chans), BF),
            pltpu.SemaphoreType.DMA((9,)),
        ],
        compiler_params=params(CONV),
        cost_estimate=cost(27 * 2 * 960 * chans * chans, 20e6),
        name="conv",
    )(
        flags,
        stats,
        line(norm1_gain),
        line(norm1_bias),
        feat,
        other,
        edge,
        cross,
        conv_weight.reshape(9, 3 * chans, chans),
        line(conv_bias),
    )

    mine0 = send(own0, to_frames(0))
    mine1 = send(own1, to_frames(1))
    stats2 = pl.pallas_call(
        stat_kernel,
        out_shape=stat_shape,
        in_specs=[whole(), whole()],
        out_specs=whole(),
        compiler_params=params(16),
        cost_estimate=cost(8e9, 2e6),
        name="stats",
    )(own0, own1)
    stats2 = over(over(stats2, "tm"), "z")
    mine = jnp.concatenate([mine0, mine1])
    swapped = send(mine, swap)
    near = send(after(mine, stats2), blocks_out)
    stats2 = over(stats2, "x")
    far = send(after(swapped, stats2), blocks_out)
    stats2 = over(stats2, "y")

    norm2 = (stats2, line(norm2_gain), line(norm2_bias))
    acc_shape = jax.ShapeDtypeStruct((cells, chans), F32)
    sum_shape = jax.ShapeDtypeStruct((cells, 128), F32)
    query0, query1, acc0, acc1, sum0, sum1 = pl.pallas_call(
        own_kernel,
        out_shape=(piece, piece, acc_shape, acc_shape, sum_shape, sum_shape),
        in_specs=[flag_spec()] + [whole()] * 8,
        out_specs=(whole(),) * 6,
        scratch_shapes=[pltpu.VMEM((OWN_KEYS, chans), BF)],
        compiler_params=params(OWN),
        cost_estimate=cost(6e9, 8e6),
        name="own",
    )(flags, *norm2, mine, swapped, near, w_query, w_key)
    relay = send(after(far, sum1), swap)

    def tail(order, query, acc, total, own):
        return pl.pallas_call(
            functools.partial(tail_kernel, order),
            out_shape=piece,
            in_specs=[flag_spec()] + [whole()] * 12,
            out_specs=whole(),
            scratch_shapes=[pltpu.VMEM((4 * cells, chans), BF)],
            compiler_params=params(TAIL),
            cost_estimate=cost(3e9, 5e6),
            name="tail%d" % order,
        )(
            flags,
            *norm2,
            far,
            relay,
            query,
            acc,
            total,
            own,
            w_value,
            w_out,
            line(out_bias),
        )

    out0 = tail(0, query0, acc0, sum0, mine0)
    out1 = tail(1, query1, acc1, sum1, mine1)
    back0 = send(out0, to_stripes(0))
    back1 = send(out1, to_stripes(1))
    output = pl.pallas_call(
        place_kernel,
        out_shape=jax.ShapeDtypeStruct((frames, cells, chans), BF),
        in_specs=[flag_spec(), whole(), whole()],
        out_specs=whole(),
        name="place",
    )(flags, back0, back1)
    return output.reshape(feat.shape)


def solution(mesh):
    fine = Mesh(mesh.devices.reshape(2, NZ, NX, NY), AXES)
    place = P("tm", ("z", "x", "y"), None, None)
    return jax.shard_map(
        shards,
        mesh=fine,
        in_specs=(place,) + (P(),) * 11,
        out_specs=place,
        check_vma=False,
    )
```

time: 167 us -> 145 us (0.87); the launches traced: 165 us -> 145 us
  waiting for transfers between devices: 59.7 us -> 46.1 us
  Pallas kernels: 48.8 us -> 39.7 us
  other arithmetic: 5.32 us -> 1.03 us
  local copies, waits for them, and re-layouts: 1.24 us -> 5.43 us
  starting transfers between devices: 49.4 us -> 52.4 us
    ppermute x37 -> x30, waiting for transfers between devices: 59.7 us -> 46.1 us  [send(): return lax.ppermute(value, AXES, pairs_of(move))]
    pallas_call x3 -> x7, Pallas kernels: 48.8 us -> 39.7 us  [the longest x1 17.7 us: shards(): pl.pallas_call(conv_kernel, out_shape=(piece, piece), in_specs=[flag_spec...]
    unnamed x20 -> x31, local copies, waits for them, and re-layouts: 1.24 us -> 5.31 us
    another operation x11 -> x0, other arithmetic: 3.47 us -> none  [the longest x8 1.24 us: merge(): return jnp.stack([mean, spread + away])]
    ppermute x37 -> x30, starting transfers between devices: 49.4 us -> 52.4 us  [send(): return lax.ppermute(value, AXES, pairs_of(move))]
  transfers between devices with their start and end apart: 37 -> 30, of which waited for: 13 -> 20; matrix products, arithmetic and copies ran while one was open for 2% -> 1% of each run, Pallas kernels for 0% -> 9%
where the time goes in v2:
time: 145 us
  starting transfers between devices  52.4 us (36%)
  waiting for transfers between devices  46.1 us (32%)
  Pallas kernels  39.7 us (27%)
  local copies, waits for them, and re-layouts  5.43 us (4%)
    ppermute x30, starting transfers between devices, send(): return lax.ppermute(value, AXES, pairs_of(move))  52.4 us
    ppermute x30, waiting for transfers between devices, send(): return lax.ppermute(value, AXES, pairs_of(move))  46.1 us
    pallas_call x1, Pallas kernels, shards(): pl.pallas_call(conv_kernel, out_shape=(piece, piece), in_specs=[flag_spec...  17.7 us
    pallas_call x1, Pallas kernels, shards(): pl.pallas_call(own_kernel, out_shape=(piece, piece, acc_shape, acc_shape,...  8.75 us
    pallas_call x2, Pallas kernels, tail(): pl.pallas_call(functools.partial(tail_kernel, order), out_shape=piece, in...  7.93 us
    unnamed x31, local copies, waits for them, and re-layouts  5.31 us
  transfers between devices with their start and end apart: 30, of which 20 were waited for; matrix products, arithmetic and copies ran while one was open for 1% of the time, Pallas kernels for 9%

profile of v2, /device:TPU:33, one launch (start us, length us, event | category | flops | bytes accessed | tf_op | source)
XLA Modules:
  0.0 145.0 jit_solution(2055898465980046668)
XLA Ops:
  0.0 0.7 collective-permute-start
  0.7 0.1 stack.43.flags
  0.8 2.3 %collective-permute-done.other_ref.past_ref = bf16[2,2,240,512]{3,2,1,0:T(8,128)(2,1)S(1)} collective-permute-done((bf16[2,2,240,512]{3,2,1,0:T(8,128)(2,1)}, bf16[2,2,240,512]{3,2,1,0:T(8,128)(2,1)S(1)}, u32[]{:S(2)}, u32[]{:S(2)}) %collective-permute-start) | collective-permute-done | bytes 983072 | tf_op jit(solution)/shard_map/ppermute | solution.py:41
  3.1 1.2 copy-done
  4.3 2.0 %edges.1 = (f32[2,512]{1,0:T(2,128)S(1)}, bf16[4,240,512]{2,1,0:T(8,128)(2,1)S(1)}) custom-call(s32[6]{0:T(128)S(1)} %stack.43.flags, bf16[2,2,240,512]{3,2,1,0:T(8,128)(2,1)S(1)} %copy-done, bf16[2,2,240,512]{3,2,1,0:T(8,128)(2,1)S(1)} %collective-permute-done.other_ref.past_ref), custom_call_target="tpu_custom_call" | custom-call | tf_op jit(solution)/shard_map/edges/pallas_call | solution.py:424
  6.3 1.4 collective-permute-start.1
  7.7 2.6 %collective-permute-start.2 = (f32[2,512]{1,0:T(2,128)S(1)}, f32[2,512]{1,0:T(2,128)S(1)}, u32[]{:S(2)}, u32[]{:S(2)}) collective-permute-start(f32[2,512]{1,0:T(2,128)S(1)} %get-tuple-element.20), channel_id=1, source_target_pairs={{0,2},{1,3},{2,0},{3,1},{4,6},{5,7},{6,4},{7,5},{8,10},{9,11},{10,... | collective-permute-start | bytes 12296 | tf_op jit(solution)/shard_map/ppermute | solution.py:41
  10.3 1.1 collective-permute-start.3
  11.4 0.3 collective-permute-done.2
  11.7 1.4 collective-permute-done.3
  13.2 1.6 %collective-permute-start.4 = (f32[2,512]{1,0:T(2,128)S(1)}, f32[2,512]{1,0:T(2,128)S(1)}, u32[]{:S(2)}, u32[]{:S(2)}) collective-permute-start(f32[2,512]{1,0:T(2,128)S(1)} %select_add_fusion.6), channel_id=1, source_target_pairs={{0,16},{1,17},{2,18},{3,19},{4,20},{5,21},{6,22},{7,23},{8,24},{9,... | collective-permute-start | bytes 12296 | tf_op jit(solution)/shard_map/ppermute | solution.py:41
  14.8 1.2 collective-permute-start.5
  16.0 2.0 %collective-permute-start.6 = (f32[2,512]{1,0:T(2,128)S(1)}, f32[2,512]{1,0:T(2,128)S(1)}, u32[]{:S(2)}, u32[]{:S(2)}) collective-permute-start(f32[2,512]{1,0:T(2,128)S(1)} %select_add_fusion.6), channel_id=1, source_target_pairs={{0,48},{1,49},{2,50},{3,51},{4,52},{5,53},{6,54},{7,55},{8,56},{9,... | collective-permute-start | bytes 12296 | tf_op jit(solution)/shard_map/ppermute | solution.py:41
  17.9 6.5 %collective-permute-start.10 = (bf16[4,240,512]{2,1,0:T(8,128)(2,1)S(1)}, bf16[4,240,512]{2,1,0:T(8,128)(2,1)S(1)}, u32[]{:S(2)}, u32[]{:S(2)}) collective-permute-start(bf16[4,240,512]{2,1,0:T(8,128)(2,1)S(1)} %get-tuple-element.22), channel_id=1, source_target_pairs={{0,1},{1,2},{2,3},{3,4},{4,5},{5,6},{6,7},{7,8},{8,9},{9,10},{10,1... | collective-permute-start | bytes 2949128 | tf_op jit(solution)/shard_map/ppermute | solution.py:41
  24.5 0.1 add_multiply_fusion.5
  24.7 1.3 collective-permute-start.8
  26.0 1.4 collective-permute-start.9
  27.4 1.3 collective-permute-done.7
  28.7 0.1 collective-permute-done.8
  28.7 6.9 %collective-permute-done.9 = f32[2,512]{1,0:T(2,128)S(1)} collective-permute-done((f32[2,512]{1,0:T(2,128)S(1)}, f32[2,512]{1,0:T(2,128)S(1)}, u32[]{:S(2)}, u32[]{:S(2)}) %collective-permute-start.9) | collective-permute-done | bytes 4128 | tf_op jit(solution)/shard_map/ppermute | solution.py:41
  35.7 0.1 add_multiply_fusion.4
  35.8 4.9 %collective-permute-start.11 = (bf16[4,240,512]{2,1,0:T(8,128)(2,1)S(1)}, bf16[4,240,512]{2,1,0:T(8,128)(2,1)S(1)}, u32[]{:S(2)}, u32[]{:S(2)}) collective-permute-start(bf16[4,240,512]{2,1,0:T(8,128)(2,1)S(1)} %collective-permute-done.10.edge_ref), channel_id=1, source_target_pairs={{0,64},{1,65},{2,66},{3,67},{4,68},{5,69},{6,70},{7,71},{8,72},{9,... | collective-permute-start | bytes 2949128 | tf_op jit(solution)/shard_map/ppermute | solution.py:41
  40.8 2.2 %collective-permute-done.11.cross_ref = bf16[4,240,512]{2,1,0:T(8,128)(2,1)S(1)} collective-permute-done((bf16[4,240,512]{2,1,0:T(8,128)(2,1)S(1)}, bf16[4,240,512]{2,1,0:T(8,128)(2,1)S(1)}, u32[]{:S(2)}, u32[]{:S(2)}) %collective-permute-start.11) | collective-permute-done | bytes 983072 | tf_op jit(solution)/shard_map/ppermute | solution.py:41
  43.0 1.2 copy-done.1
  44.2 0.7 copy-done.7
  44.9 0.7 copy-done.8
  45.5 0.7 copy-done.9
  46.2 17.7 %conv.1 = (bf16[480,512]{1,0:T(8,128)(2,1)S(1)}, bf16[480,512]{1,0:T(8,128)(2,1)S(1)}) custom-call(s32[6]{0:T(128)S(1)} %stack.43.flags, f32[2,512]{1,0:T(2,128)S(1)} %select_add_fusion.4.stat_ref, f32[1,512]{1,0:T(1,128)S(1)} %bitcast.21, f32[1,512]{1,0:T(1,128)S(1)} %bitcast.22, bf16[2,2,240,512]{3,2,1,0:T(8,128)(2,1)S(1)} %copy-done.1, ...), custom_call_target="tpu_custom_call" | custom-call | flops 13589544960 | bytes 20000000 | tf_op jit(solution)/shard_map/conv/pallas_call | solution.py:439
  64.0 1.1 stats.1
  65.1 0.5 collective-permute-start.12
  65.6 1.9 %collective-permute-start.22 = (bf16[480,512]{1,0:T(8,128)(2,1)S(1)}, bf16[480,512]{1,0:T(8,128)(2,1)S(1)}, u32[]{:S(2)}, u32[]{:S(2)}) collective-permute-start(bf16[480,512]{1,0:T(8,128)(2,1)S(1)} %get-tuple-element.24.first_ref), channel_id=1, source_target_pairs={{0,0},{1,1},{2,64},{3,65},{4,4},{5,5},{6,68},{7,69},{8,8},{9,9},{1... | collective-permute-start | bytes 1474568 | tf_op jit(solution)/shard_map/ppermute | solution.py:41
  67.6 0.1 collective-permute-start.14
  67.7 1.5 %collective-permute-start.15 = (f32[2,512]{1,0:T(2,128)S(1)}, f32[2,512]{1,0:T(2,128)S(1)}, u32[]{:S(2)}, u32[]{:S(2)}) collective-permute-start(f32[2,512]{1,0:T(2,128)S(1)} %select_add_fusion.3), channel_id=1, source_target_pairs={{0,48},{1,49},{2,50},{3,51},{4,52},{5,53},{6,54},{7,55},{8,56},{9,... | collective-permute-start | bytes 12296 | tf_op jit(solution)/shard_map/ppermute | solution.py:41
  69.2 2.5 %collective-permute-start.23 = (bf16[480,512]{1,0:T(8,128)(2,1)S(1)}, bf16[480,512]{1,0:T(8,128)(2,1)S(1)}, u32[]{:S(2)}, u32[]{:S(2)}) collective-permute-start(bf16[480,512]{1,0:T(8,128)(2,1)S(1)} %get-tuple-element.25.second_ref), channel_id=1, source_target_pairs={{0,1},{1,0},{2,65},{3,64},{4,5},{5,4},{6,69},{7,68},{8,9},{9,8},{1... | collective-permute-start | bytes 1474568 | tf_op jit(solution)/shard_map/ppermute | solution.py:41
  71.7 0.1 add_multiply_fusion.2
  71.8 10.6 %collective-permute-done.22.own_ref = bf16[480,512]{1,0:T(8,128)(2,1)S(1)} collective-permute-done((bf16[480,512]{1,0:T(8,128)(2,1)S(1)}, bf16[480,512]{1,0:T(8,128)(2,1)S(1)}, u32[]{:S(2)}, u32[]{:S(2)}) %collective-permute-start.22) | collective-permute-done | bytes 491552 | tf_op jit(solution)/shard_map/ppermute | solution.py:41
  82.4 0.7 collective-permute-done.23.own_ref
  83.2 0.1 collective-permute-start.24
  83.4 2.0 %collective-permute-start.17 = (f32[2,512]{1,0:T(2,128)S(1)}, f32[2,512]{1,0:T(2,128)S(1)}, u32[]{:S(2)}, u32[]{:S(2)}) collective-permute-start(f32[2,512]{1,0:T(2,128)S(1)} %select_add_fusion.2), channel_id=1, source_target_pairs={{0,8},{1,9},{2,10},{3,11},{4,12},{5,13},{6,14},{7,15},{8,0},{9,1},... | collective-permute-start | bytes 12296 | tf_op jit(solution)/shard_map/ppermute | solution.py:41
  85.4 1.2 collective-permute-start.18
  86.6 0.5 collective-permute-done.16
  87.1 0.4 collective-permute-done.17
  87.5 0.7 collective-permute-done.18
  88.2 0.1 add_multiply_fusion.1
  88.2 4.5 %collective-permute-start.26 = (bf16[960,512]{1,0:T(8,128)(2,1)S(1)}, bf16[960,512]{1,0:T(8,128)(2,1)S(1)}, u32[]{:S(2)}, u32[]{:S(2)}) collective-permute-start(bf16[960,512]{1,0:T(8,128)(2,1)S(1)} %constant_dynamic-update-slice_fusion.mine_ref), channel_id=1, source_target_pairs={{0,4},{1,5},{2,6},{3,7},{4,8},{5,9},{6,10},{7,11},{8,12},{9,13},{1... | collective-permute-start | bytes 2949128 | tf_op jit(solution)/shard_map/ppermute | solution.py:41
  92.8 1.3 collective-permute-start.20
  94.2 1.4 collective-permute-start.21
  95.5 1.0 collective-permute-done.19
  96.5 0.4 collective-permute-done.20
  96.9 0.5 collective-permute-done.21
  97.5 1.9 %collective-permute-start.25 = (bf16[960,512]{1,0:T(8,128)(2,1)S(1)}, bf16[960,512]{1,0:T(8,128)(2,1)S(1)}, u32[]{:S(2)}, u32[]{:S(2)}) collective-permute-start(bf16[960,512]{1,0:T(8,128)(2,1)S(1)} %collective-permute-done.24.swap_ref), channel_id=1, source_target_pairs={{0,4},{1,5},{2,6},{3,7},{4,8},{5,9},{6,10},{7,11},{8,12},{9,13},{1... | collective-permute-start | bytes 2949128 | tf_op jit(solution)/shard_map/ppermute | solution.py:41
  99.5 4.2 %collective-permute-done.26.near_ref = bf16[960,512]{1,0:T(8,128)(2,1)S(1)} collective-permute-done((bf16[960,512]{1,0:T(8,128)(2,1)S(1)}, bf16[960,512]{1,0:T(8,128)(2,1)S(1)}, u32[]{:S(2)}, u32[]{:S(2)}) %collective-permute-start.26) | collective-permute-done | bytes 983072 | tf_op jit(solution)/shard_map/ppermute | solution.py:41
  103.8 8.7 %own.1 = (bf16[480,512]{1,0:T(8,128)(2,1)S(1)}, bf16[480,512]{1,0:T(8,128)(2,1)S(1)}, f32[480,512]{1,0:T(8,128)S(1)}, f32[480,512]{1,0:T(8,128)S(1)}, f32[480,128]{1,0:T(8,128)S(1)}, /*index=5*/f32[480,128]{1,0:T(8,128)S(1)}) custom-call(s32[6]{0:T(128)S(1)} %stack.43.flags, f32[2,512]{1,0:T(2,128)S(1)} %select_add_fusion.stat_ref, f32[1,512]{1,0:T(1,128)S(1)} %bitcast.24, ...), custom_call_target="tpu_custom_call" | custom-call | flops 6000000000 | bytes 8000000 | tf_op jit(solution)/shard_map/own/pallas_call | solution.py:488
  112.5 1.8 %collective-permute-done.25.far_ref = bf16[960,512]{1,0:T(8,128)(2,1)S(1)} collective-permute-done((bf16[960,512]{1,0:T(8,128)(2,1)S(1)}, bf16[960,512]{1,0:T(8,128)(2,1)S(1)}, u32[]{:S(2)}, u32[]{:S(2)}) %collective-permute-start.25) | collective-permute-done | bytes 983072 | tf_op jit(solution)/shard_map/ppermute | solution.py:41
  114.3 4.5 %collective-permute-start.27 = (bf16[960,512]{1,0:T(8,128)(2,1)S(1)}, bf16[960,512]{1,0:T(8,128)(2,1)S(1)}, u32[]{:S(2)}, u32[]{:S(2)}) collective-permute-start(bf16[960,512]{1,0:T(8,128)(2,1)S(1)} %collective-permute-done.25.far_ref), channel_id=1, source_target_pairs={{0,64},{1,65},{2,66},{3,67},{4,68},{5,69},{6,70},{7,71},{8,72},{9,... | collective-permute-start | bytes 2949128 | tf_op jit(solution)/shard_map/ppermute | solution.py:41
  118.8 2.2 %collective-permute-done.27.relay_ref = bf16[960,512]{1,0:T(8,128)(2,1)S(1)} collective-permute-done((bf16[960,512]{1,0:T(8,128)(2,1)S(1)}, bf16[960,512]{1,0:T(8,128)(2,1)S(1)}, u32[]{:S(2)}, u32[]{:S(2)}) %collective-permute-start.27) | collective-permute-done | bytes 983072 | tf_op jit(solution)/shard_map/ppermute | solution.py:41
  121.0 4.0 %tail1.1 = bf16[480,512]{1,0:T(8,128)(2,1)S(1)} custom-call(s32[6]{0:T(128)S(1)} %stack.43.flags, f32[2,512]{1,0:T(2,128)S(1)} %select_add_fusion.stat_ref, f32[1,512]{1,0:T(1,128)S(1)} %bitcast.25, f32[1,512]{1,0:T(1,128)S(1)} %bitcast.28, bf16[960,512]{1,0:T(8,128)(2,1)S(1)} %collective-permute-done.25.far_ref, ...), custom_call_target="tpu_custom_call" | custom-call | flops 3000000000 | bytes 5000000 | tf_op jit(solution)/shard_map/tail1/pallas_call | solution.py:501
  124.9 1.5 %collective-permute-start.29 = (bf16[480,512]{1,0:T(8,128)(2,1)S(1)}, bf16[480,512]{1,0:T(8,128)(2,1)S(1)}, u32[]{:S(2)}, u32[]{:S(2)}) collective-permute-start(bf16[480,512]{1,0:T(8,128)(2,1)S(1)} %tail1.1), channel_id=1, source_target_pairs={{0,1},{1,0},{2,65},{3,64},{4,5},{5,4},{6,69},{7,68},{8,9},{9,8},{1... | collective-permute-start | bytes 1474568 | tf_op jit(solution)/shard_map/ppermute | solution.py:41
  126.4 4.0 %tail0.1 = bf16[480,512]{1,0:T(8,128)(2,1)S(1)} custom-call(s32[6]{0:T(128)S(1)} %stack.43.flags, f32[2,512]{1,0:T(2,128)S(1)} %select_add_fusion.stat_ref, f32[1,512]{1,0:T(1,128)S(1)} %bitcast.26, f32[1,512]{1,0:T(1,128)S(1)} %bitcast.29, bf16[960,512]{1,0:T(8,128)(2,1)S(1)} %collective-permute-done.25.far_ref, ...), custom_call_target="tpu_custom_call" | custom-call | flops 3000000000 | bytes 5000000 | tf_op jit(solution)/shard_map/tail0/pallas_call | solution.py:501
  130.4 3.1 %collective-permute-start.28 = (bf16[480,512]{1,0:T(8,128)(2,1)S(1)}, bf16[480,512]{1,0:T(8,128)(2,1)S(1)}, u32[]{:S(2)}, u32[]{:S(2)}) collective-permute-start(bf16[480,512]{1,0:T(8,128)(2,1)S(1)} %tail0.1), channel_id=1, source_target_pairs={{0,0},{1,1},{2,64},{3,65},{4,4},{5,5},{6,68},{7,69},{8,8},{9,9},{1... | collective-permute-start | bytes 1474568 | tf_op jit(solution)/shard_map/ppermute | solution.py:41
  133.5 1.0 collective-permute-done.29.back1_ref
  134.5 7.6 %collective-permute-done.28.back0_ref = bf16[480,512]{1,0:T(8,128)(2,1)S(1)} collective-permute-done((bf16[480,512]{1,0:T(8,128)(2,1)S(1)}, bf16[480,512]{1,0:T(8,128)(2,1)S(1)}, u32[]{:S(2)}, u32[]{:S(2)}) %collective-permute-start.28) | collective-permute-done | bytes 491552 | tf_op jit(solution)/shard_map/ppermute | solution.py:41
  142.1 0.8 copy-done.14
  142.8 2.2 %place.1 = bf16[2,480,512]{2,1,0:T(8,128)(2,1)} custom-call(s32[6]{0:T(128)} %copy-done.2, bf16[480,512]{1,0:T(8,128)(2,1)} %copy-done.14, bf16[480,512]{1,0:T(8,128)(2,1)} %copy-done.13), custom_call_target="tpu_custom_call" | custom-call | tf_op jit(solution)/shard_map/place/pallas_call | solution.py:528
  (58 shorter events, 0.9 us)
Async XLA Ops:
  0.0 3.1 %collective-permute-start = (bf16[2,2,240,512]{3,2,1,0:T(8,128)(2,1)}, bf16[2,2,240,512]{3,2,1,0:T(8,128)(2,1)S(1)}, u32[]{:S(2)}, u32[]{:S(2)}) collective-permute-start(bf16[2,2,240,512]{3,2,1,0:T(8,128)(2,1)} %own_ref.1), channel_id=1, source_target_pairs={{0,64},{1,65},{2,66},{3,67},{4,68},{5,69},{6,70},{7,71},{8,72},{9,... | collective-permute-start | bytes 2949128 | tf_op jit(solution)/shard_map/ppermute | solution.py:41
  0.8 125.7 %copy-start.2 = (s32[6]{0:T(128)}, s32[6]{0:T(128)S(1)}, u32[]{:S(2)}) copy-start(s32[6]{0:T(128)S(1)} %stack.43.flags) | copy-start | bytes 76
  3.1 1.2 copy-start
  6.3 5.1 %collective-permute-start.1 = (f32[2,512]{1,0:T(2,128)S(1)}, f32[2,512]{1,0:T(2,128)S(1)}, u32[]{:S(2)}, u32[]{:S(2)}) collective-permute-start(f32[2,512]{1,0:T(2,128)S(1)} %get-tuple-element.20), channel_id=1, source_target_pairs={{0,1},{1,2},{2,3},{3,0},{4,5},{5,6},{6,7},{7,4},{8,9},{9,10},{10,1... | collective-permute-start | bytes 12296 | tf_op jit(solution)/shard_map/ppermute | solution.py:41
  7.7 4.0 %collective-permute-start.2 = (f32[2,512]{1,0:T(2,128)S(1)}, f32[2,512]{1,0:T(2,128)S(1)}, u32[]{:S(2)}, u32[]{:S(2)}) collective-permute-start(f32[2,512]{1,0:T(2,128)S(1)} %get-tuple-element.20), channel_id=1, source_target_pairs={{0,2},{1,3},{2,0},{3,1},{4,6},{5,7},{6,4},{7,5},{8,10},{9,11},{10,... | collective-permute-start | bytes 12296 | tf_op jit(solution)/shard_map/ppermute | solution.py:41
  10.3 2.8 %collective-permute-start.3 = (f32[2,512]{1,0:T(2,128)S(1)}, f32[2,512]{1,0:T(2,128)S(1)}, u32[]{:S(2)}, u32[]{:S(2)}) collective-permute-start(f32[2,512]{1,0:T(2,128)S(1)} %get-tuple-element.20), channel_id=1, source_target_pairs={{0,3},{1,0},{2,1},{3,2},{4,7},{5,4},{6,5},{7,6},{8,11},{9,8},{10,9... | collective-permute-start | bytes 12296 | tf_op jit(solution)/shard_map/ppermute | solution.py:41
  13.2 11.3 %collective-permute-start.4 = (f32[2,512]{1,0:T(2,128)S(1)}, f32[2,512]{1,0:T(2,128)S(1)}, u32[]{:S(2)}, u32[]{:S(2)}) collective-permute-start(f32[2,512]{1,0:T(2,128)S(1)} %select_add_fusion.6), channel_id=1, source_target_pairs={{0,16},{1,17},{2,18},{3,19},{4,20},{5,21},{6,22},{7,23},{8,24},{9,... | collective-permute-start | bytes 12296 | tf_op jit(solution)/shard_map/ppermute | solution.py:41
  14.8 9.7 %collective-permute-start.5 = (f32[2,512]{1,0:T(2,128)S(1)}, f32[2,512]{1,0:T(2,128)S(1)}, u32[]{:S(2)}, u32[]{:S(2)}) collective-permute-start(f32[2,512]{1,0:T(2,128)S(1)} %select_add_fusion.6), channel_id=1, source_target_pairs={{0,32},{1,33},{2,34},{3,35},{4,36},{5,37},{6,38},{7,39},{8,40},{9,... | collective-permute-start | bytes 12296 | tf_op jit(solution)/shard_map/ppermute | solution.py:41
  16.0 8.5 %collective-permute-start.6 = (f32[2,512]{1,0:T(2,128)S(1)}, f32[2,512]{1,0:T(2,128)S(1)}, u32[]{:S(2)}, u32[]{:S(2)}) collective-permute-start(f32[2,512]{1,0:T(2,128)S(1)} %select_add_fusion.6), channel_id=1, source_target_pairs={{0,48},{1,49},{2,50},{3,51},{4,52},{5,53},{6,54},{7,55},{8,56},{9,... | collective-permute-start | bytes 12296 | tf_op jit(solution)/shard_map/ppermute | solution.py:41
  17.9 17.9 %collective-permute-start.10 = (bf16[4,240,512]{2,1,0:T(8,128)(2,1)S(1)}, bf16[4,240,512]{2,1,0:T(8,128)(2,1)S(1)}, u32[]{:S(2)}, u32[]{:S(2)}) collective-permute-start(bf16[4,240,512]{2,1,0:T(8,128)(2,1)S(1)} %get-tuple-element.22), channel_id=1, source_target_pairs={{0,1},{1,2},{2,3},{3,4},{4,5},{5,6},{6,7},{7,8},{8,9},{9,10},{10,1... | collective-permute-start | bytes 2949128 | tf_op jit(solution)/shard_map/ppermute | solution.py:41
  24.7 4.0 %collective-permute-start.7 = (f32[2,512]{1,0:T(2,128)S(1)}, f32[2,512]{1,0:T(2,128)S(1)}, u32[]{:S(2)}, u32[]{:S(2)}) collective-permute-start(f32[2,512]{1,0:T(2,128)S(1)} %select_add_fusion.5), channel_id=1, source_target_pairs={{0,4},{1,5},{2,6},{3,7},{4,8},{5,9},{6,10},{7,11},{8,12},{9,13},{1... | collective-permute-start | bytes 12296 | tf_op jit(solution)/shard_map/ppermute | solution.py:41
  24.7 4.0 %collective-permute-start.8 = (f32[2,512]{1,0:T(2,128)S(1)}, f32[2,512]{1,0:T(2,128)S(1)}, u32[]{:S(2)}, u32[]{:S(2)}) collective-permute-start(f32[2,512]{1,0:T(2,128)S(1)} %select_add_fusion.5), channel_id=1, source_target_pairs={{0,8},{1,9},{2,10},{3,11},{4,12},{5,13},{6,14},{7,15},{8,0},{9,1},... | collective-permute-start | bytes 12296 | tf_op jit(solution)/shard_map/ppermute | solution.py:41
  26.0 9.7 %collective-permute-start.9 = (f32[2,512]{1,0:T(2,128)S(1)}, f32[2,512]{1,0:T(2,128)S(1)}, u32[]{:S(2)}, u32[]{:S(2)}) collective-permute-start(f32[2,512]{1,0:T(2,128)S(1)} %select_add_fusion.5), channel_id=1, source_target_pairs={{0,12},{1,13},{2,14},{3,15},{4,0},{5,1},{6,2},{7,3},{8,4},{9,5},{1... | collective-permute-start | bytes 12296 | tf_op jit(solution)/shard_map/ppermute | solution.py:41
  35.8 7.1 %collective-permute-start.11 = (bf16[4,240,512]{2,1,0:T(8,128)(2,1)S(1)}, bf16[4,240,512]{2,1,0:T(8,128)(2,1)S(1)}, u32[]{:S(2)}, u32[]{:S(2)}) collective-permute-start(bf16[4,240,512]{2,1,0:T(8,128)(2,1)S(1)} %collective-permute-done.10.edge_ref), channel_id=1, source_target_pairs={{0,64},{1,65},{2,66},{3,67},{4,68},{5,69},{6,70},{7,71},{8,72},{9,... | collective-permute-start | bytes 2949128 | tf_op jit(solution)/shard_map/ppermute | solution.py:41
  43.0 1.2 copy-start.1
  44.2 0.7 copy-start.7
  44.9 0.7 copy-start.8
  45.5 0.7 copy-start.9
  64.0 39.8 %copy-start.3 = (bf16[512,512]{1,0:T(8,128)(2,1)S(1)}, bf16[512,512]{1,0:T(8,128)(2,1)}, u32[]{:S(2)}) copy-start(bf16[512,512]{1,0:T(8,128)(2,1)} %wq_ref.1) | copy-start | bytes 1572868
  64.0 39.8 %copy-start.4 = (bf16[512,512]{1,0:T(8,128)(2,1)S(1)}, bf16[512,512]{1,0:T(8,128)(2,1)}, u32[]{:S(2)}) copy-start(bf16[512,512]{1,0:T(8,128)(2,1)} %wk_ref.1) | copy-start | bytes 1572868
  64.0 39.8 %copy-start.10 = (f32[512]{0:T(512)S(1)}, f32[512]{0:T(512)}, u32[]{:S(2)}) copy-start(f32[512]{0:T(512)} %param.17) | copy-start | bytes 6148
  64.0 39.8 %copy-start.11 = (f32[512]{0:T(512)S(1)}, f32[512]{0:T(512)}, u32[]{:S(2)}) copy-start(f32[512]{0:T(512)} %param.18) | copy-start | bytes 6148
  65.1 55.9 %copy-start.5 = (bf16[512,512]{1,0:T(8,128)(2,1)S(1)}, bf16[512,512]{1,0:T(8,128)(2,1)}, u32[]{:S(2)}) copy-start(bf16[512,512]{1,0:T(8,128)(2,1)} %wv_ref.3) | copy-start | bytes 1572868
  65.1 55.9 %copy-start.6 = (bf16[512,512]{1,0:T(8,128)(2,1)S(1)}, bf16[512,512]{1,0:T(8,128)(2,1)}, u32[]{:S(2)}) copy-start(bf16[512,512]{1,0:T(8,128)(2,1)} %wo_ref.3) | copy-start | bytes 1572868
  65.1 55.9 %copy-start.12 = (f32[512]{0:T(512)S(1)}, f32[512]{0:T(512)}, u32[]{:S(2)}) copy-start(f32[512]{0:T(512)} %param.23) | copy-start | bytes 6148
  65.1 2.4 %collective-permute-start.12 = (f32[2,512]{1,0:T(2,128)S(1)}, f32[2,512]{1,0:T(2,128)S(1)}, u32[]{:S(2)}, u32[]{:S(2)}) collective-permute-start(f32[2,512]{1,0:T(2,128)S(1)} %stats.1), channel_id=1, source_target_pairs={{0,64},{1,65},{2,66},{3,67},{4,68},{5,69},{6,70},{7,71},{8,72},{9,... | collective-permute-start | bytes 12296 | tf_op jit(solution)/shard_map/ppermute | solution.py:41
  65.6 16.9 %collective-permute-start.22 = (bf16[480,512]{1,0:T(8,128)(2,1)S(1)}, bf16[480,512]{1,0:T(8,128)(2,1)S(1)}, u32[]{:S(2)}, u32[]{:S(2)}) collective-permute-start(bf16[480,512]{1,0:T(8,128)(2,1)S(1)} %get-tuple-element.24.first_ref), channel_id=1, source_target_pairs={{0,0},{1,1},{2,64},{3,65},{4,4},{5,5},{6,68},{7,69},{8,8},{9,9},{1... | collective-permute-start | bytes 1474568 | tf_op jit(solution)/shard_map/ppermute | solution.py:41
  67.6 4.1 %collective-permute-start.13 = (f32[2,512]{1,0:T(2,128)S(1)}, f32[2,512]{1,0:T(2,128)S(1)}, u32[]{:S(2)}, u32[]{:S(2)}) collective-permute-start(f32[2,512]{1,0:T(2,128)S(1)} %select_add_fusion.3), channel_id=1, source_target_pairs={{0,16},{1,17},{2,18},{3,19},{4,20},{5,21},{6,22},{7,23},{8,24},{9,... | collective-permute-start | bytes 12296 | tf_op jit(solution)/shard_map/ppermute | solution.py:41
  67.6 4.1 %collective-permute-start.14 = (f32[2,512]{1,0:T(2,128)S(1)}, f32[2,512]{1,0:T(2,128)S(1)}, u32[]{:S(2)}, u32[]{:S(2)}) collective-permute-start(f32[2,512]{1,0:T(2,128)S(1)} %select_add_fusion.3), channel_id=1, source_target_pairs={{0,32},{1,33},{2,34},{3,35},{4,36},{5,37},{6,38},{7,39},{8,40},{9,... | collective-permute-start | bytes 12296 | tf_op jit(solution)/shard_map/ppermute | solution.py:41
  67.7 4.0 %collective-permute-start.15 = (f32[2,512]{1,0:T(2,128)S(1)}, f32[2,512]{1,0:T(2,128)S(1)}, u32[]{:S(2)}, u32[]{:S(2)}) collective-permute-start(f32[2,512]{1,0:T(2,128)S(1)} %select_add_fusion.3), channel_id=1, source_target_pairs={{0,48},{1,49},{2,50},{3,51},{4,52},{5,53},{6,54},{7,55},{8,56},{9,... | collective-permute-start | bytes 12296 | tf_op jit(solution)/shard_map/ppermute | solution.py:41
  69.2 14.0 %collective-permute-start.23 = (bf16[480,512]{1,0:T(8,128)(2,1)S(1)}, bf16[480,512]{1,0:T(8,128)(2,1)S(1)}, u32[]{:S(2)}, u32[]{:S(2)}) collective-permute-start(bf16[480,512]{1,0:T(8,128)(2,1)S(1)} %get-tuple-element.25.second_ref), channel_id=1, source_target_pairs={{0,1},{1,0},{2,65},{3,64},{4,5},{5,4},{6,69},{7,68},{8,9},{9,8},{1... | collective-permute-start | bytes 1474568 | tf_op jit(solution)/shard_map/ppermute | solution.py:41
  83.2 14.3 %collective-permute-start.24 = (bf16[960,512]{1,0:T(8,128)(2,1)S(1)}, bf16[960,512]{1,0:T(8,128)(2,1)S(1)}, u32[]{:S(2)}, u32[]{:S(2)}) collective-permute-start(bf16[960,512]{1,0:T(8,128)(2,1)S(1)} %constant_dynamic-update-slice_fusion.mine_ref), channel_id=1, source_target_pairs={{0,64},{1,65},{2,66},{3,67},{4,68},{5,69},{6,70},{7,71},{8,72},{9,... | collective-permute-start | bytes 2949128 | tf_op jit(solution)/shard_map/ppermute | solution.py:41
  83.4 3.7 %collective-permute-start.16 = (f32[2,512]{1,0:T(2,128)S(1)}, f32[2,512]{1,0:T(2,128)S(1)}, u32[]{:S(2)}, u32[]{:S(2)}) collective-permute-start(f32[2,512]{1,0:T(2,128)S(1)} %select_add_fusion.2), channel_id=1, source_target_pairs={{0,4},{1,5},{2,6},{3,7},{4,8},{5,9},{6,10},{7,11},{8,12},{9,13},{1... | collective-permute-start | bytes 12296 | tf_op jit(solution)/shard_map/ppermute | solution.py:41
  83.4 4.0 %collective-permute-start.17 = (f32[2,512]{1,0:T(2,128)S(1)}, f32[2,512]{1,0:T(2,128)S(1)}, u32[]{:S(2)}, u32[]{:S(2)}) collective-permute-start(f32[2,512]{1,0:T(2,128)S(1)} %select_add_fusion.2), channel_id=1, source_target_pairs={{0,8},{1,9},{2,10},{3,11},{4,12},{5,13},{6,14},{7,15},{8,0},{9,1},... | collective-permute-start | bytes 12296 | tf_op jit(solution)/shard_map/ppermute | solution.py:41
  85.4 2.8 %collective-permute-start.18 = (f32[2,512]{1,0:T(2,128)S(1)}, f32[2,512]{1,0:T(2,128)S(1)}, u32[]{:S(2)}, u32[]{:S(2)}) collective-permute-start(f32[2,512]{1,0:T(2,128)S(1)} %select_add_fusion.2), channel_id=1, source_target_pairs={{0,12},{1,13},{2,14},{3,15},{4,0},{5,1},{6,2},{7,3},{8,4},{9,5},{1... | collective-permute-start | bytes 12296 | tf_op jit(solution)/shard_map/ppermute | solution.py:41
  88.2 15.5 %collective-permute-start.26 = (bf16[960,512]{1,0:T(8,128)(2,1)S(1)}, bf16[960,512]{1,0:T(8,128)(2,1)S(1)}, u32[]{:S(2)}, u32[]{:S(2)}) collective-permute-start(bf16[960,512]{1,0:T(8,128)(2,1)S(1)} %constant_dynamic-update-slice_fusion.mine_ref), channel_id=1, source_target_pairs={{0,4},{1,5},{2,6},{3,7},{4,8},{5,9},{6,10},{7,11},{8,12},{9,13},{1... | collective-permute-start | bytes 2949128 | tf_op jit(solution)/shard_map/ppermute | solution.py:41
  92.8 3.7 %collective-permute-start.19 = (f32[2,512]{1,0:T(2,128)S(1)}, f32[2,512]{1,0:T(2,128)S(1)}, u32[]{:S(2)}, u32[]{:S(2)}) collective-permute-start(f32[2,512]{1,0:T(2,128)S(1)} %select_add_fusion.1), channel_id=1, source_target_pairs={{0,1},{1,2},{2,3},{3,0},{4,5},{5,6},{6,7},{7,4},{8,9},{9,10},{10,1... | collective-permute-start | bytes 12296 | tf_op jit(solution)/shard_map/ppermute | solution.py:41
  92.8 4.0 %collective-permute-start.20 = (f32[2,512]{1,0:T(2,128)S(1)}, f32[2,512]{1,0:T(2,128)S(1)}, u32[]{:S(2)}, u32[]{:S(2)}) collective-permute-start(f32[2,512]{1,0:T(2,128)S(1)} %select_add_fusion.1), channel_id=1, source_target_pairs={{0,2},{1,3},{2,0},{3,1},{4,6},{5,7},{6,4},{7,5},{8,10},{9,11},{10,... | collective-permute-start | bytes 12296 | tf_op jit(solution)/shard_map/ppermute | solution.py:41
  94.2 3.3 %collective-permute-start.21 = (f32[2,512]{1,0:T(2,128)S(1)}, f32[2,512]{1,0:T(2,128)S(1)}, u32[]{:S(2)}, u32[]{:S(2)}) collective-permute-start(f32[2,512]{1,0:T(2,128)S(1)} %select_add_fusion.1), channel_id=1, source_target_pairs={{0,3},{1,0},{2,1},{3,2},{4,7},{5,4},{6,5},{7,6},{8,11},{9,8},{10,9... | collective-permute-start | bytes 12296 | tf_op jit(solution)/shard_map/ppermute | solution.py:41
  97.5 16.8 %collective-permute-start.25 = (bf16[960,512]{1,0:T(8,128)(2,1)S(1)}, bf16[960,512]{1,0:T(8,128)(2,1)S(1)}, u32[]{:S(2)}, u32[]{:S(2)}) collective-permute-start(bf16[960,512]{1,0:T(8,128)(2,1)S(1)} %collective-permute-done.24.swap_ref), channel_id=1, source_target_pairs={{0,4},{1,5},{2,6},{3,7},{4,8},{5,9},{6,10},{7,11},{8,12},{9,13},{1... | collective-permute-start | bytes 2949128 | tf_op jit(solution)/shard_map/ppermute | solution.py:41
  114.3 6.7 %collective-permute-start.27 = (bf16[960,512]{1,0:T(8,128)(2,1)S(1)}, bf16[960,512]{1,0:T(8,128)(2,1)S(1)}, u32[]{:S(2)}, u32[]{:S(2)}) collective-permute-start(bf16[960,512]{1,0:T(8,128)(2,1)S(1)} %collective-permute-done.25.far_ref), channel_id=1, source_target_pairs={{0,64},{1,65},{2,66},{3,67},{4,68},{5,69},{6,70},{7,71},{8,72},{9,... | collective-permute-start | bytes 2949128 | tf_op jit(solution)/shard_map/ppermute | solution.py:41
  124.9 9.5 %collective-permute-start.29 = (bf16[480,512]{1,0:T(8,128)(2,1)S(1)}, bf16[480,512]{1,0:T(8,128)(2,1)S(1)}, u32[]{:S(2)}, u32[]{:S(2)}) collective-permute-start(bf16[480,512]{1,0:T(8,128)(2,1)S(1)} %tail1.1), channel_id=1, source_target_pairs={{0,1},{1,0},{2,65},{3,64},{4,5},{5,4},{6,69},{7,68},{8,9},{9,8},{1... | collective-permute-start | bytes 1474568 | tf_op jit(solution)/shard_map/ppermute | solution.py:41
  130.4 11.7 %collective-permute-start.28 = (bf16[480,512]{1,0:T(8,128)(2,1)S(1)}, bf16[480,512]{1,0:T(8,128)(2,1)S(1)}, u32[]{:S(2)}, u32[]{:S(2)}) collective-permute-start(bf16[480,512]{1,0:T(8,128)(2,1)S(1)} %tail0.1), channel_id=1, source_target_pairs={{0,0},{1,1},{2,64},{3,65},{4,4},{5,5},{6,68},{7,69},{8,8},{9,9},{1... | collective-permute-start | bytes 1474568 | tf_op jit(solution)/shard_map/ppermute | solution.py:41
  134.5 7.6 %copy-start.13 = (bf16[480,512]{1,0:T(8,128)(2,1)}, bf16[480,512]{1,0:T(8,128)(2,1)S(1)}, u32[]{:S(2)}) copy-start(bf16[480,512]{1,0:T(8,128)(2,1)S(1)} %collective-permute-done.29.back1_ref) | copy-start | bytes 1474564
  142.1 0.8 copy-start.14

commit v3 on v2

--- a/solution.py
+++ b/solution.py
@@ -141,40 +141,41 @@
     stat_ref[1:2, :] = spread[0:1]
 
 
-def edge_kernel(flags, feat_ref, other_ref, stat_ref, edge_ref):
-    frames = feat_ref.shape[0]
+def stat_kernel(flags, *refs):
+    local_stats(
+        [functools.partial(lambda ref, i: ref[i], ref, i) for ref in refs[:-1] for i in range(ref.shape[0])],
+        refs[-1],
+    )
+
+
+def edge_kernel(flags, feat_ref, other_ref, first_ref, stat_ref, edge_ref):
+    frames = feat_ref.shape[0] // 2
     core = flags[0]
     row = 1 - core
     for f in range(frames):
-        edge_ref[frames * core + f] = feat_ref[f, row]
-        edge_ref[frames * (1 - core) + f] = other_ref[f, row]
-    local_stats(
-        [
-            functools.partial(lambda ref, f, h: ref[f, h], ref, f, h)
-            for ref in (feat_ref, other_ref)
-            for f in range(frames)
-            for h in range(2)
-        ],
-        stat_ref,
-    )
-
-
-def affine(stat_ref, gain_ref, bias_ref):
-    scale = lax.rsqrt(stat_ref[1:2, :] + EPS) * gain_ref[...]
-    return scale, bias_ref[...] - stat_ref[0:1, :] * scale
+        edge_ref[frames * core + f] = feat_ref[2 * f + row]
+        edge_ref[frames * (1 - core) + f] = other_ref[2 * f + row]
+    stat_kernel(flags, other_ref, stat_ref)
+    mean, spread = stat_ref[0:1, :], stat_ref[1:2, :]
+    away = (mean - first_ref[0:1, :]) * 0.5
+    stat_ref[0:1, :] = (mean + first_ref[0:1, :]) * 0.5
+    stat_ref[1:2, :] = (spread + first_ref[1:2, :]) * 0.5 + away * away
+
+
+def affine(stat_ref, vector_ref, first):
+    scale = lax.rsqrt(stat_ref[1:2, :] + EPS) * vector_ref[first : first + 1, :]
+    return scale, vector_ref[first + 1 : first + 2, :] - stat_ref[0:1, :] * scale
 
 
 def conv_kernel(
     flags,
     stat_ref,
-    gain_ref,
-    bias_ref,
+    vector_ref,
     own_ref,
     past_ref,
     edge_ref,
     cross_ref,
     weight_ref,
-    conv_bias_ref,
     out0_ref,
     out1_ref,
     act_ref,
@@ -190,7 +191,7 @@
     ]
     for copy in copies:
         copy.start()
-    scale, shift = affine(stat_ref, gain_ref, bias_ref)
+    scale, shift = affine(stat_ref, vector_ref, 0)
     half_scale, half_shift = scale * 0.5, shift * 0.5
     zero = jnp.zeros((1, chans), BF)
 
@@ -233,20 +234,8 @@
     for p in range(2):
         frame = (parity + p) & 1
         for h in range(2):
-            value = own_ref[frame, h].astype(F32) + (acc_ref[frame, h] + conv_bias_ref[...])
+            value = own_ref[frame, h].astype(F32) + (acc_ref[frame, h] + vector_ref[2:3, :])
             outs[p][h * width : (h + 1) * width, :] = value.astype(BF)
-
-
-def stat_kernel(first_ref, second_ref, stat_ref):
-    half = first_ref.shape[0] // 2
-    local_stats(
-        [
-            functools.partial(lambda ref, h: ref[h * half : (h + 1) * half, :], ref, h)
-            for ref in (first_ref, second_ref)
-            for h in range(2)
-        ],
-        stat_ref,
-    )
 
 
 def dot_t(a, b):
@@ -300,8 +289,7 @@
 def own_kernel(
     flags,
     stat_ref,
-    gain_ref,
-    bias_ref,
+    vector_ref,
     mine_ref,
     swap_ref,
     near_ref,
@@ -316,7 +304,7 @@
     key_ref,
 ):
     cells, chans = query0_ref.shape
-    scale, shift = affine(stat_ref, gain_ref, bias_ref)
+    scale, shift = affine(stat_ref, vector_ref, 3)
     for i, ref in enumerate((mine_ref, swap_ref, near_ref)):
         raw = ref[...].astype(F32)
         key_ref[2 * i * cells : 2 * (i + 1) * cells, :] = (raw * scale + shift).astype(BF)
@@ -338,8 +326,7 @@
     order,
     flags,
     stat_ref,
-    gain_ref,
-    bias_ref,
+    vector_ref,
     far_ref,
     relay_ref,
     query_ref,
@@ -348,12 +335,11 @@
     own_ref,
     wv_ref,
     wo_ref,
-    out_bias_ref,
     out_ref,
     key_ref,
 ):
     cells = out_ref.shape[0]
-    scale, shift = affine(stat_ref, gain_ref, bias_ref)
+    scale, shift = affine(stat_ref, vector_ref, 3)
     for i, ref in enumerate((far_ref, relay_ref)):
         raw = ref[...].astype(F32)
         key_ref[2 * i * cells : 2 * (i + 1) * cells, :] = (raw * scale + shift).astype(BF)
@@ -367,7 +353,7 @@
     attn = jnp.dot(mixed, wv_ref[...], preferred_element_type=F32).astype(BF)
     result = jnp.dot(attn, wo_ref[...], preferred_element_type=F32)
     own = own_ref[...].astype(F32)
-    out_ref[...] = (own + out_bias_ref[...] + result).astype(BF)
+    out_ref[...] = (own + vector_ref[5:6, :] + result).astype(BF)
 
 
 def place_kernel(flags, back0_ref, back1_ref, out_ref):
@@ -415,31 +401,49 @@
     block = z * NX + x
     stripe = block * NY + y
     i32 = lambda *v: jnp.stack([jnp.asarray(a, jnp.int32) for a in v])
-    line = lambda v: v.reshape(1, chans)
 
     stat_shape = jax.ShapeDtypeStruct((2, chans), F32)
     flags = i32(t, y & 1, stripe > 0, stripe < NZ * NX * NY - 1, block > 0, block < NZ * NX - 1)
+    vectors = jnp.stack([norm1_gain, norm1_bias, conv_bias, norm2_gain, norm2_bias, out_bias])
     swap = turned("tm", 1)
+    stat_shape = jax.ShapeDtypeStruct((2, chans), F32)
+
+    def stats_of(*pieces):
+        return pl.pallas_call(
+            stat_kernel,
+            out_shape=stat_shape,
+            in_specs=[flag_spec()] + [whole()] * len(pieces),
+            out_specs=whole(),
+            compiler_params=params(16),
+            name="stats",
+        )(flags, *[a.reshape(-1, width, chans) for a in pieces])
+
     other = send(feat, swap)
     stats, edge = pl.pallas_call(
         edge_kernel,
         out_shape=(stat_shape, jax.ShapeDtypeStruct((2 * frames, width, chans), BF)),
-        in_specs=[flag_spec(), whole(), whole()],
+        in_specs=[flag_spec(), whole(), whole(), whole()],
         out_specs=(whole(), whole()),
         compiler_params=params(16),
         name="edges",
-    )(flags, feat, other)
-    parts = gathered(stats, "y")
-    edge = send(after(edge, parts[1]), edges_out)
-    stats = over(over(merge(parts), "z"), "x")
-    cross = send(after(edge, stats), swap)
+    )(
+        flags,
+        feat.reshape(-1, width, chans),
+        other.reshape(-1, width, chans),
+        stats_of(feat),
+    )
+    edge = send(edge, edges_out)
+    stats = over(stats, "z")
+    edge, stats = lax.optimization_barrier((edge, stats))
+    cross = send(edge, swap)
+    stats = over(over(stats, "x"), "y")
 
     cells = rows * width
     piece = jax.ShapeDtypeStruct((cells, chans), BF)
     own0, own1 = pl.pallas_call(
         conv_kernel,
         out_shape=(piece, piece),
-        in_specs=[flag_spec()] + [whole()] * 7 + [remote(), whole()],
+        in_specs=[flag_spec()] + [whole()] * 6 + [remote()],
         out_specs=(whole(),) * 2,
         scratch_shapes=[
             pltpu.VMEM((4, 4, width, 3 * chans), BF),
@@ -453,27 +457,17 @@
     )(
         flags,
         stats,
-        line(norm1_gain),
-        line(norm1_bias),
+        vectors,
         feat,
         other,
         edge,
         cross,
         conv_weight.reshape(9, 3 * chans, chans),
-        line(conv_bias),
     )
 
     mine0 = send(own0, to_frames(0))
     mine1 = send(own1, to_frames(1))
-    stats2 = pl.pallas_call(
-        stat_kernel,
-        out_shape=stat_shape,
-        in_specs=[whole(), whole()],
-        out_specs=whole(),
-        compiler_params=params(16),
-        cost_estimate=cost(8e9, 2e6),
-        name="stats",
-    )(own0, own1)
+    stats2 = stats_of(own0, own1)
     stats2 = over(over(stats2, "tm"), "z")
     mine = jnp.concatenate([mine0, mine1])
     swapped = send(mine, swap)
@@ -482,13 +476,13 @@
     far = send(after(swapped, stats2), blocks_out)
     stats2 = over(stats2, "y")
 
-    norm2 = (stats2, line(norm2_gain), line(norm2_bias))
+    norm2 = (stats2, vectors)
     acc_shape = jax.ShapeDtypeStruct((cells, chans), F32)
     sum_shape = jax.ShapeDtypeStruct((cells, 128), F32)
     query0, query1, acc0, acc1, sum0, sum1 = pl.pallas_call(
         own_kernel,
         out_shape=(piece, piece, acc_shape, acc_shape, sum_shape, sum_shape),
-        in_specs=[flag_spec()] + [whole()] * 8,
+        in_specs=[flag_spec()] + [whole()] * 7,
         out_specs=(whole(),) * 6,
         scratch_shapes=[pltpu.VMEM((OWN_KEYS, chans), BF)],
         compiler_params=params(OWN),
@@ -501,7 +495,7 @@
         return pl.pallas_call(
             functools.partial(tail_kernel, order),
             out_shape=piece,
-            in_specs=[flag_spec()] + [whole()] * 12,
+            in_specs=[flag_spec()] + [whole()] * 10,
             out_specs=whole(),
             scratch_shapes=[pltpu.VMEM((4 * cells, chans), BF)],
             compiler_params=params(TAIL),
@@ -518,7 +512,6 @@
             own,
             w_value,
             w_out,
-            line(out_bias),
         )
 
     out0 = tail(0, query0, acc0, sum0, mine0)
@@ -530,6 +523,7 @@
         out_shape=jax.ShapeDtypeStruct((frames, cells, chans), BF),
         in_specs=[flag_spec(), whole(), whole()],
         out_specs=whole(),
+        compiler_params=params(8),
         name="place",
     )(flags, back0, back1)
     return output.reshape(feat.shape)

time: 145 us -> 140 us (0.966)
  waiting for transfers between devices: 46.1 us -> 35.3 us
  starting transfers between devices: 52.4 us -> 58.6 us
  local copies, waits for them, and re-layouts: 5.43 us -> 3.36 us
    ppermute x30, waiting for transfers between devices: 46.1 us -> 35.3 us  [send(): return lax.ppermute(value, AXES, pairs_of(move))]
    ppermute x30, starting transfers between devices: 52.4 us -> 58.6 us  [send(): return lax.ppermute(value, AXES, pairs_of(move))]
    unnamed x31 -> x13, local copies, waits for them, and re-layouts: 5.31 us -> 2.46 us
    pallas_call x1 -> x2, Pallas kernels: 1.06 us -> 3.2 us  [stats_of(): pl.pallas_call(stat_kernel, out_shape=stat_shape, in_specs=[flag_spec()]...]
  transfers between devices with their start and end apart: 30 -> 30, of which waited for: 20 -> 15; matrix products, arithmetic and copies ran while one was open for 1% -> 1% of each run, Pallas kernels for 9% -> 10%
where the time goes in v3:
time: 140 us; the launch traced here: 139 us
  starting transfers between devices  58.6 us (42%)
  Pallas kernels  40.8 us (29%)
  waiting for transfers between devices  35.3 us (25%)
  local copies, waits for them, and re-layouts  3.36 us (2%)
    ppermute x30, starting transfers between devices, send(): return lax.ppermute(value, AXES, pairs_of(move))  58.6 us
    ppermute x30, waiting for transfers between devices, send(): return lax.ppermute(value, AXES, pairs_of(move))  35.3 us
    pallas_call x1, Pallas kernels, shards(): pl.pallas_call(conv_kernel, out_shape=(piece, piece), in_specs=[flag_spec...  17.7 us
    pallas_call x1, Pallas kernels, shards(): pl.pallas_call(own_kernel, out_shape=(piece, piece, acc_shape, acc_shape,...  8.77 us
    pallas_call x2, Pallas kernels, tail(): pl.pallas_call(functools.partial(tail_kernel, order), out_shape=piece, in...  8 us
    pallas_call x2, Pallas kernels, stats_of(): pl.pallas_call(stat_kernel, out_shape=stat_shape, in_specs=[flag_spec()]...  3.2 us
  transfers between devices with their start and end apart: 30, of which 15 were waited for; matrix products, arithmetic and copies ran while one was open for 1% of the time, Pallas kernels for 10%

profile of v3, /device:TPU:33, one launch (start us, length us, event | category | flops | bytes accessed | tf_op | source)
XLA Modules:
  0.0 139.3 jit_solution(12337766818994807060)
XLA Ops:
  0.0 0.7 collective-permute-start
  0.7 0.1 stack.64.flags
  0.8 1.2 copy-done
  2.0 1.6 %stats.2.first_ref = f32[2,512]{1,0:T(2,128)S(1)} custom-call(s32[6]{0:T(128)S(1)} %stack.64.flags, bf16[4,240,512]{2,1,0:T(8,128)(2,1)S(1)} %bitcast.25), custom_call_target="tpu_custom_call" | custom-call | tf_op jit(solution)/shard_map/stats/pallas_call | solution.py:412
  3.6 1.6 %edges.1 = (f32[2,512]{1,0:T(2,128)S(1)}, bf16[4,240,512]{2,1,0:T(8,128)(2,1)S(1)}) custom-call(s32[6]{0:T(128)S(1)} %stack.64.flags, bf16[4,240,512]{2,1,0:T(8,128)(2,1)S(1)} %bitcast.26, bf16[4,240,512]{2,1,0:T(8,128)(2,1)S(1)} %bitcast.27, f32[2,512]{1,0:T(2,128)S(1)} %stats.2.first_ref), custom_call_target="tpu_custom_call" | custom-call | tf_op jit(solution)/shard_map/edges/pallas_call | solution.py:422
  5.2 6.4 %collective-permute-start.1 = (bf16[4,240,512]{2,1,0:T(8,128)(2,1)S(1)}, bf16[4,240,512]{2,1,0:T(8,128)(2,1)S(1)}, u32[]{:S(2)}, u32[]{:S(2)}) collective-permute-start(bf16[4,240,512]{2,1,0:T(8,128)(2,1)S(1)} %get-tuple-element.20), channel_id=1, source_target_pairs={{0,1},{1,2},{2,3},{3,4},{4,5},{5,6},{6,7},{7,8},{8,9},{9,10},{10,1... | collective-permute-start | bytes 2949128 | tf_op jit(solution)/shard_map/ppermute | solution.py:41
  11.6 1.7 %collective-permute-start.2 = (f32[2,512]{1,0:T(2,128)S(1)}, f32[2,512]{1,0:T(2,128)S(1)}, u32[]{:S(2)}, u32[]{:S(2)}) collective-permute-start(f32[2,512]{1,0:T(2,128)S(1)} %get-tuple-element.21), channel_id=1, source_target_pairs={{0,16},{1,17},{2,18},{3,19},{4,20},{5,21},{6,22},{7,23},{8,24},{9,... | collective-permute-start | bytes 12296 | tf_op jit(solution)/shard_map/ppermute | solution.py:41
  13.3 1.4 %collective-permute-start.3 = (f32[2,512]{1,0:T(2,128)S(1)}, f32[2,512]{1,0:T(2,128)S(1)}, u32[]{:S(2)}, u32[]{:S(2)}) collective-permute-start(f32[2,512]{1,0:T(2,128)S(1)} %get-tuple-element.21), channel_id=1, source_target_pairs={{0,32},{1,33},{2,34},{3,35},{4,36},{5,37},{6,38},{7,39},{8,40},{9,... | collective-permute-start | bytes 12296 | tf_op jit(solution)/shard_map/ppermute | solution.py:41
  14.7 2.0 %collective-permute-start.4 = (f32[2,512]{1,0:T(2,128)S(1)}, f32[2,512]{1,0:T(2,128)S(1)}, u32[]{:S(2)}, u32[]{:S(2)}) collective-permute-start(f32[2,512]{1,0:T(2,128)S(1)} %get-tuple-element.21), channel_id=1, source_target_pairs={{0,48},{1,49},{2,50},{3,51},{4,52},{5,53},{6,54},{7,55},{8,56},{9,... | collective-permute-start | bytes 12296 | tf_op jit(solution)/shard_map/ppermute | solution.py:41
  16.7 0.8 collective-permute-done.3
  17.6 0.1 select_add_fusion.6
  17.7 4.9 %collective-permute-done.1.edge_ref = bf16[4,240,512]{2,1,0:T(8,128)(2,1)S(1)} collective-permute-done((bf16[4,240,512]{2,1,0:T(8,128)(2,1)S(1)}, bf16[4,240,512]{2,1,0:T(8,128)(2,1)S(1)}, u32[]{:S(2)}, u32[]{:S(2)}) %collective-permute-start.1) | collective-permute-done | bytes 983072 | tf_op jit(solution)/shard_map/ppermute | solution.py:41
  22.6 2.2 %collective-permute-start.6 = (f32[2,512]{1,0:T(2,128)S(1)}, f32[2,512]{1,0:T(2,128)S(1)}, u32[]{:S(2)}, u32[]{:S(2)}) collective-permute-start(f32[2,512]{1,0:T(2,128)S(1)} %select_add_fusion.6), channel_id=1, source_target_pairs={{0,8},{1,9},{2,10},{3,11},{4,12},{5,13},{6,14},{7,15},{8,0},{9,1},... | collective-permute-start | bytes 12296 | tf_op jit(solution)/shard_map/ppermute | solution.py:41
  24.8 0.9 collective-permute-start.7
  25.7 3.3 %collective-permute-start.11 = (bf16[4,240,512]{2,1,0:T(8,128)(2,1)S(1)}, bf16[4,240,512]{2,1,0:T(8,128)(2,1)S(1)}, u32[]{:S(2)}, u32[]{:S(2)}) collective-permute-start(bf16[4,240,512]{2,1,0:T(8,128)(2,1)S(1)} %collective-permute-done.1.edge_ref), channel_id=1, source_target_pairs={{0,64},{1,65},{2,66},{3,67},{4,68},{5,69},{6,70},{7,71},{8,72},{9,... | collective-permute-start | bytes 2949128 | tf_op jit(solution)/shard_map/ppermute | solution.py:41
  29.0 0.1 select_add_fusion.5
  29.1 4.2 %collective-permute-start.10 = (f32[2,512]{1,0:T(2,128)S(1)}, f32[2,512]{1,0:T(2,128)S(1)}, u32[]{:S(2)}, u32[]{:S(2)}) collective-permute-start(f32[2,512]{1,0:T(2,128)S(1)} %select_add_fusion.5), channel_id=1, source_target_pairs={{0,3},{1,0},{2,1},{3,2},{4,7},{5,4},{6,5},{7,6},{8,11},{9,8},{10,9... | collective-permute-start | bytes 12296 | tf_op jit(solution)/shard_map/ppermute | solution.py:41
  33.3 1.3 collective-permute-start.9
  34.6 0.8 stack.71.vector_ref
  35.4 1.6 %collective-permute-done.8 = f32[2,512]{1,0:T(2,128)S(1)} collective-permute-done((f32[2,512]{1,0:T(2,128)S(1)}, f32[2,512]{1,0:T(2,128)S(1)}, u32[]{:S(2)}, u32[]{:S(2)}) %collective-permute-start.8) | collective-permute-done | bytes 4128 | tf_op jit(solution)/shard_map/ppermute | solution.py:41
  37.0 0.3 collective-permute-done.9
  37.3 0.1 add_multiply_fusion.4
  37.5 1.2 copy-done.1
  38.7 17.7 %conv.1 = (bf16[480,512]{1,0:T(8,128)(2,1)S(1)}, bf16[480,512]{1,0:T(8,128)(2,1)S(1)}) custom-call(s32[6]{0:T(128)S(1)} %stack.64.flags, f32[2,512]{1,0:T(2,128)S(1)} %select_add_fusion.4.stat_ref, f32[6,512]{1,0:T(8,128)S(1)} %stack.71.vector_ref, bf16[2,2,240,512]{3,2,1,0:T(8,128)(2,1)S(1)} %copy-done.1, ...), custom_call_target="tpu_custom_call" | custom-call | flops 13589544960 | bytes 20000000 | tf_op jit(solution)/shard_map/conv/pallas_call | solution.py:443
  56.4 1.6 %stats.3 = f32[2,512]{1,0:T(2,128)S(1)} custom-call(s32[6]{0:T(128)S(1)} %stack.64.flags, bf16[2,240,512]{2,1,0:T(8,128)(2,1)S(1)} %bitcast.29, bf16[2,240,512]{2,1,0:T(8,128)(2,1)S(1)} %bitcast.28), custom_call_target="tpu_custom_call" | custom-call | tf_op jit(solution)/shard_map/stats/pallas_call | solution.py:412
  58.0 1.3 collective-permute-start.12
  59.3 2.6 %collective-permute-start.22 = (bf16[480,512]{1,0:T(8,128)(2,1)S(1)}, bf16[480,512]{1,0:T(8,128)(2,1)S(1)}, u32[]{:S(2)}, u32[]{:S(2)}) collective-permute-start(bf16[480,512]{1,0:T(8,128)(2,1)S(1)} %get-tuple-element.24), channel_id=1, source_target_pairs={{0,0},{1,1},{2,64},{3,65},{4,4},{5,5},{6,68},{7,69},{8,8},{9,9},{1... | collective-permute-start | bytes 1474568 | tf_op jit(solution)/shard_map/ppermute | solution.py:41
  61.9 0.1 select_add_fusion.3
  62.0 1.6 %collective-permute-start.13 = (f32[2,512]{1,0:T(2,128)S(1)}, f32[2,512]{1,0:T(2,128)S(1)}, u32[]{:S(2)}, u32[]{:S(2)}) collective-permute-start(f32[2,512]{1,0:T(2,128)S(1)} %select_add_fusion.3), channel_id=1, source_target_pairs={{0,16},{1,17},{2,18},{3,19},{4,20},{5,21},{6,22},{7,23},{8,24},{9,... | collective-permute-start | bytes 12296 | tf_op jit(solution)/shard_map/ppermute | solution.py:41
  63.6 1.2 collective-permute-start.14
  64.7 2.0 %collective-permute-start.15 = (f32[2,512]{1,0:T(2,128)S(1)}, f32[2,512]{1,0:T(2,128)S(1)}, u32[]{:S(2)}, u32[]{:S(2)}) collective-permute-start(f32[2,512]{1,0:T(2,128)S(1)} %select_add_fusion.3), channel_id=1, source_target_pairs={{0,48},{1,49},{2,50},{3,51},{4,52},{5,53},{6,54},{7,55},{8,56},{9,... | collective-permute-start | bytes 12296 | tf_op jit(solution)/shard_map/ppermute | solution.py:41
  66.7 2.6 %collective-permute-start.23 = (bf16[480,512]{1,0:T(8,128)(2,1)S(1)}, bf16[480,512]{1,0:T(8,128)(2,1)S(1)}, u32[]{:S(2)}, u32[]{:S(2)}) collective-permute-start(bf16[480,512]{1,0:T(8,128)(2,1)S(1)} %get-tuple-element.25), channel_id=1, source_target_pairs={{0,1},{1,0},{2,65},{3,64},{4,5},{5,4},{6,69},{7,68},{8,9},{9,8},{1... | collective-permute-start | bytes 1474568 | tf_op jit(solution)/shard_map/ppermute | solution.py:41
  69.3 0.1 add_multiply_fusion.2
  69.4 3.5 %collective-permute-done.22.own_ref = bf16[480,512]{1,0:T(8,128)(2,1)S(1)} collective-permute-done((bf16[480,512]{1,0:T(8,128)(2,1)S(1)}, bf16[480,512]{1,0:T(8,128)(2,1)S(1)}, u32[]{:S(2)}, u32[]{:S(2)}) %collective-permute-start.22) | collective-permute-done | bytes 491552 | tf_op jit(solution)/shard_map/ppermute | solution.py:41
  73.0 4.2 %collective-permute-done.23.own_ref = bf16[480,512]{1,0:T(8,128)(2,1)S(1)} collective-permute-done((bf16[480,512]{1,0:T(8,128)(2,1)S(1)}, bf16[480,512]{1,0:T(8,128)(2,1)S(1)}, u32[]{:S(2)}, u32[]{:S(2)}) %collective-permute-start.23) | collective-permute-done | bytes 491552 | tf_op jit(solution)/shard_map/ppermute | solution.py:41
  77.2 0.1 collective-permute-start.24
  77.3 0.1 select_add_fusion.2
  77.4 1.9 %collective-permute-start.16 = (f32[2,512]{1,0:T(2,128)S(1)}, f32[2,512]{1,0:T(2,128)S(1)}, u32[]{:S(2)}, u32[]{:S(2)}) collective-permute-start(f32[2,512]{1,0:T(2,128)S(1)} %select_add_fusion.2), channel_id=1, source_target_pairs={{0,4},{1,5},{2,6},{3,7},{4,8},{5,9},{6,10},{7,11},{8,12},{9,13},{1... | collective-permute-start | bytes 12296 | tf_op jit(solution)/shard_map/ppermute | solution.py:41
  79.3 1.7 %collective-permute-start.17 = (f32[2,512]{1,0:T(2,128)S(1)}, f32[2,512]{1,0:T(2,128)S(1)}, u32[]{:S(2)}, u32[]{:S(2)}) collective-permute-start(f32[2,512]{1,0:T(2,128)S(1)} %select_add_fusion.2), channel_id=1, source_target_pairs={{0,8},{1,9},{2,10},{3,11},{4,12},{5,13},{6,14},{7,15},{8,0},{9,1},... | collective-permute-start | bytes 12296 | tf_op jit(solution)/shard_map/ppermute | solution.py:41
  80.9 0.8 collective-permute-start.18
  81.8 1.5 %collective-permute-done.17 = f32[2,512]{1,0:T(2,128)S(1)} collective-permute-done((f32[2,512]{1,0:T(2,128)S(1)}, f32[2,512]{1,0:T(2,128)S(1)}, u32[]{:S(2)}, u32[]{:S(2)}) %collective-permute-start.17) | collective-permute-done | bytes 4128 | tf_op jit(solution)/shard_map/ppermute | solution.py:41
  83.2 0.2 collective-permute-done.18
  83.4 0.1 add_multiply_fusion.1
  83.5 3.2 %collective-permute-start.26 = (bf16[960,512]{1,0:T(8,128)(2,1)S(1)}, bf16[960,512]{1,0:T(8,128)(2,1)S(1)}, u32[]{:S(2)}, u32[]{:S(2)}) collective-permute-start(bf16[960,512]{1,0:T(8,128)(2,1)S(1)} %constant_dynamic-update-slice_fusion.mine_ref), channel_id=1, source_target_pairs={{0,4},{1,5},{2,6},{3,7},{4,8},{5,9},{6,10},{7,11},{8,12},{9,13},{1... | collective-permute-start | bytes 2949128 | tf_op jit(solution)/shard_map/ppermute | solution.py:41
  86.7 0.5 collective-permute-start.19
  87.3 3.3 %collective-permute-start.20 = (f32[2,512]{1,0:T(2,128)S(1)}, f32[2,512]{1,0:T(2,128)S(1)}, u32[]{:S(2)}, u32[]{:S(2)}) collective-permute-start(f32[2,512]{1,0:T(2,128)S(1)} %select_add_fusion.1), channel_id=1, source_target_pairs={{0,2},{1,3},{2,0},{3,1},{4,6},{5,7},{6,4},{7,5},{8,10},{9,11},{10,... | collective-permute-start | bytes 12296 | tf_op jit(solution)/shard_map/ppermute | solution.py:41
  90.6 0.5 collective-permute-start.21
  91.2 0.5 collective-permute-done.20
  91.7 1.7 %collective-permute-done.21 = f32[2,512]{1,0:T(2,128)S(1)} collective-permute-done((f32[2,512]{1,0:T(2,128)S(1)}, f32[2,512]{1,0:T(2,128)S(1)}, u32[]{:S(2)}, u32[]{:S(2)}) %collective-permute-start.21) | collective-permute-done | bytes 4128 | tf_op jit(solution)/shard_map/ppermute | solution.py:41
  93.4 0.1 add_multiply_fusion
  93.5 1.9 %collective-permute-start.25 = (bf16[960,512]{1,0:T(8,128)(2,1)S(1)}, bf16[960,512]{1,0:T(8,128)(2,1)S(1)}, u32[]{:S(2)}, u32[]{:S(2)}) collective-permute-start(bf16[960,512]{1,0:T(8,128)(2,1)S(1)} %collective-permute-done.24.swap_ref), channel_id=1, source_target_pairs={{0,4},{1,5},{2,6},{3,7},{4,8},{5,9},{6,10},{7,11},{8,12},{9,13},{1... | collective-permute-start | bytes 2949128 | tf_op jit(solution)/shard_map/ppermute | solution.py:41
  95.4 0.1 select_add_fusion.stat_ref
  95.5 3.1 %collective-permute-done.26.near_ref = bf16[960,512]{1,0:T(8,128)(2,1)S(1)} collective-permute-done((bf16[960,512]{1,0:T(8,128)(2,1)S(1)}, bf16[960,512]{1,0:T(8,128)(2,1)S(1)}, u32[]{:S(2)}, u32[]{:S(2)}) %collective-permute-start.26) | collective-permute-done | bytes 983072 | tf_op jit(solution)/shard_map/ppermute | solution.py:41
  98.6 8.8 %own.1 = (bf16[480,512]{1,0:T(8,128)(2,1)S(1)}, bf16[480,512]{1,0:T(8,128)(2,1)S(1)}, f32[480,512]{1,0:T(8,128)S(1)}, f32[480,512]{1,0:T(8,128)S(1)}, f32[480,128]{1,0:T(8,128)S(1)}, /*index=5*/f32[480,128]{1,0:T(8,128)S(1)}) custom-call(s32[6]{0:T(128)S(1)} %stack.64.flags, f32[2,512]{1,0:T(2,128)S(1)} %select_add_fusion.stat_ref, ...), custom_call_target="tpu_custom_call" | custom-call | flops 6000000000 | bytes 8000000 | tf_op jit(solution)/shard_map/own/pallas_call | solution.py:482
  107.4 1.8 %collective-permute-done.25.far_ref = bf16[960,512]{1,0:T(8,128)(2,1)S(1)} collective-permute-done((bf16[960,512]{1,0:T(8,128)(2,1)S(1)}, bf16[960,512]{1,0:T(8,128)(2,1)S(1)}, u32[]{:S(2)}, u32[]{:S(2)}) %collective-permute-start.25) | collective-permute-done | bytes 983072 | tf_op jit(solution)/shard_map/ppermute | solution.py:41
  109.1 5.2 %collective-permute-start.27 = (bf16[960,512]{1,0:T(8,128)(2,1)S(1)}, bf16[960,512]{1,0:T(8,128)(2,1)S(1)}, u32[]{:S(2)}, u32[]{:S(2)}) collective-permute-start(bf16[960,512]{1,0:T(8,128)(2,1)S(1)} %collective-permute-done.25.far_ref), channel_id=1, source_target_pairs={{0,64},{1,65},{2,66},{3,67},{4,68},{5,69},{6,70},{7,71},{8,72},{9,... | collective-permute-start | bytes 2949128 | tf_op jit(solution)/shard_map/ppermute | solution.py:41
  114.3 2.2 %collective-permute-done.27.relay_ref = bf16[960,512]{1,0:T(8,128)(2,1)S(1)} collective-permute-done((bf16[960,512]{1,0:T(8,128)(2,1)S(1)}, bf16[960,512]{1,0:T(8,128)(2,1)S(1)}, u32[]{:S(2)}, u32[]{:S(2)}) %collective-permute-start.27) | collective-permute-done | bytes 983072 | tf_op jit(solution)/shard_map/ppermute | solution.py:41
  116.5 4.0 %tail1.1 = bf16[480,512]{1,0:T(8,128)(2,1)S(1)} custom-call(s32[6]{0:T(128)S(1)} %stack.64.flags, f32[2,512]{1,0:T(2,128)S(1)} %select_add_fusion.stat_ref, f32[6,512]{1,0:T(8,128)S(1)} %stack.71.vector_ref, bf16[960,512]{1,0:T(8,128)(2,1)S(1)} %collective-permute-done.25.far_ref, bf16[960,512]{1,0:T(8,128)(2,1)S(1)} %collective-permute-done.27.relay_ref, ...), custom_call_target="tpu_custom_call" | custom-call | flops 3000000000 | bytes 5000000 | tf_op jit(solution)/shard_map/tail1/pallas_call | solution.py:495
  120.5 1.6 %collective-permute-start.29 = (bf16[480,512]{1,0:T(8,128)(2,1)S(1)}, bf16[480,512]{1,0:T(8,128)(2,1)S(1)}, u32[]{:S(2)}, u32[]{:S(2)}) collective-permute-start(bf16[480,512]{1,0:T(8,128)(2,1)S(1)} %tail1.1), channel_id=1, source_target_pairs={{0,1},{1,0},{2,65},{3,64},{4,5},{5,4},{6,69},{7,68},{8,9},{9,8},{1... | collective-permute-start | bytes 1474568 | tf_op jit(solution)/shard_map/ppermute | solution.py:41
  122.1 4.0 %tail0.1 = bf16[480,512]{1,0:T(8,128)(2,1)S(1)} custom-call(s32[6]{0:T(128)S(1)} %stack.64.flags, f32[2,512]{1,0:T(2,128)S(1)} %select_add_fusion.stat_ref, f32[6,512]{1,0:T(8,128)S(1)} %stack.71.vector_ref, bf16[960,512]{1,0:T(8,128)(2,1)S(1)} %collective-permute-done.25.far_ref, bf16[960,512]{1,0:T(8,128)(2,1)S(1)} %collective-permute-done.27.relay_ref, ...), custom_call_target="tpu_custom_call" | custom-call | flops 3000000000 | bytes 5000000 | tf_op jit(solution)/shard_map/tail0/pallas_call | solution.py:495
  126.1 2.7 %collective-permute-start.28 = (bf16[480,512]{1,0:T(8,128)(2,1)S(1)}, bf16[480,512]{1,0:T(8,128)(2,1)S(1)}, u32[]{:S(2)}, u32[]{:S(2)}) collective-permute-start(bf16[480,512]{1,0:T(8,128)(2,1)S(1)} %tail0.1), channel_id=1, source_target_pairs={{0,0},{1,1},{2,64},{3,65},{4,4},{5,5},{6,68},{7,69},{8,8},{9,9},{1... | collective-permute-start | bytes 1474568 | tf_op jit(solution)/shard_map/ppermute | solution.py:41
  128.8 1.3 collective-permute-done.29.back1_ref
  130.0 7.7 %collective-permute-done.28.back0_ref = bf16[480,512]{1,0:T(8,128)(2,1)S(1)} collective-permute-done((bf16[480,512]{1,0:T(8,128)(2,1)S(1)}, bf16[480,512]{1,0:T(8,128)(2,1)S(1)}, u32[]{:S(2)}, u32[]{:S(2)}) %collective-permute-start.28) | collective-permute-done | bytes 491552 | tf_op jit(solution)/shard_map/ppermute | solution.py:41
  137.7 1.6 %place.1 = bf16[2,480,512]{2,1,0:T(8,128)(2,1)} custom-call(s32[6]{0:T(128)S(1)} %stack.64.flags, bf16[480,512]{1,0:T(8,128)(2,1)S(1)} %collective-permute-done.28.back0_ref, bf16[480,512]{1,0:T(8,128)(2,1)S(1)} %collective-permute-done.29.back1_ref), custom_call_target="tpu_custom_call" | custom-call | tf_op jit(solution)/shard_map/place/pallas_call | solution.py:521
  (42 shorter events, 0.4 us)
Async XLA Ops:
  0.0 3.6 %collective-permute-start = (bf16[2,2,240,512]{3,2,1,0:T(8,128)(2,1)}, bf16[2,2,240,512]{3,2,1,0:T(8,128)(2,1)S(1)}, u32[]{:S(2)}, u32[]{:S(2)}) collective-permute-start(bf16[2,2,240,512]{3,2,1,0:T(8,128)(2,1)} %own_ref.1), channel_id=1, source_target_pairs={{0,64},{1,65},{2,66},{3,67},{4,68},{5,69},{6,70},{7,71},{8,72},{9,... | collective-permute-start | bytes 2949128 | tf_op jit(solution)/shard_map/ppermute | solution.py:41
  0.8 1.2 copy-start
  5.2 17.4 %collective-permute-start.1 = (bf16[4,240,512]{2,1,0:T(8,128)(2,1)S(1)}, bf16[4,240,512]{2,1,0:T(8,128)(2,1)S(1)}, u32[]{:S(2)}, u32[]{:S(2)}) collective-permute-start(bf16[4,240,512]{2,1,0:T(8,128)(2,1)S(1)} %get-tuple-element.20), channel_id=1, source_target_pairs={{0,1},{1,2},{2,3},{3,4},{4,5},{5,6},{6,7},{7,8},{8,9},{9,10},{10,1... | collective-permute-start | bytes 2949128 | tf_op jit(solution)/shard_map/ppermute | solution.py:41
  11.6 5.1 %collective-permute-start.2 = (f32[2,512]{1,0:T(2,128)S(1)}, f32[2,512]{1,0:T(2,128)S(1)}, u32[]{:S(2)}, u32[]{:S(2)}) collective-permute-start(f32[2,512]{1,0:T(2,128)S(1)} %get-tuple-element.21), channel_id=1, source_target_pairs={{0,16},{1,17},{2,18},{3,19},{4,20},{5,21},{6,22},{7,23},{8,24},{9,... | collective-permute-start | bytes 12296 | tf_op jit(solution)/shard_map/ppermute | solution.py:41
  13.3 4.3 %collective-permute-start.3 = (f32[2,512]{1,0:T(2,128)S(1)}, f32[2,512]{1,0:T(2,128)S(1)}, u32[]{:S(2)}, u32[]{:S(2)}) collective-permute-start(f32[2,512]{1,0:T(2,128)S(1)} %get-tuple-element.21), channel_id=1, source_target_pairs={{0,32},{1,33},{2,34},{3,35},{4,36},{5,37},{6,38},{7,39},{8,40},{9,... | collective-permute-start | bytes 12296 | tf_op jit(solution)/shard_map/ppermute | solution.py:41
  14.7 2.8 %collective-permute-start.4 = (f32[2,512]{1,0:T(2,128)S(1)}, f32[2,512]{1,0:T(2,128)S(1)}, u32[]{:S(2)}, u32[]{:S(2)}) collective-permute-start(f32[2,512]{1,0:T(2,128)S(1)} %get-tuple-element.21), channel_id=1, source_target_pairs={{0,48},{1,49},{2,50},{3,51},{4,52},{5,53},{6,54},{7,55},{8,56},{9,... | collective-permute-start | bytes 12296 | tf_op jit(solution)/shard_map/ppermute | solution.py:41
  22.6 6.4 %collective-permute-start.5 = (f32[2,512]{1,0:T(2,128)S(1)}, f32[2,512]{1,0:T(2,128)S(1)}, u32[]{:S(2)}, u32[]{:S(2)}) collective-permute-start(f32[2,512]{1,0:T(2,128)S(1)} %select_add_fusion.6), channel_id=1, source_target_pairs={{0,4},{1,5},{2,6},{3,7},{4,8},{5,9},{6,10},{7,11},{8,12},{9,13},{1... | collective-permute-start | bytes 12296 | tf_op jit(solution)/shard_map/ppermute | solution.py:41
  22.6 6.4 %collective-permute-start.6 = (f32[2,512]{1,0:T(2,128)S(1)}, f32[2,512]{1,0:T(2,128)S(1)}, u32[]{:S(2)}, u32[]{:S(2)}) collective-permute-start(f32[2,512]{1,0:T(2,128)S(1)} %select_add_fusion.6), channel_id=1, source_target_pairs={{0,8},{1,9},{2,10},{3,11},{4,12},{5,13},{6,14},{7,15},{8,0},{9,1},... | collective-permute-start | bytes 12296 | tf_op jit(solution)/shard_map/ppermute | solution.py:41
  24.8 4.2 %collective-permute-start.7 = (f32[2,512]{1,0:T(2,128)S(1)}, f32[2,512]{1,0:T(2,128)S(1)}, u32[]{:S(2)}, u32[]{:S(2)}) collective-permute-start(f32[2,512]{1,0:T(2,128)S(1)} %select_add_fusion.6), channel_id=1, source_target_pairs={{0,12},{1,13},{2,14},{3,15},{4,0},{5,1},{6,2},{7,3},{8,4},{9,5},{1... | collective-permute-start | bytes 12296 | tf_op jit(solution)/shard_map/ppermute | solution.py:41
  25.7 11.8 %collective-permute-start.11 = (bf16[4,240,512]{2,1,0:T(8,128)(2,1)S(1)}, bf16[4,240,512]{2,1,0:T(8,128)(2,1)S(1)}, u32[]{:S(2)}, u32[]{:S(2)}) collective-permute-start(bf16[4,240,512]{2,1,0:T(8,128)(2,1)S(1)} %collective-permute-done.1.edge_ref), channel_id=1, source_target_pairs={{0,64},{1,65},{2,66},{3,67},{4,68},{5,69},{6,70},{7,71},{8,72},{9,... | collective-permute-start | bytes 2949128 | tf_op jit(solution)/shard_map/ppermute | solution.py:41
  29.1 6.3 %collective-permute-start.10 = (f32[2,512]{1,0:T(2,128)S(1)}, f32[2,512]{1,0:T(2,128)S(1)}, u32[]{:S(2)}, u32[]{:S(2)}) collective-permute-start(f32[2,512]{1,0:T(2,128)S(1)} %select_add_fusion.5), channel_id=1, source_target_pairs={{0,3},{1,0},{2,1},{3,2},{4,7},{5,4},{6,5},{7,6},{8,11},{9,8},{10,9... | collective-permute-start | bytes 12296 | tf_op jit(solution)/shard_map/ppermute | solution.py:41
  33.3 3.7 %collective-permute-start.8 = (f32[2,512]{1,0:T(2,128)S(1)}, f32[2,512]{1,0:T(2,128)S(1)}, u32[]{:S(2)}, u32[]{:S(2)}) collective-permute-start(f32[2,512]{1,0:T(2,128)S(1)} %select_add_fusion.5), channel_id=1, source_target_pairs={{0,1},{1,2},{2,3},{3,0},{4,5},{5,6},{6,7},{7,4},{8,9},{9,10},{10,1... | collective-permute-start | bytes 12296 | tf_op jit(solution)/shard_map/ppermute | solution.py:41
  33.3 4.0 %collective-permute-start.9 = (f32[2,512]{1,0:T(2,128)S(1)}, f32[2,512]{1,0:T(2,128)S(1)}, u32[]{:S(2)}, u32[]{:S(2)}) collective-permute-start(f32[2,512]{1,0:T(2,128)S(1)} %select_add_fusion.5), channel_id=1, source_target_pairs={{0,2},{1,3},{2,0},{3,1},{4,6},{5,7},{6,4},{7,5},{8,10},{9,11},{10,... | collective-permute-start | bytes 12296 | tf_op jit(solution)/shard_map/ppermute | solution.py:41
  37.5 1.2 copy-start.1
  38.7 59.9 %copy-start.2 = (bf16[512,512]{1,0:T(8,128)(2,1)S(1)}, bf16[512,512]{1,0:T(8,128)(2,1)}, u32[]{:S(2)}) copy-start(bf16[512,512]{1,0:T(8,128)(2,1)} %wq_ref.1) | copy-start | bytes 1572868
  38.7 59.9 %copy-start.3 = (bf16[512,512]{1,0:T(8,128)(2,1)S(1)}, bf16[512,512]{1,0:T(8,128)(2,1)}, u32[]{:S(2)}) copy-start(bf16[512,512]{1,0:T(8,128)(2,1)} %wk_ref.1) | copy-start | bytes 1572868
  56.4 60.1 %copy-start.4 = (bf16[512,512]{1,0:T(8,128)(2,1)S(1)}, bf16[512,512]{1,0:T(8,128)(2,1)}, u32[]{:S(2)}) copy-start(bf16[512,512]{1,0:T(8,128)(2,1)} %wv_ref.3) | copy-start | bytes 1572868
  56.4 60.1 %copy-start.5 = (bf16[512,512]{1,0:T(8,128)(2,1)S(1)}, bf16[512,512]{1,0:T(8,128)(2,1)}, u32[]{:S(2)}) copy-start(bf16[512,512]{1,0:T(8,128)(2,1)} %wo_ref.3) | copy-start | bytes 1572868
  58.0 3.9 %collective-permute-start.12 = (f32[2,512]{1,0:T(2,128)S(1)}, f32[2,512]{1,0:T(2,128)S(1)}, u32[]{:S(2)}, u32[]{:S(2)}) collective-permute-start(f32[2,512]{1,0:T(2,128)S(1)} %stats.3), channel_id=1, source_target_pairs={{0,64},{1,65},{2,66},{3,67},{4,68},{5,69},{6,70},{7,71},{8,72},{9,... | collective-permute-start | bytes 12296 | tf_op jit(solution)/shard_map/ppermute | solution.py:41
  59.3 13.7 %collective-permute-start.22 = (bf16[480,512]{1,0:T(8,128)(2,1)S(1)}, bf16[480,512]{1,0:T(8,128)(2,1)S(1)}, u32[]{:S(2)}, u32[]{:S(2)}) collective-permute-start(bf16[480,512]{1,0:T(8,128)(2,1)S(1)} %get-tuple-element.24), channel_id=1, source_target_pairs={{0,0},{1,1},{2,64},{3,65},{4,4},{5,5},{6,68},{7,69},{8,8},{9,9},{1... | collective-permute-start | bytes 1474568 | tf_op jit(solution)/shard_map/ppermute | solution.py:41
  62.0 7.3 %collective-permute-start.13 = (f32[2,512]{1,0:T(2,128)S(1)}, f32[2,512]{1,0:T(2,128)S(1)}, u32[]{:S(2)}, u32[]{:S(2)}) collective-permute-start(f32[2,512]{1,0:T(2,128)S(1)} %select_add_fusion.3), channel_id=1, source_target_pairs={{0,16},{1,17},{2,18},{3,19},{4,20},{5,21},{6,22},{7,23},{8,24},{9,... | collective-permute-start | bytes 12296 | tf_op jit(solution)/shard_map/ppermute | solution.py:41
  63.6 5.7 %collective-permute-start.14 = (f32[2,512]{1,0:T(2,128)S(1)}, f32[2,512]{1,0:T(2,128)S(1)}, u32[]{:S(2)}, u32[]{:S(2)}) collective-permute-start(f32[2,512]{1,0:T(2,128)S(1)} %select_add_fusion.3), channel_id=1, source_target_pairs={{0,32},{1,33},{2,34},{3,35},{4,36},{5,37},{6,38},{7,39},{8,40},{9,... | collective-permute-start | bytes 12296 | tf_op jit(solution)/shard_map/ppermute | solution.py:41
  64.7 4.6 %collective-permute-start.15 = (f32[2,512]{1,0:T(2,128)S(1)}, f32[2,512]{1,0:T(2,128)S(1)}, u32[]{:S(2)}, u32[]{:S(2)}) collective-permute-start(f32[2,512]{1,0:T(2,128)S(1)} %select_add_fusion.3), channel_id=1, source_target_pairs={{0,48},{1,49},{2,50},{3,51},{4,52},{5,53},{6,54},{7,55},{8,56},{9,... | collective-permute-start | bytes 12296 | tf_op jit(solution)/shard_map/ppermute | solution.py:41
  66.7 10.5 %collective-permute-start.23 = (bf16[480,512]{1,0:T(8,128)(2,1)S(1)}, bf16[480,512]{1,0:T(8,128)(2,1)S(1)}, u32[]{:S(2)}, u32[]{:S(2)}) collective-permute-start(bf16[480,512]{1,0:T(8,128)(2,1)S(1)} %get-tuple-element.25), channel_id=1, source_target_pairs={{0,1},{1,0},{2,65},{3,64},{4,5},{5,4},{6,69},{7,68},{8,9},{9,8},{1... | collective-permute-start | bytes 1474568 | tf_op jit(solution)/shard_map/ppermute | solution.py:41
  77.2 16.2 %collective-permute-start.24 = (bf16[960,512]{1,0:T(8,128)(2,1)S(1)}, bf16[960,512]{1,0:T(8,128)(2,1)S(1)}, u32[]{:S(2)}, u32[]{:S(2)}) collective-permute-start(bf16[960,512]{1,0:T(8,128)(2,1)S(1)} %constant_dynamic-update-slice_fusion.mine_ref), channel_id=1, source_target_pairs={{0,64},{1,65},{2,66},{3,67},{4,68},{5,69},{6,70},{7,71},{8,72},{9,... | collective-permute-start | bytes 2949128 | tf_op jit(solution)/shard_map/ppermute | solution.py:41
  77.4 4.4 %collective-permute-start.16 = (f32[2,512]{1,0:T(2,128)S(1)}, f32[2,512]{1,0:T(2,128)S(1)}, u32[]{:S(2)}, u32[]{:S(2)}) collective-permute-start(f32[2,512]{1,0:T(2,128)S(1)} %select_add_fusion.2), channel_id=1, source_target_pairs={{0,4},{1,5},{2,6},{3,7},{4,8},{5,9},{6,10},{7,11},{8,12},{9,13},{1... | collective-permute-start | bytes 12296 | tf_op jit(solution)/shard_map/ppermute | solution.py:41
  79.3 4.0 %collective-permute-start.17 = (f32[2,512]{1,0:T(2,128)S(1)}, f32[2,512]{1,0:T(2,128)S(1)}, u32[]{:S(2)}, u32[]{:S(2)}) collective-permute-start(f32[2,512]{1,0:T(2,128)S(1)} %select_add_fusion.2), channel_id=1, source_target_pairs={{0,8},{1,9},{2,10},{3,11},{4,12},{5,13},{6,14},{7,15},{8,0},{9,1},... | collective-permute-start | bytes 12296 | tf_op jit(solution)/shard_map/ppermute | solution.py:41
  80.9 2.5 %collective-permute-start.18 = (f32[2,512]{1,0:T(2,128)S(1)}, f32[2,512]{1,0:T(2,128)S(1)}, u32[]{:S(2)}, u32[]{:S(2)}) collective-permute-start(f32[2,512]{1,0:T(2,128)S(1)} %select_add_fusion.2), channel_id=1, source_target_pairs={{0,12},{1,13},{2,14},{3,15},{4,0},{5,1},{6,2},{7,3},{8,4},{9,5},{1... | collective-permute-start | bytes 12296 | tf_op jit(solution)/shard_map/ppermute | solution.py:41
  83.5 15.1 %collective-permute-start.26 = (bf16[960,512]{1,0:T(8,128)(2,1)S(1)}, bf16[960,512]{1,0:T(8,128)(2,1)S(1)}, u32[]{:S(2)}, u32[]{:S(2)}) collective-permute-start(bf16[960,512]{1,0:T(8,128)(2,1)S(1)} %constant_dynamic-update-slice_fusion.mine_ref), channel_id=1, source_target_pairs={{0,4},{1,5},{2,6},{3,7},{4,8},{5,9},{6,10},{7,11},{8,12},{9,13},{1... | collective-permute-start | bytes 2949128 | tf_op jit(solution)/shard_map/ppermute | solution.py:41
  86.7 4.4 %collective-permute-start.19 = (f32[2,512]{1,0:T(2,128)S(1)}, f32[2,512]{1,0:T(2,128)S(1)}, u32[]{:S(2)}, u32[]{:S(2)}) collective-permute-start(f32[2,512]{1,0:T(2,128)S(1)} %select_add_fusion.1), channel_id=1, source_target_pairs={{0,1},{1,2},{2,3},{3,0},{4,5},{5,6},{6,7},{7,4},{8,9},{9,10},{10,1... | collective-permute-start | bytes 12296 | tf_op jit(solution)/shard_map/ppermute | solution.py:41
  87.3 4.4 %collective-permute-start.20 = (f32[2,512]{1,0:T(2,128)S(1)}, f32[2,512]{1,0:T(2,128)S(1)}, u32[]{:S(2)}, u32[]{:S(2)}) collective-permute-start(f32[2,512]{1,0:T(2,128)S(1)} %select_add_fusion.1), channel_id=1, source_target_pairs={{0,2},{1,3},{2,0},{3,1},{4,6},{5,7},{6,4},{7,5},{8,10},{9,11},{10,... | collective-permute-start | bytes 12296 | tf_op jit(solution)/shard_map/ppermute | solution.py:41
  90.6 2.8 %collective-permute-start.21 = (f32[2,512]{1,0:T(2,128)S(1)}, f32[2,512]{1,0:T(2,128)S(1)}, u32[]{:S(2)}, u32[]{:S(2)}) collective-permute-start(f32[2,512]{1,0:T(2,128)S(1)} %select_add_fusion.1), channel_id=1, source_target_pairs={{0,3},{1,0},{2,1},{3,2},{4,7},{5,4},{6,5},{7,6},{8,11},{9,8},{10,9... | collective-permute-start | bytes 12296 | tf_op jit(solution)/shard_map/ppermute | solution.py:41
  93.5 15.7 %collective-permute-start.25 = (bf16[960,512]{1,0:T(8,128)(2,1)S(1)}, bf16[960,512]{1,0:T(8,128)(2,1)S(1)}, u32[]{:S(2)}, u32[]{:S(2)}) collective-permute-start(bf16[960,512]{1,0:T(8,128)(2,1)S(1)} %collective-permute-done.24.swap_ref), channel_id=1, source_target_pairs={{0,4},{1,5},{2,6},{3,7},{4,8},{5,9},{6,10},{7,11},{8,12},{9,13},{1... | collective-permute-start | bytes 2949128 | tf_op jit(solution)/shard_map/ppermute | solution.py:41
  109.1 7.4 %collective-permute-start.27 = (bf16[960,512]{1,0:T(8,128)(2,1)S(1)}, bf16[960,512]{1,0:T(8,128)(2,1)S(1)}, u32[]{:S(2)}, u32[]{:S(2)}) collective-permute-start(bf16[960,512]{1,0:T(8,128)(2,1)S(1)} %collective-permute-done.25.far_ref), channel_id=1, source_target_pairs={{0,64},{1,65},{2,66},{3,67},{4,68},{5,69},{6,70},{7,71},{8,72},{9,... | collective-permute-start | bytes 2949128 | tf_op jit(solution)/shard_map/ppermute | solution.py:41
  120.5 9.5 %collective-permute-start.29 = (bf16[480,512]{1,0:T(8,128)(2,1)S(1)}, bf16[480,512]{1,0:T(8,128)(2,1)S(1)}, u32[]{:S(2)}, u32[]{:S(2)}) collective-permute-start(bf16[480,512]{1,0:T(8,128)(2,1)S(1)} %tail1.1), channel_id=1, source_target_pairs={{0,1},{1,0},{2,65},{3,64},{4,5},{5,4},{6,69},{7,68},{8,9},{9,8},{1... | collective-permute-start | bytes 1474568 | tf_op jit(solution)/shard_map/ppermute | solution.py:41
  126.1 11.7 %collective-permute-start.28 = (bf16[480,512]{1,0:T(8,128)(2,1)S(1)}, bf16[480,512]{1,0:T(8,128)(2,1)S(1)}, u32[]{:S(2)}, u32[]{:S(2)}) collective-permute-start(bf16[480,512]{1,0:T(8,128)(2,1)S(1)} %tail0.1), channel_id=1, source_target_pairs={{0,0},{1,1},{2,64},{3,65},{4,4},{5,5},{6,68},{7,69},{8,8},{9,9},{1... | collective-permute-start | bytes 1474568 | tf_op jit(solution)/shard_map/ppermute | solution.py:41

commit v4 on v3

--- a/solution.py
+++ b/solution.py
@@ -146,6 +146,12 @@
         [functools.partial(lambda ref, i: ref[i], ref, i) for ref in refs[:-1] for i in range(ref.shape[0])],
         refs[-1],
     )
+
+
+def first_kernel(flags, feat_ref, few_ref, stat_ref, kept_ref, vector_ref):
+    kept_ref[...] = feat_ref[...]
+    vector_ref[...] = few_ref[...]
+    stat_kernel(flags, feat_ref, stat_ref)
 
 
 def edge_kernel(flags, feat_ref, other_ref, first_ref, stat_ref, edge_ref):
@@ -419,24 +425,28 @@
         )(flags, *[a.reshape(-1, width, chans) for a in pieces])
 
     other = send(feat, swap)
+    row_shape = jax.ShapeDtypeStruct((2 * frames, width, chans), BF)
+    first, kept, vectors = pl.pallas_call(
+        first_kernel,
+        out_shape=(stat_shape, row_shape, jax.ShapeDtypeStruct(vectors.shape, F32)),
+        in_specs=[flag_spec(), whole(), whole()],
+        out_specs=(whole(),) * 3,
+        compiler_params=params(16),
+        name="first",
+    )(flags, feat.reshape(-1, width, chans), vectors)
     stats, edge = pl.pallas_call(
         edge_kernel,
-        out_shape=(stat_shape, jax.ShapeDtypeStruct((2 * frames, width, chans), BF)),
+        out_shape=(stat_shape, row_shape),
         in_specs=[flag_spec(), whole(), whole(), whole()],
         out_specs=(whole(), whole()),
         compiler_params=params(16),
         name="edges",
-    )(
-        flags,
-        feat.reshape(-1, width, chans),
-        other.reshape(-1, width, chans),
-        stats_of(feat),
-    )
+    )(flags, kept, other.reshape(-1, width, chans), first)
     edge = send(edge, edges_out)
-    stats = over(stats, "z")
+    stats = over(over(stats, "z"), "x")
     edge, stats = lax.optimization_barrier((edge, stats))
     cross = send(edge, swap)
-    stats = over(over(stats, "x"), "y")
+    stats = over(stats, "y")
 
     cells = rows * width
     piece = jax.ShapeDtypeStruct((cells, chans), BF)
@@ -458,7 +468,7 @@
         flags,
         stats,
         vectors,
-        feat,
+        kept.reshape(feat.shape),
         other,
         edge,
         cross,
@@ -472,8 +482,8 @@
     mine = jnp.concatenate([mine0, mine1])
     swapped = send(mine, swap)
     near = send(after(mine, stats2), blocks_out)
-    stats2 = over(stats2, "x")
-    far = send(after(swapped, stats2), blocks_out)
+    swapped, stats2 = lax.optimization_barrier((swapped, over(stats2, "x")))
+    far = send(swapped, blocks_out)
     stats2 = over(stats2, "y")
 
     norm2 = (stats2, vectors)

time: 140 us -> 139 us (level)
  waiting for transfers between devices: 35.3 us -> 42.9 us
  starting transfers between devices: 58.6 us -> 51.4 us
    ppermute x30, waiting for transfers between devices: 35.3 us -> 42.9 us  [send(): return lax.ppermute(value, AXES, pairs_of(move))]
    ppermute x30, starting transfers between devices: 58.6 us -> 51.4 us  [send(): return lax.ppermute(value, AXES, pairs_of(move))]
    pallas_call x1 -> x2, Pallas kernels: 1.62 us -> 3.22 us  [the longest x1 1.62 us: shards(): pl.pallas_call(edge_kernel, out_shape=(stat_shape, row_shape), in_specs=[...]
    pallas_call x2 -> x1, Pallas kernels: 3.2 us -> 1.6 us  [stats_of(): pl.pallas_call(stat_kernel, out_shape=stat_shape, in_specs=[flag_spec()]...]
  transfers between devices with their start and end apart: 30 -> 30, of which waited for: 15 -> 19; matrix products, arithmetic and copies ran while one was open for 1% -> 1% of each run, Pallas kernels for 10% -> 10%
where the time goes in v4:
time: 139 us
  starting transfers between devices  51.4 us (37%)
  waiting for transfers between devices  42.9 us (31%)
  Pallas kernels  40.9 us (29%)
  local copies, waits for them, and re-layouts  2.15 us (2%)
    ppermute x30, starting transfers between devices, send(): return lax.ppermute(value, AXES, pairs_of(move))  51.4 us
    ppermute x30, waiting for transfers between devices, send(): return lax.ppermute(value, AXES, pairs_of(move))  42.9 us
    pallas_call x1, Pallas kernels, shards(): pl.pallas_call(conv_kernel, out_shape=(piece, piece), in_specs=[flag_spec...  17.7 us
    pallas_call x1, Pallas kernels, shards(): pl.pallas_call(own_kernel, out_shape=(piece, piece, acc_shape, acc_shape,...  8.76 us
    pallas_call x2, Pallas kernels, tail(): pl.pallas_call(functools.partial(tail_kernel, order), out_shape=piece, in...  8.04 us
  transfers between devices with their start and end apart: 30, of which 19 were waited for; matrix products, arithmetic and copies ran while one was open for 1% of the time, Pallas kernels for 10%

profile of v4, /device:TPU:33, one launch (start us, length us, event | category | flops | bytes accessed | tf_op | source)
XLA Modules:
  0.0 138.5 jit_solution(16006396735163563054)
XLA Ops:
  0.0 0.7 collective-permute-start
  0.7 0.1 stack.64.flags
  0.8 0.8 stack.71.few_ref
  1.6 1.2 copy-done
  2.8 1.6 %first.1 = (f32[2,512]{1,0:T(2,128)S(1)}, bf16[4,240,512]{2,1,0:T(8,128)(2,1)S(1)}, f32[6,512]{1,0:T(8,128)S(1)}) custom-call(s32[6]{0:T(128)S(1)} %stack.64.flags, bf16[4,240,512]{2,1,0:T(8,128)(2,1)S(1)} %bitcast.26, f32[6,512]{1,0:T(8,128)S(1)} %stack.71.few_ref), custom_call_target="tpu_custom_call" | custom-call | tf_op jit(solution)/shard_map/first/pallas_call | solution.py:429
  4.4 1.6 %edges.1 = (f32[2,512]{1,0:T(2,128)S(1)}, bf16[4,240,512]{2,1,0:T(8,128)(2,1)S(1)}) custom-call(s32[6]{0:T(128)S(1)} %stack.64.flags, bf16[4,240,512]{2,1,0:T(8,128)(2,1)S(1)} %get-tuple-element.24.feat_ref, bf16[4,240,512]{2,1,0:T(8,128)(2,1)S(1)} %bitcast.27, f32[2,512]{1,0:T(2,128)S(1)} %get-tuple-element.25.first_ref), custom_call_target="tpu_custom_call" | custom-call | tf_op jit(solution)/shard_map/edges/pallas_call | solution.py:437
  6.0 1.7 %collective-permute-start.2 = (f32[2,512]{1,0:T(2,128)S(1)}, f32[2,512]{1,0:T(2,128)S(1)}, u32[]{:S(2)}, u32[]{:S(2)}) collective-permute-start(f32[2,512]{1,0:T(2,128)S(1)} %get-tuple-element.27), channel_id=1, source_target_pairs={{0,16},{1,17},{2,18},{3,19},{4,20},{5,21},{6,22},{7,23},{8,24},{9,... | collective-permute-start | bytes 12296 | tf_op jit(solution)/shard_map/ppermute | solution.py:41
  7.7 1.2 collective-permute-start.3
  8.9 2.0 %collective-permute-start.4 = (f32[2,512]{1,0:T(2,128)S(1)}, f32[2,512]{1,0:T(2,128)S(1)}, u32[]{:S(2)}, u32[]{:S(2)}) collective-permute-start(f32[2,512]{1,0:T(2,128)S(1)} %get-tuple-element.27), channel_id=1, source_target_pairs={{0,48},{1,49},{2,50},{3,51},{4,52},{5,53},{6,54},{7,55},{8,56},{9,... | collective-permute-start | bytes 12296 | tf_op jit(solution)/shard_map/ppermute | solution.py:41
  10.8 7.3 %collective-permute-start.1 = (bf16[4,240,512]{2,1,0:T(8,128)(2,1)S(1)}, bf16[4,240,512]{2,1,0:T(8,128)(2,1)S(1)}, u32[]{:S(2)}, u32[]{:S(2)}) collective-permute-start(bf16[4,240,512]{2,1,0:T(8,128)(2,1)S(1)} %get-tuple-element.26), channel_id=1, source_target_pairs={{0,1},{1,2},{2,3},{3,4},{4,5},{5,6},{6,7},{7,8},{8,9},{9,10},{10,1... | collective-permute-start | bytes 2949128 | tf_op jit(solution)/shard_map/ppermute | solution.py:41
  18.2 0.1 select_add_fusion.6
  18.3 1.3 collective-permute-start.6
  19.6 1.4 %collective-permute-start.7 = (f32[2,512]{1,0:T(2,128)S(1)}, f32[2,512]{1,0:T(2,128)S(1)}, u32[]{:S(2)}, u32[]{:S(2)}) collective-permute-start(f32[2,512]{1,0:T(2,128)S(1)} %select_add_fusion.6), channel_id=1, source_target_pairs={{0,12},{1,13},{2,14},{3,15},{4,0},{5,1},{6,2},{7,3},{8,4},{9,5},{1... | collective-permute-start | bytes 12296 | tf_op jit(solution)/shard_map/ppermute | solution.py:41
  20.9 1.3 collective-permute-done.5
  22.2 0.4 collective-permute-done.6
  22.6 6.7 %collective-permute-done.7 = f32[2,512]{1,0:T(2,128)S(1)} collective-permute-done((f32[2,512]{1,0:T(2,128)S(1)}, f32[2,512]{1,0:T(2,128)S(1)}, u32[]{:S(2)}, u32[]{:S(2)}) %collective-permute-start.7) | collective-permute-done | bytes 4128 | tf_op jit(solution)/shard_map/ppermute | solution.py:41
  29.3 0.1 add_multiply_fusion.5
  29.4 0.1 select_add_fusion.5
  29.5 2.4 %collective-permute-start.11 = (bf16[4,240,512]{2,1,0:T(8,128)(2,1)S(1)}, bf16[4,240,512]{2,1,0:T(8,128)(2,1)S(1)}, u32[]{:S(2)}, u32[]{:S(2)}) collective-permute-start(bf16[4,240,512]{2,1,0:T(8,128)(2,1)S(1)} %collective-permute-done.1.edge_ref), channel_id=1, source_target_pairs={{0,64},{1,65},{2,66},{3,67},{4,68},{5,69},{6,70},{7,71},{8,72},{9,... | collective-permute-start | bytes 2949128 | tf_op jit(solution)/shard_map/ppermute | solution.py:41
  31.9 0.7 collective-permute-start.10
  32.6 0.8 collective-permute-start.8
  33.4 0.4 collective-permute-start.9
  33.8 0.6 collective-permute-done.10
  34.4 1.9 %collective-permute-done.8 = f32[2,512]{1,0:T(2,128)S(1)} collective-permute-done((f32[2,512]{1,0:T(2,128)S(1)}, f32[2,512]{1,0:T(2,128)S(1)}, u32[]{:S(2)}, u32[]{:S(2)}) %collective-permute-start.8) | collective-permute-done | bytes 4128 | tf_op jit(solution)/shard_map/ppermute | solution.py:41
  36.3 1.1 collective-permute-done.9
  37.4 0.1 select_add_fusion.4.stat_ref
  37.5 17.7 %conv.1 = (bf16[480,512]{1,0:T(8,128)(2,1)S(1)}, bf16[480,512]{1,0:T(8,128)(2,1)S(1)}) custom-call(s32[6]{0:T(128)S(1)} %stack.64.flags, f32[2,512]{1,0:T(2,128)S(1)} %select_add_fusion.4.stat_ref, f32[6,512]{1,0:T(8,128)S(1)} %get-tuple-element.29.vector_ref, bf16[2,2,240,512]{3,2,1,0:T(8,128)(2,1)S(1)} %bitcast.28, ...), custom_call_target="tpu_custom_call" | custom-call | flops 13589544960 | bytes 20000000 | tf_op jit(solution)/shard_map/conv/pallas_call | solution.py:453
  55.2 1.6 %stats.1 = f32[2,512]{1,0:T(2,128)S(1)} custom-call(s32[6]{0:T(128)S(1)} %stack.64.flags, bf16[2,240,512]{2,1,0:T(8,128)(2,1)S(1)} %bitcast.30, bf16[2,240,512]{2,1,0:T(8,128)(2,1)S(1)} %bitcast.29), custom_call_target="tpu_custom_call" | custom-call | tf_op jit(solution)/shard_map/stats/pallas_call | solution.py:418
  56.8 1.8 %collective-permute-start.15 = (f32[2,512]{1,0:T(2,128)S(1)}, f32[2,512]{1,0:T(2,128)S(1)}, u32[]{:S(2)}, u32[]{:S(2)}) collective-permute-start(f32[2,512]{1,0:T(2,128)S(1)} %stats.1), channel_id=1, source_target_pairs={{0,64},{1,65},{2,66},{3,67},{4,68},{5,69},{6,70},{7,71},{8,72},{9,... | collective-permute-start | bytes 12296 | tf_op jit(solution)/shard_map/ppermute | solution.py:41
  58.6 2.1 %collective-permute-start.12 = (bf16[480,512]{1,0:T(8,128)(2,1)S(1)}, bf16[480,512]{1,0:T(8,128)(2,1)S(1)}, u32[]{:S(2)}, u32[]{:S(2)}) collective-permute-start(bf16[480,512]{1,0:T(8,128)(2,1)S(1)} %get-tuple-element.31), channel_id=1, source_target_pairs={{0,0},{1,1},{2,64},{3,65},{4,4},{5,5},{6,68},{7,69},{8,8},{9,9},{1... | collective-permute-start | bytes 1474568 | tf_op jit(solution)/shard_map/ppermute | solution.py:41
  60.7 2.3 %collective-permute-start.13 = (bf16[480,512]{1,0:T(8,128)(2,1)S(1)}, bf16[480,512]{1,0:T(8,128)(2,1)S(1)}, u32[]{:S(2)}, u32[]{:S(2)}) collective-permute-start(bf16[480,512]{1,0:T(8,128)(2,1)S(1)} %get-tuple-element.32), channel_id=1, source_target_pairs={{0,1},{1,0},{2,65},{3,64},{4,5},{5,4},{6,69},{7,68},{8,9},{9,8},{1... | collective-permute-start | bytes 1474568 | tf_op jit(solution)/shard_map/ppermute | solution.py:41
  63.1 0.2 collective-permute-start.16
  63.3 1.9 %collective-permute-start.17 = (f32[2,512]{1,0:T(2,128)S(1)}, f32[2,512]{1,0:T(2,128)S(1)}, u32[]{:S(2)}, u32[]{:S(2)}) collective-permute-start(f32[2,512]{1,0:T(2,128)S(1)} %select_add_fusion.3), channel_id=1, source_target_pairs={{0,32},{1,33},{2,34},{3,35},{4,36},{5,37},{6,38},{7,39},{8,40},{9,... | collective-permute-start | bytes 12296 | tf_op jit(solution)/shard_map/ppermute | solution.py:41
  65.2 0.7 collective-permute-done.16
  65.9 1.4 collective-permute-done.17
  67.2 0.7 collective-permute-done.18
  67.9 0.1 add_multiply_fusion.2
  68.0 6.1 %collective-permute-done.12.own_ref = bf16[480,512]{1,0:T(8,128)(2,1)S(1)} collective-permute-done((bf16[480,512]{1,0:T(8,128)(2,1)S(1)}, bf16[480,512]{1,0:T(8,128)(2,1)S(1)}, u32[]{:S(2)}, u32[]{:S(2)}) %collective-permute-start.12) | collective-permute-done | bytes 491552 | tf_op jit(solution)/shard_map/ppermute | solution.py:41
  74.1 1.4 collective-permute-done.13.own_ref
  75.5 0.1 collective-permute-start.14
  75.7 0.1 select_add_fusion.2
  75.8 3.6 %collective-permute-start.20 = (f32[2,512]{1,0:T(2,128)S(1)}, f32[2,512]{1,0:T(2,128)S(1)}, u32[]{:S(2)}, u32[]{:S(2)}) collective-permute-start(f32[2,512]{1,0:T(2,128)S(1)} %select_add_fusion.2), channel_id=1, source_target_pairs={{0,8},{1,9},{2,10},{3,11},{4,12},{5,13},{6,14},{7,15},{8,0},{9,1},... | collective-permute-start | bytes 12296 | tf_op jit(solution)/shard_map/ppermute | solution.py:41
  79.4 1.0 collective-permute-done.20
  80.4 1.4 %collective-permute-done.21 = f32[2,512]{1,0:T(2,128)S(1)} collective-permute-done((f32[2,512]{1,0:T(2,128)S(1)}, f32[2,512]{1,0:T(2,128)S(1)}, u32[]{:S(2)}, u32[]{:S(2)}) %collective-permute-start.21) | collective-permute-done | bytes 4128 | tf_op jit(solution)/shard_map/ppermute | solution.py:41
  81.8 0.1 add_multiply_fusion.1
  81.9 3.9 %collective-permute-start.26 = (bf16[960,512]{1,0:T(8,128)(2,1)S(1)}, bf16[960,512]{1,0:T(8,128)(2,1)S(1)}, u32[]{:S(2)}, u32[]{:S(2)}) collective-permute-start(bf16[960,512]{1,0:T(8,128)(2,1)S(1)} %constant_dynamic-update-slice_fusion.mine_ref), channel_id=1, source_target_pairs={{0,4},{1,5},{2,6},{3,7},{4,8},{5,9},{6,10},{7,11},{8,12},{9,13},{1... | collective-permute-start | bytes 2949128 | tf_op jit(solution)/shard_map/ppermute | solution.py:41
  85.9 0.1 select_add_fusion.1
  85.9 0.8 collective-permute-start.22
  86.7 2.6 %collective-permute-start.23 = (f32[2,512]{1,0:T(2,128)S(1)}, f32[2,512]{1,0:T(2,128)S(1)}, u32[]{:S(2)}, u32[]{:S(2)}) collective-permute-start(f32[2,512]{1,0:T(2,128)S(1)} %select_add_fusion.1), channel_id=1, source_target_pairs={{0,2},{1,3},{2,0},{3,1},{4,6},{5,7},{6,4},{7,5},{8,10},{9,11},{10,... | collective-permute-start | bytes 12296 | tf_op jit(solution)/shard_map/ppermute | solution.py:41
  89.3 2.5 %collective-permute-start.25 = (bf16[960,512]{1,0:T(8,128)(2,1)S(1)}, bf16[960,512]{1,0:T(8,128)(2,1)S(1)}, u32[]{:S(2)}, u32[]{:S(2)}) collective-permute-start(bf16[960,512]{1,0:T(8,128)(2,1)S(1)} %collective-permute-done.14.swap_ref), channel_id=1, source_target_pairs={{0,4},{1,5},{2,6},{3,7},{4,8},{5,9},{6,10},{7,11},{8,12},{9,13},{1... | collective-permute-start | bytes 2949128 | tf_op jit(solution)/shard_map/ppermute | solution.py:41
  91.8 0.2 collective-permute-done.24
  92.0 0.1 select_add_fusion.stat_ref
  92.1 4.9 %collective-permute-done.26.near_ref = bf16[960,512]{1,0:T(8,128)(2,1)S(1)} collective-permute-done((bf16[960,512]{1,0:T(8,128)(2,1)S(1)}, bf16[960,512]{1,0:T(8,128)(2,1)S(1)}, u32[]{:S(2)}, u32[]{:S(2)}) %collective-permute-start.26) | collective-permute-done | bytes 983072 | tf_op jit(solution)/shard_map/ppermute | solution.py:41
  97.1 8.8 %own.1 = (bf16[480,512]{1,0:T(8,128)(2,1)S(1)}, bf16[480,512]{1,0:T(8,128)(2,1)S(1)}, f32[480,512]{1,0:T(8,128)S(1)}, f32[480,512]{1,0:T(8,128)S(1)}, f32[480,128]{1,0:T(8,128)S(1)}, /*index=5*/f32[480,128]{1,0:T(8,128)S(1)}) custom-call(s32[6]{0:T(128)S(1)} %stack.64.flags, f32[2,512]{1,0:T(2,128)S(1)} %select_add_fusion.stat_ref, ...), custom_call_target="tpu_custom_call" | custom-call | flops 6000000000 | bytes 8000000 | tf_op jit(solution)/shard_map/own/pallas_call | solution.py:492
  105.8 1.8 %collective-permute-done.25.far_ref = bf16[960,512]{1,0:T(8,128)(2,1)S(1)} collective-permute-done((bf16[960,512]{1,0:T(8,128)(2,1)S(1)}, bf16[960,512]{1,0:T(8,128)(2,1)S(1)}, u32[]{:S(2)}, u32[]{:S(2)}) %collective-permute-start.25) | collective-permute-done | bytes 983072 | tf_op jit(solution)/shard_map/ppermute | solution.py:41
  107.6 5.2 %collective-permute-start.27 = (bf16[960,512]{1,0:T(8,128)(2,1)S(1)}, bf16[960,512]{1,0:T(8,128)(2,1)S(1)}, u32[]{:S(2)}, u32[]{:S(2)}) collective-permute-start(bf16[960,512]{1,0:T(8,128)(2,1)S(1)} %collective-permute-done.25.far_ref), channel_id=1, source_target_pairs={{0,64},{1,65},{2,66},{3,67},{4,68},{5,69},{6,70},{7,71},{8,72},{9,... | collective-permute-start | bytes 2949128 | tf_op jit(solution)/shard_map/ppermute | solution.py:41
  112.7 2.2 %collective-permute-done.27.relay_ref = bf16[960,512]{1,0:T(8,128)(2,1)S(1)} collective-permute-done((bf16[960,512]{1,0:T(8,128)(2,1)S(1)}, bf16[960,512]{1,0:T(8,128)(2,1)S(1)}, u32[]{:S(2)}, u32[]{:S(2)}) %collective-permute-start.27) | collective-permute-done | bytes 983072 | tf_op jit(solution)/shard_map/ppermute | solution.py:41
  114.9 4.0 %tail1.1 = bf16[480,512]{1,0:T(8,128)(2,1)S(1)} custom-call(s32[6]{0:T(128)S(1)} %stack.64.flags, f32[2,512]{1,0:T(2,128)S(1)} %select_add_fusion.stat_ref, f32[6,512]{1,0:T(8,128)S(1)} %get-tuple-element.29.vector_ref, bf16[960,512]{1,0:T(8,128)(2,1)S(1)} %collective-permute-done.25.far_ref, bf16[960,512]{1,0:T(8,128)(2,1)S(1)} %collective-permute-done.27.relay_ref, ...), custom_call_target="tpu_custom_call" | custom-call | flops 3000000000 | bytes 5000000 | tf_op jit(solution)/shard_map/tail1/pallas_call | solution.py:505
  119.0 2.3 %collective-permute-start.29 = (bf16[480,512]{1,0:T(8,128)(2,1)S(1)}, bf16[480,512]{1,0:T(8,128)(2,1)S(1)}, u32[]{:S(2)}, u32[]{:S(2)}) collective-permute-start(bf16[480,512]{1,0:T(8,128)(2,1)S(1)} %tail1.1), channel_id=1, source_target_pairs={{0,1},{1,0},{2,65},{3,64},{4,5},{5,4},{6,69},{7,68},{8,9},{9,8},{1... | collective-permute-start | bytes 1474568 | tf_op jit(solution)/shard_map/ppermute | solution.py:41
  121.3 4.0 %tail0.1 = bf16[480,512]{1,0:T(8,128)(2,1)S(1)} custom-call(s32[6]{0:T(128)S(1)} %stack.64.flags, f32[2,512]{1,0:T(2,128)S(1)} %select_add_fusion.stat_ref, f32[6,512]{1,0:T(8,128)S(1)} %get-tuple-element.29.vector_ref, bf16[960,512]{1,0:T(8,128)(2,1)S(1)} %collective-permute-done.25.far_ref, bf16[960,512]{1,0:T(8,128)(2,1)S(1)} %collective-permute-done.27.relay_ref, ...), custom_call_target="tpu_custom_call" | custom-call | flops 3000000000 | bytes 5000000 | tf_op jit(solution)/shard_map/tail0/pallas_call | solution.py:505
  125.3 2.5 %collective-permute-start.28 = (bf16[480,512]{1,0:T(8,128)(2,1)S(1)}, bf16[480,512]{1,0:T(8,128)(2,1)S(1)}, u32[]{:S(2)}, u32[]{:S(2)}) collective-permute-start(bf16[480,512]{1,0:T(8,128)(2,1)S(1)} %tail0.1), channel_id=1, source_target_pairs={{0,0},{1,1},{2,64},{3,65},{4,4},{5,5},{6,68},{7,69},{8,8},{9,9},{1... | collective-permute-start | bytes 1474568 | tf_op jit(solution)/shard_map/ppermute | solution.py:41
  127.8 0.7 collective-permute-done.29.back1_ref
  128.5 8.5 %collective-permute-done.28.back0_ref = bf16[480,512]{1,0:T(8,128)(2,1)S(1)} collective-permute-done((bf16[480,512]{1,0:T(8,128)(2,1)S(1)}, bf16[480,512]{1,0:T(8,128)(2,1)S(1)}, u32[]{:S(2)}, u32[]{:S(2)}) %collective-permute-start.28) | collective-permute-done | bytes 491552 | tf_op jit(solution)/shard_map/ppermute | solution.py:41
  137.0 1.6 %place.1 = bf16[2,480,512]{2,1,0:T(8,128)(2,1)} custom-call(s32[6]{0:T(128)S(1)} %stack.64.flags, bf16[480,512]{1,0:T(8,128)(2,1)S(1)} %collective-permute-done.28.back0_ref, bf16[480,512]{1,0:T(8,128)(2,1)S(1)} %collective-permute-done.29.back1_ref), custom_call_target="tpu_custom_call" | custom-call | tf_op jit(solution)/shard_map/place/pallas_call | solution.py:531
  (40 shorter events, 0.4 us)
Async XLA Ops:
  0.0 4.4 %collective-permute-start = (bf16[2,2,240,512]{3,2,1,0:T(8,128)(2,1)}, bf16[2,2,240,512]{3,2,1,0:T(8,128)(2,1)S(1)}, u32[]{:S(2)}, u32[]{:S(2)}) collective-permute-start(bf16[2,2,240,512]{3,2,1,0:T(8,128)(2,1)} %param.12), channel_id=1, source_target_pairs={{0,64},{1,65},{2,66},{3,67},{4,68},{5,69},{6,70},{7,71},{8,72},{9,... | collective-permute-start | bytes 2949128 | tf_op jit(solution)/shard_map/ppermute | solution.py:41
  1.5 1.2 copy-start
  6.0 12.1 %collective-permute-start.2 = (f32[2,512]{1,0:T(2,128)S(1)}, f32[2,512]{1,0:T(2,128)S(1)}, u32[]{:S(2)}, u32[]{:S(2)}) collective-permute-start(f32[2,512]{1,0:T(2,128)S(1)} %get-tuple-element.27), channel_id=1, source_target_pairs={{0,16},{1,17},{2,18},{3,19},{4,20},{5,21},{6,22},{7,23},{8,24},{9,... | collective-permute-start | bytes 12296 | tf_op jit(solution)/shard_map/ppermute | solution.py:41
  7.7 10.4 %collective-permute-start.3 = (f32[2,512]{1,0:T(2,128)S(1)}, f32[2,512]{1,0:T(2,128)S(1)}, u32[]{:S(2)}, u32[]{:S(2)}) collective-permute-start(f32[2,512]{1,0:T(2,128)S(1)} %get-tuple-element.27), channel_id=1, source_target_pairs={{0,32},{1,33},{2,34},{3,35},{4,36},{5,37},{6,38},{7,39},{8,40},{9,... | collective-permute-start | bytes 12296 | tf_op jit(solution)/shard_map/ppermute | solution.py:41
  8.9 9.3 %collective-permute-start.4 = (f32[2,512]{1,0:T(2,128)S(1)}, f32[2,512]{1,0:T(2,128)S(1)}, u32[]{:S(2)}, u32[]{:S(2)}) collective-permute-start(f32[2,512]{1,0:T(2,128)S(1)} %get-tuple-element.27), channel_id=1, source_target_pairs={{0,48},{1,49},{2,50},{3,51},{4,52},{5,53},{6,54},{7,55},{8,56},{9,... | collective-permute-start | bytes 12296 | tf_op jit(solution)/shard_map/ppermute | solution.py:41
  10.8 18.6 %collective-permute-start.1 = (bf16[4,240,512]{2,1,0:T(8,128)(2,1)S(1)}, bf16[4,240,512]{2,1,0:T(8,128)(2,1)S(1)}, u32[]{:S(2)}, u32[]{:S(2)}) collective-permute-start(bf16[4,240,512]{2,1,0:T(8,128)(2,1)S(1)} %get-tuple-element.26), channel_id=1, source_target_pairs={{0,1},{1,2},{2,3},{3,4},{4,5},{5,6},{6,7},{7,8},{8,9},{9,10},{10,1... | collective-permute-start | bytes 2949128 | tf_op jit(solution)/shard_map/ppermute | solution.py:41
  18.3 4.0 %collective-permute-start.5 = (f32[2,512]{1,0:T(2,128)S(1)}, f32[2,512]{1,0:T(2,128)S(1)}, u32[]{:S(2)}, u32[]{:S(2)}) collective-permute-start(f32[2,512]{1,0:T(2,128)S(1)} %select_add_fusion.6), channel_id=1, source_target_pairs={{0,4},{1,5},{2,6},{3,7},{4,8},{5,9},{6,10},{7,11},{8,12},{9,13},{1... | collective-permute-start | bytes 12296 | tf_op jit(solution)/shard_map/ppermute | solution.py:41
  18.3 4.3 %collective-permute-start.6 = (f32[2,512]{1,0:T(2,128)S(1)}, f32[2,512]{1,0:T(2,128)S(1)}, u32[]{:S(2)}, u32[]{:S(2)}) collective-permute-start(f32[2,512]{1,0:T(2,128)S(1)} %select_add_fusion.6), channel_id=1, source_target_pairs={{0,8},{1,9},{2,10},{3,11},{4,12},{5,13},{6,14},{7,15},{8,0},{9,1},... | collective-permute-start | bytes 12296 | tf_op jit(solution)/shard_map/ppermute | solution.py:41
  19.6 9.8 %collective-permute-start.7 = (f32[2,512]{1,0:T(2,128)S(1)}, f32[2,512]{1,0:T(2,128)S(1)}, u32[]{:S(2)}, u32[]{:S(2)}) collective-permute-start(f32[2,512]{1,0:T(2,128)S(1)} %select_add_fusion.6), channel_id=1, source_target_pairs={{0,12},{1,13},{2,14},{3,15},{4,0},{5,1},{6,2},{7,3},{8,4},{9,5},{1... | collective-permute-start | bytes 12296 | tf_op jit(solution)/shard_map/ppermute | solution.py:41
  29.5 8.0 %collective-permute-start.11 = (bf16[4,240,512]{2,1,0:T(8,128)(2,1)S(1)}, bf16[4,240,512]{2,1,0:T(8,128)(2,1)S(1)}, u32[]{:S(2)}, u32[]{:S(2)}) collective-permute-start(bf16[4,240,512]{2,1,0:T(8,128)(2,1)S(1)} %collective-permute-done.1.edge_ref), channel_id=1, source_target_pairs={{0,64},{1,65},{2,66},{3,67},{4,68},{5,69},{6,70},{7,71},{8,72},{9,... | collective-permute-start | bytes 2949128 | tf_op jit(solution)/shard_map/ppermute | solution.py:41
  31.9 2.5 %collective-permute-start.10 = (f32[2,512]{1,0:T(2,128)S(1)}, f32[2,512]{1,0:T(2,128)S(1)}, u32[]{:S(2)}, u32[]{:S(2)}) collective-permute-start(f32[2,512]{1,0:T(2,128)S(1)} %select_add_fusion.5), channel_id=1, source_target_pairs={{0,3},{1,0},{2,1},{3,2},{4,7},{5,4},{6,5},{7,6},{8,11},{9,8},{10,9... | collective-permute-start | bytes 12296 | tf_op jit(solution)/shard_map/ppermute | solution.py:41
  32.6 3.7 %collective-permute-start.8 = (f32[2,512]{1,0:T(2,128)S(1)}, f32[2,512]{1,0:T(2,128)S(1)}, u32[]{:S(2)}, u32[]{:S(2)}) collective-permute-start(f32[2,512]{1,0:T(2,128)S(1)} %select_add_fusion.5), channel_id=1, source_target_pairs={{0,1},{1,2},{2,3},{3,0},{4,5},{5,6},{6,7},{7,4},{8,9},{9,10},{10,1... | collective-permute-start | bytes 12296 | tf_op jit(solution)/shard_map/ppermute | solution.py:41
  33.4 4.0 %collective-permute-start.9 = (f32[2,512]{1,0:T(2,128)S(1)}, f32[2,512]{1,0:T(2,128)S(1)}, u32[]{:S(2)}, u32[]{:S(2)}) collective-permute-start(f32[2,512]{1,0:T(2,128)S(1)} %select_add_fusion.5), channel_id=1, source_target_pairs={{0,2},{1,3},{2,0},{3,1},{4,6},{5,7},{6,4},{7,5},{8,10},{9,11},{10,... | collective-permute-start | bytes 12296 | tf_op jit(solution)/shard_map/ppermute | solution.py:41
  37.5 59.6 %copy-start.1 = (bf16[512,512]{1,0:T(8,128)(2,1)S(1)}, bf16[512,512]{1,0:T(8,128)(2,1)}, u32[]{:S(2)}) copy-start(bf16[512,512]{1,0:T(8,128)(2,1)} %wq_ref.1) | copy-start | bytes 1572868
  37.5 59.6 %copy-start.2 = (bf16[512,512]{1,0:T(8,128)(2,1)S(1)}, bf16[512,512]{1,0:T(8,128)(2,1)}, u32[]{:S(2)}) copy-start(bf16[512,512]{1,0:T(8,128)(2,1)} %wk_ref.1) | copy-start | bytes 1572868
  55.2 59.8 %copy-start.3 = (bf16[512,512]{1,0:T(8,128)(2,1)S(1)}, bf16[512,512]{1,0:T(8,128)(2,1)}, u32[]{:S(2)}) copy-start(bf16[512,512]{1,0:T(8,128)(2,1)} %wv_ref.3) | copy-start | bytes 1572868
  55.2 59.7 %copy-start.4 = (bf16[512,512]{1,0:T(8,128)(2,1)S(1)}, bf16[512,512]{1,0:T(8,128)(2,1)}, u32[]{:S(2)}) copy-start(bf16[512,512]{1,0:T(8,128)(2,1)} %wo_ref.3) | copy-start | bytes 1572868
  56.8 6.2 %collective-permute-start.15 = (f32[2,512]{1,0:T(2,128)S(1)}, f32[2,512]{1,0:T(2,128)S(1)}, u32[]{:S(2)}, u32[]{:S(2)}) collective-permute-start(f32[2,512]{1,0:T(2,128)S(1)} %stats.1), channel_id=1, source_target_pairs={{0,64},{1,65},{2,66},{3,67},{4,68},{5,69},{6,70},{7,71},{8,72},{9,... | collective-permute-start | bytes 12296 | tf_op jit(solution)/shard_map/ppermute | solution.py:41
  58.6 15.5 %collective-permute-start.12 = (bf16[480,512]{1,0:T(8,128)(2,1)S(1)}, bf16[480,512]{1,0:T(8,128)(2,1)S(1)}, u32[]{:S(2)}, u32[]{:S(2)}) collective-permute-start(bf16[480,512]{1,0:T(8,128)(2,1)S(1)} %get-tuple-element.31), channel_id=1, source_target_pairs={{0,0},{1,1},{2,64},{3,65},{4,4},{5,5},{6,68},{7,69},{8,8},{9,9},{1... | collective-permute-start | bytes 1474568 | tf_op jit(solution)/shard_map/ppermute | solution.py:41
  60.7 14.8 %collective-permute-start.13 = (bf16[480,512]{1,0:T(8,128)(2,1)S(1)}, bf16[480,512]{1,0:T(8,128)(2,1)S(1)}, u32[]{:S(2)}, u32[]{:S(2)}) collective-permute-start(bf16[480,512]{1,0:T(8,128)(2,1)S(1)} %get-tuple-element.32), channel_id=1, source_target_pairs={{0,1},{1,0},{2,65},{3,64},{4,5},{5,4},{6,69},{7,68},{8,9},{9,8},{1... | collective-permute-start | bytes 1474568 | tf_op jit(solution)/shard_map/ppermute | solution.py:41
  63.1 2.8 %collective-permute-start.16 = (f32[2,512]{1,0:T(2,128)S(1)}, f32[2,512]{1,0:T(2,128)S(1)}, u32[]{:S(2)}, u32[]{:S(2)}) collective-permute-start(f32[2,512]{1,0:T(2,128)S(1)} %select_add_fusion.3), channel_id=1, source_target_pairs={{0,16},{1,17},{2,18},{3,19},{4,20},{5,21},{6,22},{7,23},{8,24},{9,... | collective-permute-start | bytes 12296 | tf_op jit(solution)/shard_map/ppermute | solution.py:41
  63.3 4.0 %collective-permute-start.17 = (f32[2,512]{1,0:T(2,128)S(1)}, f32[2,512]{1,0:T(2,128)S(1)}, u32[]{:S(2)}, u32[]{:S(2)}) collective-permute-start(f32[2,512]{1,0:T(2,128)S(1)} %select_add_fusion.3), channel_id=1, source_target_pairs={{0,32},{1,33},{2,34},{3,35},{4,36},{5,37},{6,38},{7,39},{8,40},{9,... | collective-permute-start | bytes 12296 | tf_op jit(solution)/shard_map/ppermute | solution.py:41
  65.2 2.8 %collective-permute-start.18 = (f32[2,512]{1,0:T(2,128)S(1)}, f32[2,512]{1,0:T(2,128)S(1)}, u32[]{:S(2)}, u32[]{:S(2)}) collective-permute-start(f32[2,512]{1,0:T(2,128)S(1)} %select_add_fusion.3), channel_id=1, source_target_pairs={{0,48},{1,49},{2,50},{3,51},{4,52},{5,53},{6,54},{7,55},{8,56},{9,... | collective-permute-start | bytes 12296 | tf_op jit(solution)/shard_map/ppermute | solution.py:41
  75.5 10.4 %collective-permute-start.14 = (bf16[960,512]{1,0:T(8,128)(2,1)S(1)}, bf16[960,512]{1,0:T(8,128)(2,1)S(1)}, u32[]{:S(2)}, u32[]{:S(2)}) collective-permute-start(bf16[960,512]{1,0:T(8,128)(2,1)S(1)} %constant_dynamic-update-slice_fusion.mine_ref), channel_id=1, source_target_pairs={{0,64},{1,65},{2,66},{3,67},{4,68},{5,69},{6,70},{7,71},{8,72},{9,... | collective-permute-start | bytes 2949128 | tf_op jit(solution)/shard_map/ppermute | solution.py:41
  75.7 3.7 %collective-permute-start.19 = (f32[2,512]{1,0:T(2,128)S(1)}, f32[2,512]{1,0:T(2,128)S(1)}, u32[]{:S(2)}, u32[]{:S(2)}) collective-permute-start(f32[2,512]{1,0:T(2,128)S(1)} %select_add_fusion.2), channel_id=1, source_target_pairs={{0,4},{1,5},{2,6},{3,7},{4,8},{5,9},{6,10},{7,11},{8,12},{9,13},{1... | collective-permute-start | bytes 12296 | tf_op jit(solution)/shard_map/ppermute | solution.py:41
  75.8 4.7 %collective-permute-start.20 = (f32[2,512]{1,0:T(2,128)S(1)}, f32[2,512]{1,0:T(2,128)S(1)}, u32[]{:S(2)}, u32[]{:S(2)}) collective-permute-start(f32[2,512]{1,0:T(2,128)S(1)} %select_add_fusion.2), channel_id=1, source_target_pairs={{0,8},{1,9},{2,10},{3,11},{4,12},{5,13},{6,14},{7,15},{8,0},{9,1},... | collective-permute-start | bytes 12296 | tf_op jit(solution)/shard_map/ppermute | solution.py:41
  79.4 2.5 %collective-permute-start.21 = (f32[2,512]{1,0:T(2,128)S(1)}, f32[2,512]{1,0:T(2,128)S(1)}, u32[]{:S(2)}, u32[]{:S(2)}) collective-permute-start(f32[2,512]{1,0:T(2,128)S(1)} %select_add_fusion.2), channel_id=1, source_target_pairs={{0,12},{1,13},{2,14},{3,15},{4,0},{5,1},{6,2},{7,3},{8,4},{9,5},{1... | collective-permute-start | bytes 12296 | tf_op jit(solution)/shard_map/ppermute | solution.py:41
  81.9 15.1 %collective-permute-start.26 = (bf16[960,512]{1,0:T(8,128)(2,1)S(1)}, bf16[960,512]{1,0:T(8,128)(2,1)S(1)}, u32[]{:S(2)}, u32[]{:S(2)}) collective-permute-start(bf16[960,512]{1,0:T(8,128)(2,1)S(1)} %constant_dynamic-update-slice_fusion.mine_ref), channel_id=1, source_target_pairs={{0,4},{1,5},{2,6},{3,7},{4,8},{5,9},{6,10},{7,11},{8,12},{9,13},{1... | collective-permute-start | bytes 2949128 | tf_op jit(solution)/shard_map/ppermute | solution.py:41
  85.9 5.8 %collective-permute-start.22 = (f32[2,512]{1,0:T(2,128)S(1)}, f32[2,512]{1,0:T(2,128)S(1)}, u32[]{:S(2)}, u32[]{:S(2)}) collective-permute-start(f32[2,512]{1,0:T(2,128)S(1)} %select_add_fusion.1), channel_id=1, source_target_pairs={{0,1},{1,2},{2,3},{3,0},{4,5},{5,6},{6,7},{7,4},{8,9},{9,10},{10,1... | collective-permute-start | bytes 12296 | tf_op jit(solution)/shard_map/ppermute | solution.py:41
  86.7 5.1 %collective-permute-start.23 = (f32[2,512]{1,0:T(2,128)S(1)}, f32[2,512]{1,0:T(2,128)S(1)}, u32[]{:S(2)}, u32[]{:S(2)}) collective-permute-start(f32[2,512]{1,0:T(2,128)S(1)} %select_add_fusion.1), channel_id=1, source_target_pairs={{0,2},{1,3},{2,0},{3,1},{4,6},{5,7},{6,4},{7,5},{8,10},{9,11},{10,... | collective-permute-start | bytes 12296 | tf_op jit(solution)/shard_map/ppermute | solution.py:41
  89.3 2.8 %collective-permute-start.24 = (f32[2,512]{1,0:T(2,128)S(1)}, f32[2,512]{1,0:T(2,128)S(1)}, u32[]{:S(2)}, u32[]{:S(2)}) collective-permute-start(f32[2,512]{1,0:T(2,128)S(1)} %select_add_fusion.1), channel_id=1, source_target_pairs={{0,3},{1,0},{2,1},{3,2},{4,7},{5,4},{6,5},{7,6},{8,11},{9,8},{10,9... | collective-permute-start | bytes 12296 | tf_op jit(solution)/shard_map/ppermute | solution.py:41
  89.3 18.3 %collective-permute-start.25 = (bf16[960,512]{1,0:T(8,128)(2,1)S(1)}, bf16[960,512]{1,0:T(8,128)(2,1)S(1)}, u32[]{:S(2)}, u32[]{:S(2)}) collective-permute-start(bf16[960,512]{1,0:T(8,128)(2,1)S(1)} %collective-permute-done.14.swap_ref), channel_id=1, source_target_pairs={{0,4},{1,5},{2,6},{3,7},{4,8},{5,9},{6,10},{7,11},{8,12},{9,13},{1... | collective-permute-start | bytes 2949128 | tf_op jit(solution)/shard_map/ppermute | solution.py:41
  107.6 7.4 %collective-permute-start.27 = (bf16[960,512]{1,0:T(8,128)(2,1)S(1)}, bf16[960,512]{1,0:T(8,128)(2,1)S(1)}, u32[]{:S(2)}, u32[]{:S(2)}) collective-permute-start(bf16[960,512]{1,0:T(8,128)(2,1)S(1)} %collective-permute-done.25.far_ref), channel_id=1, source_target_pairs={{0,64},{1,65},{2,66},{3,67},{4,68},{5,69},{6,70},{7,71},{8,72},{9,... | collective-permute-start | bytes 2949128 | tf_op jit(solution)/shard_map/ppermute | solution.py:41
  119.0 9.5 %collective-permute-start.29 = (bf16[480,512]{1,0:T(8,128)(2,1)S(1)}, bf16[480,512]{1,0:T(8,128)(2,1)S(1)}, u32[]{:S(2)}, u32[]{:S(2)}) collective-permute-start(bf16[480,512]{1,0:T(8,128)(2,1)S(1)} %tail1.1), channel_id=1, source_target_pairs={{0,1},{1,0},{2,65},{3,64},{4,5},{5,4},{6,69},{7,68},{8,9},{9,8},{1... | collective-permute-start | bytes 1474568 | tf_op jit(solution)/shard_map/ppermute | solution.py:41
  125.3 11.7 %collective-permute-start.28 = (bf16[480,512]{1,0:T(8,128)(2,1)S(1)}, bf16[480,512]{1,0:T(8,128)(2,1)S(1)}, u32[]{:S(2)}, u32[]{:S(2)}) collective-permute-start(bf16[480,512]{1,0:T(8,128)(2,1)S(1)} %tail0.1), channel_id=1, source_target_pairs={{0,0},{1,1},{2,64},{3,65},{4,4},{5,5},{6,68},{7,69},{8,8},{9,9},{1... | collective-permute-start | bytes 1474568 | tf_op jit(solution)/shard_map/ppermute | solution.py:41

commit v5 on v4

--- a/solution.py
+++ b/solution.py
@@ -362,10 +362,16 @@
     out_ref[...] = (own + vector_ref[5:6, :] + result).astype(BF)
 
 
-def place_kernel(flags, back0_ref, back1_ref, out_ref):
+def place_kernel(flags, back0_ref, back1_ref, out_hbm, sems):
     odd = flags[1]
-    out_ref[odd] = back0_ref[...]
-    out_ref[1 - odd] = back1_ref[...]
+    copies = [
+        pltpu.make_async_copy(back0_ref, out_hbm.at[odd], sems.at[0]),
+        pltpu.make_async_copy(back1_ref, out_hbm.at[1 - odd], sems.at[1]),
+    ]
+    for copy in copies:
+        copy.start()
+    for copy in copies:
+        copy.wait()
 
 
 def whole():
@@ -532,7 +538,8 @@
         place_kernel,
         out_shape=jax.ShapeDtypeStruct((frames, cells, chans), BF),
         in_specs=[flag_spec(), whole(), whole()],
-        out_specs=whole(),
+        out_specs=remote(),
+        scratch_shapes=[pltpu.SemaphoreType.DMA((2,))],
         compiler_params=params(8),
         name="place",
     )(flags, back0, back1)

time: 139 us -> 139 us (level)
  no operation moved by 1% of the time
where the time goes in v5:
time: 139 us
  starting transfers between devices  51.4 us (37%)
  waiting for transfers between devices  42.9 us (31%)
  Pallas kernels  40.8 us (29%)
  local copies, waits for them, and re-layouts  2.15 us (2%)
    ppermute x30, starting transfers between devices, send(): return lax.ppermute(value, AXES, pairs_of(move))  51.4 us
    ppermute x30, waiting for transfers between devices, send(): return lax.ppermute(value, AXES, pairs_of(move))  42.9 us
    pallas_call x1, Pallas kernels, shards(): pl.pallas_call(conv_kernel, out_shape=(piece, piece), in_specs=[flag_spec...  17.7 us
    pallas_call x1, Pallas kernels, shards(): pl.pallas_call(own_kernel, out_shape=(piece, piece, acc_shape, acc_shape,...  8.76 us
    pallas_call x2, Pallas kernels, tail(): pl.pallas_call(functools.partial(tail_kernel, order), out_shape=piece, in...  8.04 us
  transfers between devices with their start and end apart: 30, of which 19 were waited for; matrix products, arithmetic and copies ran while one was open for 1% of the time, Pallas kernels for 10%

profile of v5, /device:TPU:33, one launch (start us, length us, event | category | flops | bytes accessed | tf_op | source)
XLA Modules:
  0.0 138.7 jit_solution(10145150997311020270)
XLA Ops:
  0.0 0.7 collective-permute-start
  0.7 0.1 stack.64.flags
  0.8 0.8 stack.71.few_ref
  1.6 1.2 copy-done
  2.8 1.6 %first.1 = (f32[2,512]{1,0:T(2,128)S(1)}, bf16[4,240,512]{2,1,0:T(8,128)(2,1)S(1)}, f32[6,512]{1,0:T(8,128)S(1)}) custom-call(s32[6]{0:T(128)S(1)} %stack.64.flags, bf16[4,240,512]{2,1,0:T(8,128)(2,1)S(1)} %bitcast.26, f32[6,512]{1,0:T(8,128)S(1)} %stack.71.few_ref), custom_call_target="tpu_custom_call" | custom-call | tf_op jit(solution)/shard_map/first/pallas_call | solution.py:435
  4.4 1.6 %edges.1 = (f32[2,512]{1,0:T(2,128)S(1)}, bf16[4,240,512]{2,1,0:T(8,128)(2,1)S(1)}) custom-call(s32[6]{0:T(128)S(1)} %stack.64.flags, bf16[4,240,512]{2,1,0:T(8,128)(2,1)S(1)} %get-tuple-element.24.feat_ref, bf16[4,240,512]{2,1,0:T(8,128)(2,1)S(1)} %bitcast.27, f32[2,512]{1,0:T(2,128)S(1)} %get-tuple-element.25.first_ref), custom_call_target="tpu_custom_call" | custom-call | tf_op jit(solution)/shard_map/edges/pallas_call | solution.py:443
  6.0 1.7 %collective-permute-start.2 = (f32[2,512]{1,0:T(2,128)S(1)}, f32[2,512]{1,0:T(2,128)S(1)}, u32[]{:S(2)}, u32[]{:S(2)}) collective-permute-start(f32[2,512]{1,0:T(2,128)S(1)} %get-tuple-element.27), channel_id=1, source_target_pairs={{0,16},{1,17},{2,18},{3,19},{4,20},{5,21},{6,22},{7,23},{8,24},{9,... | collective-permute-start | bytes 12296 | tf_op jit(solution)/shard_map/ppermute | solution.py:41
  7.7 1.2 collective-permute-start.3
  8.9 2.0 %collective-permute-start.4 = (f32[2,512]{1,0:T(2,128)S(1)}, f32[2,512]{1,0:T(2,128)S(1)}, u32[]{:S(2)}, u32[]{:S(2)}) collective-permute-start(f32[2,512]{1,0:T(2,128)S(1)} %get-tuple-element.27), channel_id=1, source_target_pairs={{0,48},{1,49},{2,50},{3,51},{4,52},{5,53},{6,54},{7,55},{8,56},{9,... | collective-permute-start | bytes 12296 | tf_op jit(solution)/shard_map/ppermute | solution.py:41
  10.8 7.3 %collective-permute-start.1 = (bf16[4,240,512]{2,1,0:T(8,128)(2,1)S(1)}, bf16[4,240,512]{2,1,0:T(8,128)(2,1)S(1)}, u32[]{:S(2)}, u32[]{:S(2)}) collective-permute-start(bf16[4,240,512]{2,1,0:T(8,128)(2,1)S(1)} %get-tuple-element.26), channel_id=1, source_target_pairs={{0,1},{1,2},{2,3},{3,4},{4,5},{5,6},{6,7},{7,8},{8,9},{9,10},{10,1... | collective-permute-start | bytes 2949128 | tf_op jit(solution)/shard_map/ppermute | solution.py:41
  18.2 0.1 select_add_fusion.6
  18.3 1.3 collective-permute-start.6
  19.6 1.4 %collective-permute-start.7 = (f32[2,512]{1,0:T(2,128)S(1)}, f32[2,512]{1,0:T(2,128)S(1)}, u32[]{:S(2)}, u32[]{:S(2)}) collective-permute-start(f32[2,512]{1,0:T(2,128)S(1)} %select_add_fusion.6), channel_id=1, source_target_pairs={{0,12},{1,13},{2,14},{3,15},{4,0},{5,1},{6,2},{7,3},{8,4},{9,5},{1... | collective-permute-start | bytes 12296 | tf_op jit(solution)/shard_map/ppermute | solution.py:41
  20.9 1.3 collective-permute-done.5
  22.2 0.4 collective-permute-done.6
  22.6 6.7 %collective-permute-done.7 = f32[2,512]{1,0:T(2,128)S(1)} collective-permute-done((f32[2,512]{1,0:T(2,128)S(1)}, f32[2,512]{1,0:T(2,128)S(1)}, u32[]{:S(2)}, u32[]{:S(2)}) %collective-permute-start.7) | collective-permute-done | bytes 4128 | tf_op jit(solution)/shard_map/ppermute | solution.py:41
  29.3 0.1 add_multiply_fusion.5
  29.4 0.1 select_add_fusion.5
  29.5 2.4 %collective-permute-start.11 = (bf16[4,240,512]{2,1,0:T(8,128)(2,1)S(1)}, bf16[4,240,512]{2,1,0:T(8,128)(2,1)S(1)}, u32[]{:S(2)}, u32[]{:S(2)}) collective-permute-start(bf16[4,240,512]{2,1,0:T(8,128)(2,1)S(1)} %collective-permute-done.1.edge_ref), channel_id=1, source_target_pairs={{0,64},{1,65},{2,66},{3,67},{4,68},{5,69},{6,70},{7,71},{8,72},{9,... | collective-permute-start | bytes 2949128 | tf_op jit(solution)/shard_map/ppermute | solution.py:41
  31.9 0.7 collective-permute-start.10
  32.6 0.8 collective-permute-start.8
  33.4 0.4 collective-permute-start.9
  33.8 0.6 collective-permute-done.10
  34.4 1.9 %collective-permute-done.8 = f32[2,512]{1,0:T(2,128)S(1)} collective-permute-done((f32[2,512]{1,0:T(2,128)S(1)}, f32[2,512]{1,0:T(2,128)S(1)}, u32[]{:S(2)}, u32[]{:S(2)}) %collective-permute-start.8) | collective-permute-done | bytes 4128 | tf_op jit(solution)/shard_map/ppermute | solution.py:41
  36.3 1.1 collective-permute-done.9
  37.4 0.1 select_add_fusion.4.stat_ref
  37.5 17.7 %conv.1 = (bf16[480,512]{1,0:T(8,128)(2,1)S(1)}, bf16[480,512]{1,0:T(8,128)(2,1)S(1)}) custom-call(s32[6]{0:T(128)S(1)} %stack.64.flags, f32[2,512]{1,0:T(2,128)S(1)} %select_add_fusion.4.stat_ref, f32[6,512]{1,0:T(8,128)S(1)} %get-tuple-element.29.vector_ref, bf16[2,2,240,512]{3,2,1,0:T(8,128)(2,1)S(1)} %bitcast.28, ...), custom_call_target="tpu_custom_call" | custom-call | flops 13589544960 | bytes 20000000 | tf_op jit(solution)/shard_map/conv/pallas_call | solution.py:459
  55.2 1.6 %stats.1 = f32[2,512]{1,0:T(2,128)S(1)} custom-call(s32[6]{0:T(128)S(1)} %stack.64.flags, bf16[2,240,512]{2,1,0:T(8,128)(2,1)S(1)} %bitcast.30, bf16[2,240,512]{2,1,0:T(8,128)(2,1)S(1)} %bitcast.29), custom_call_target="tpu_custom_call" | custom-call | tf_op jit(solution)/shard_map/stats/pallas_call | solution.py:424
  56.8 1.8 %collective-permute-start.15 = (f32[2,512]{1,0:T(2,128)S(1)}, f32[2,512]{1,0:T(2,128)S(1)}, u32[]{:S(2)}, u32[]{:S(2)}) collective-permute-start(f32[2,512]{1,0:T(2,128)S(1)} %stats.1), channel_id=1, source_target_pairs={{0,64},{1,65},{2,66},{3,67},{4,68},{5,69},{6,70},{7,71},{8,72},{9,... | collective-permute-start | bytes 12296 | tf_op jit(solution)/shard_map/ppermute | solution.py:41
  58.6 2.1 %collective-permute-start.12 = (bf16[480,512]{1,0:T(8,128)(2,1)S(1)}, bf16[480,512]{1,0:T(8,128)(2,1)S(1)}, u32[]{:S(2)}, u32[]{:S(2)}) collective-permute-start(bf16[480,512]{1,0:T(8,128)(2,1)S(1)} %get-tuple-element.31), channel_id=1, source_target_pairs={{0,0},{1,1},{2,64},{3,65},{4,4},{5,5},{6,68},{7,69},{8,8},{9,9},{1... | collective-permute-start | bytes 1474568 | tf_op jit(solution)/shard_map/ppermute | solution.py:41
  60.7 2.3 %collective-permute-start.13 = (bf16[480,512]{1,0:T(8,128)(2,1)S(1)}, bf16[480,512]{1,0:T(8,128)(2,1)S(1)}, u32[]{:S(2)}, u32[]{:S(2)}) collective-permute-start(bf16[480,512]{1,0:T(8,128)(2,1)S(1)} %get-tuple-element.32), channel_id=1, source_target_pairs={{0,1},{1,0},{2,65},{3,64},{4,5},{5,4},{6,69},{7,68},{8,9},{9,8},{1... | collective-permute-start | bytes 1474568 | tf_op jit(solution)/shard_map/ppermute | solution.py:41
  63.0 0.1 select_add_fusion.3
  63.1 0.2 collective-permute-start.16
  63.3 1.9 %collective-permute-start.17 = (f32[2,512]{1,0:T(2,128)S(1)}, f32[2,512]{1,0:T(2,128)S(1)}, u32[]{:S(2)}, u32[]{:S(2)}) collective-permute-start(f32[2,512]{1,0:T(2,128)S(1)} %select_add_fusion.3), channel_id=1, source_target_pairs={{0,32},{1,33},{2,34},{3,35},{4,36},{5,37},{6,38},{7,39},{8,40},{9,... | collective-permute-start | bytes 12296 | tf_op jit(solution)/shard_map/ppermute | solution.py:41
  65.2 0.7 collective-permute-done.16
  65.9 1.4 collective-permute-done.17
  67.2 0.7 collective-permute-done.18
  67.9 0.1 add_multiply_fusion.2
  68.0 6.1 %collective-permute-done.12.own_ref = bf16[480,512]{1,0:T(8,128)(2,1)S(1)} collective-permute-done((bf16[480,512]{1,0:T(8,128)(2,1)S(1)}, bf16[480,512]{1,0:T(8,128)(2,1)S(1)}, u32[]{:S(2)}, u32[]{:S(2)}) %collective-permute-start.12) | collective-permute-done | bytes 491552 | tf_op jit(solution)/shard_map/ppermute | solution.py:41
  74.1 1.4 collective-permute-done.13.own_ref
  75.5 0.1 collective-permute-start.14
  75.7 0.1 select_add_fusion.2
  75.8 3.6 %collective-permute-start.20 = (f32[2,512]{1,0:T(2,128)S(1)}, f32[2,512]{1,0:T(2,128)S(1)}, u32[]{:S(2)}, u32[]{:S(2)}) collective-permute-start(f32[2,512]{1,0:T(2,128)S(1)} %select_add_fusion.2), channel_id=1, source_target_pairs={{0,8},{1,9},{2,10},{3,11},{4,12},{5,13},{6,14},{7,15},{8,0},{9,1},... | collective-permute-start | bytes 12296 | tf_op jit(solution)/shard_map/ppermute | solution.py:41
  79.4 1.0 collective-permute-done.20
  80.4 1.4 %collective-permute-done.21 = f32[2,512]{1,0:T(2,128)S(1)} collective-permute-done((f32[2,512]{1,0:T(2,128)S(1)}, f32[2,512]{1,0:T(2,128)S(1)}, u32[]{:S(2)}, u32[]{:S(2)}) %collective-permute-start.21) | collective-permute-done | bytes 4128 | tf_op jit(solution)/shard_map/ppermute | solution.py:41
  81.8 0.1 add_multiply_fusion.1
  81.9 3.9 %collective-permute-start.26 = (bf16[960,512]{1,0:T(8,128)(2,1)S(1)}, bf16[960,512]{1,0:T(8,128)(2,1)S(1)}, u32[]{:S(2)}, u32[]{:S(2)}) collective-permute-start(bf16[960,512]{1,0:T(8,128)(2,1)S(1)} %constant_dynamic-update-slice_fusion.mine_ref), channel_id=1, source_target_pairs={{0,4},{1,5},{2,6},{3,7},{4,8},{5,9},{6,10},{7,11},{8,12},{9,13},{1... | collective-permute-start | bytes 2949128 | tf_op jit(solution)/shard_map/ppermute | solution.py:41
  85.9 0.1 select_add_fusion.1
  85.9 0.8 collective-permute-start.22
  86.7 2.6 %collective-permute-start.23 = (f32[2,512]{1,0:T(2,128)S(1)}, f32[2,512]{1,0:T(2,128)S(1)}, u32[]{:S(2)}, u32[]{:S(2)}) collective-permute-start(f32[2,512]{1,0:T(2,128)S(1)} %select_add_fusion.1), channel_id=1, source_target_pairs={{0,2},{1,3},{2,0},{3,1},{4,6},{5,7},{6,4},{7,5},{8,10},{9,11},{10,... | collective-permute-start | bytes 12296 | tf_op jit(solution)/shard_map/ppermute | solution.py:41
  89.3 2.5 %collective-permute-start.25 = (bf16[960,512]{1,0:T(8,128)(2,1)S(1)}, bf16[960,512]{1,0:T(8,128)(2,1)S(1)}, u32[]{:S(2)}, u32[]{:S(2)}) collective-permute-start(bf16[960,512]{1,0:T(8,128)(2,1)S(1)} %collective-permute-done.14.swap_ref), channel_id=1, source_target_pairs={{0,4},{1,5},{2,6},{3,7},{4,8},{5,9},{6,10},{7,11},{8,12},{9,13},{1... | collective-permute-start | bytes 2949128 | tf_op jit(solution)/shard_map/ppermute | solution.py:41
  91.8 0.2 collective-permute-done.24
  92.1 4.9 %collective-permute-done.26.near_ref = bf16[960,512]{1,0:T(8,128)(2,1)S(1)} collective-permute-done((bf16[960,512]{1,0:T(8,128)(2,1)S(1)}, bf16[960,512]{1,0:T(8,128)(2,1)S(1)}, u32[]{:S(2)}, u32[]{:S(2)}) %collective-permute-start.26) | collective-permute-done | bytes 983072 | tf_op jit(solution)/shard_map/ppermute | solution.py:41
  97.1 8.8 %own.1 = (bf16[480,512]{1,0:T(8,128)(2,1)S(1)}, bf16[480,512]{1,0:T(8,128)(2,1)S(1)}, f32[480,512]{1,0:T(8,128)S(1)}, f32[480,512]{1,0:T(8,128)S(1)}, f32[480,128]{1,0:T(8,128)S(1)}, /*index=5*/f32[480,128]{1,0:T(8,128)S(1)}) custom-call(s32[6]{0:T(128)S(1)} %stack.64.flags, f32[2,512]{1,0:T(2,128)S(1)} %select_add_fusion.stat_ref, ...), custom_call_target="tpu_custom_call" | custom-call | flops 6000000000 | bytes 8000000 | tf_op jit(solution)/shard_map/own/pallas_call | solution.py:498
  105.8 1.8 %collective-permute-done.25.far_ref = bf16[960,512]{1,0:T(8,128)(2,1)S(1)} collective-permute-done((bf16[960,512]{1,0:T(8,128)(2,1)S(1)}, bf16[960,512]{1,0:T(8,128)(2,1)S(1)}, u32[]{:S(2)}, u32[]{:S(2)}) %collective-permute-start.25) | collective-permute-done | bytes 983072 | tf_op jit(solution)/shard_map/ppermute | solution.py:41
  107.6 5.2 %collective-permute-start.27 = (bf16[960,512]{1,0:T(8,128)(2,1)S(1)}, bf16[960,512]{1,0:T(8,128)(2,1)S(1)}, u32[]{:S(2)}, u32[]{:S(2)}) collective-permute-start(bf16[960,512]{1,0:T(8,128)(2,1)S(1)} %collective-permute-done.25.far_ref), channel_id=1, source_target_pairs={{0,64},{1,65},{2,66},{3,67},{4,68},{5,69},{6,70},{7,71},{8,72},{9,... | collective-permute-start | bytes 2949128 | tf_op jit(solution)/shard_map/ppermute | solution.py:41
  112.7 2.2 %collective-permute-done.27.relay_ref = bf16[960,512]{1,0:T(8,128)(2,1)S(1)} collective-permute-done((bf16[960,512]{1,0:T(8,128)(2,1)S(1)}, bf16[960,512]{1,0:T(8,128)(2,1)S(1)}, u32[]{:S(2)}, u32[]{:S(2)}) %collective-permute-start.27) | collective-permute-done | bytes 983072 | tf_op jit(solution)/shard_map/ppermute | solution.py:41
  114.9 4.0 %tail1.1 = bf16[480,512]{1,0:T(8,128)(2,1)S(1)} custom-call(s32[6]{0:T(128)S(1)} %stack.64.flags, f32[2,512]{1,0:T(2,128)S(1)} %select_add_fusion.stat_ref, f32[6,512]{1,0:T(8,128)S(1)} %get-tuple-element.29.vector_ref, bf16[960,512]{1,0:T(8,128)(2,1)S(1)} %collective-permute-done.25.far_ref, bf16[960,512]{1,0:T(8,128)(2,1)S(1)} %collective-permute-done.27.relay_ref, ...), custom_call_target="tpu_custom_call" | custom-call | flops 3000000000 | bytes 5000000 | tf_op jit(solution)/shard_map/tail1/pallas_call | solution.py:511
  119.0 2.3 %collective-permute-start.29 = (bf16[480,512]{1,0:T(8,128)(2,1)S(1)}, bf16[480,512]{1,0:T(8,128)(2,1)S(1)}, u32[]{:S(2)}, u32[]{:S(2)}) collective-permute-start(bf16[480,512]{1,0:T(8,128)(2,1)S(1)} %tail1.1), channel_id=1, source_target_pairs={{0,1},{1,0},{2,65},{3,64},{4,5},{5,4},{6,69},{7,68},{8,9},{9,8},{1... | collective-permute-start | bytes 1474568 | tf_op jit(solution)/shard_map/ppermute | solution.py:41
  121.3 4.0 %tail0.1 = bf16[480,512]{1,0:T(8,128)(2,1)S(1)} custom-call(s32[6]{0:T(128)S(1)} %stack.64.flags, f32[2,512]{1,0:T(2,128)S(1)} %select_add_fusion.stat_ref, f32[6,512]{1,0:T(8,128)S(1)} %get-tuple-element.29.vector_ref, bf16[960,512]{1,0:T(8,128)(2,1)S(1)} %collective-permute-done.25.far_ref, bf16[960,512]{1,0:T(8,128)(2,1)S(1)} %collective-permute-done.27.relay_ref, ...), custom_call_target="tpu_custom_call" | custom-call | flops 3000000000 | bytes 5000000 | tf_op jit(solution)/shard_map/tail0/pallas_call | solution.py:511
  125.3 2.5 %collective-permute-start.28 = (bf16[480,512]{1,0:T(8,128)(2,1)S(1)}, bf16[480,512]{1,0:T(8,128)(2,1)S(1)}, u32[]{:S(2)}, u32[]{:S(2)}) collective-permute-start(bf16[480,512]{1,0:T(8,128)(2,1)S(1)} %tail0.1), channel_id=1, source_target_pairs={{0,0},{1,1},{2,64},{3,65},{4,4},{5,5},{6,68},{7,69},{8,8},{9,9},{1... | collective-permute-start | bytes 1474568 | tf_op jit(solution)/shard_map/ppermute | solution.py:41
  127.8 0.7 collective-permute-done.29.back1_ref
  128.5 8.5 %collective-permute-done.28.back0_ref = bf16[480,512]{1,0:T(8,128)(2,1)S(1)} collective-permute-done((bf16[480,512]{1,0:T(8,128)(2,1)S(1)}, bf16[480,512]{1,0:T(8,128)(2,1)S(1)}, u32[]{:S(2)}, u32[]{:S(2)}) %collective-permute-start.28) | collective-permute-done | bytes 491552 | tf_op jit(solution)/shard_map/ppermute | solution.py:41
  137.0 1.5 %place.1 = bf16[2,480,512]{2,1,0:T(8,128)(2,1)} custom-call(s32[6]{0:T(128)S(1)} %stack.64.flags, bf16[480,512]{1,0:T(8,128)(2,1)S(1)} %collective-permute-done.28.back0_ref, bf16[480,512]{1,0:T(8,128)(2,1)S(1)} %collective-permute-done.29.back1_ref), custom_call_target="tpu_custom_call" | custom-call | tf_op jit(solution)/shard_map/place/pallas_call | solution.py:537
  (40 shorter events, 0.4 us)
Async XLA Ops:
  0.0 4.4 %collective-permute-start = (bf16[2,2,240,512]{3,2,1,0:T(8,128)(2,1)}, bf16[2,2,240,512]{3,2,1,0:T(8,128)(2,1)S(1)}, u32[]{:S(2)}, u32[]{:S(2)}) collective-permute-start(bf16[2,2,240,512]{3,2,1,0:T(8,128)(2,1)} %param.12), channel_id=1, source_target_pairs={{0,64},{1,65},{2,66},{3,67},{4,68},{5,69},{6,70},{7,71},{8,72},{9,... | collective-permute-start | bytes 2949128 | tf_op jit(solution)/shard_map/ppermute | solution.py:41
  1.5 1.2 copy-start
  6.0 12.1 %collective-permute-start.2 = (f32[2,512]{1,0:T(2,128)S(1)}, f32[2,512]{1,0:T(2,128)S(1)}, u32[]{:S(2)}, u32[]{:S(2)}) collective-permute-start(f32[2,512]{1,0:T(2,128)S(1)} %get-tuple-element.27), channel_id=1, source_target_pairs={{0,16},{1,17},{2,18},{3,19},{4,20},{5,21},{6,22},{7,23},{8,24},{9,... | collective-permute-start | bytes 12296 | tf_op jit(solution)/shard_map/ppermute | solution.py:41
  7.7 10.4 %collective-permute-start.3 = (f32[2,512]{1,0:T(2,128)S(1)}, f32[2,512]{1,0:T(2,128)S(1)}, u32[]{:S(2)}, u32[]{:S(2)}) collective-permute-start(f32[2,512]{1,0:T(2,128)S(1)} %get-tuple-element.27), channel_id=1, source_target_pairs={{0,32},{1,33},{2,34},{3,35},{4,36},{5,37},{6,38},{7,39},{8,40},{9,... | collective-permute-start | bytes 12296 | tf_op jit(solution)/shard_map/ppermute | solution.py:41
  8.9 9.3 %collective-permute-start.4 = (f32[2,512]{1,0:T(2,128)S(1)}, f32[2,512]{1,0:T(2,128)S(1)}, u32[]{:S(2)}, u32[]{:S(2)}) collective-permute-start(f32[2,512]{1,0:T(2,128)S(1)} %get-tuple-element.27), channel_id=1, source_target_pairs={{0,48},{1,49},{2,50},{3,51},{4,52},{5,53},{6,54},{7,55},{8,56},{9,... | collective-permute-start | bytes 12296 | tf_op jit(solution)/shard_map/ppermute | solution.py:41
  10.8 18.6 %collective-permute-start.1 = (bf16[4,240,512]{2,1,0:T(8,128)(2,1)S(1)}, bf16[4,240,512]{2,1,0:T(8,128)(2,1)S(1)}, u32[]{:S(2)}, u32[]{:S(2)}) collective-permute-start(bf16[4,240,512]{2,1,0:T(8,128)(2,1)S(1)} %get-tuple-element.26), channel_id=1, source_target_pairs={{0,1},{1,2},{2,3},{3,4},{4,5},{5,6},{6,7},{7,8},{8,9},{9,10},{10,1... | collective-permute-start | bytes 2949128 | tf_op jit(solution)/shard_map/ppermute | solution.py:41
  18.3 4.0 %collective-permute-start.5 = (f32[2,512]{1,0:T(2,128)S(1)}, f32[2,512]{1,0:T(2,128)S(1)}, u32[]{:S(2)}, u32[]{:S(2)}) collective-permute-start(f32[2,512]{1,0:T(2,128)S(1)} %select_add_fusion.6), channel_id=1, source_target_pairs={{0,4},{1,5},{2,6},{3,7},{4,8},{5,9},{6,10},{7,11},{8,12},{9,13},{1... | collective-permute-start | bytes 12296 | tf_op jit(solution)/shard_map/ppermute | solution.py:41
  18.3 4.3 %collective-permute-start.6 = (f32[2,512]{1,0:T(2,128)S(1)}, f32[2,512]{1,0:T(2,128)S(1)}, u32[]{:S(2)}, u32[]{:S(2)}) collective-permute-start(f32[2,512]{1,0:T(2,128)S(1)} %select_add_fusion.6), channel_id=1, source_target_pairs={{0,8},{1,9},{2,10},{3,11},{4,12},{5,13},{6,14},{7,15},{8,0},{9,1},... | collective-permute-start | bytes 12296 | tf_op jit(solution)/shard_map/ppermute | solution.py:41
  19.6 9.8 %collective-permute-start.7 = (f32[2,512]{1,0:T(2,128)S(1)}, f32[2,512]{1,0:T(2,128)S(1)}, u32[]{:S(2)}, u32[]{:S(2)}) collective-permute-start(f32[2,512]{1,0:T(2,128)S(1)} %select_add_fusion.6), channel_id=1, source_target_pairs={{0,12},{1,13},{2,14},{3,15},{4,0},{5,1},{6,2},{7,3},{8,4},{9,5},{1... | collective-permute-start | bytes 12296 | tf_op jit(solution)/shard_map/ppermute | solution.py:41
  29.5 8.0 %collective-permute-start.11 = (bf16[4,240,512]{2,1,0:T(8,128)(2,1)S(1)}, bf16[4,240,512]{2,1,0:T(8,128)(2,1)S(1)}, u32[]{:S(2)}, u32[]{:S(2)}) collective-permute-start(bf16[4,240,512]{2,1,0:T(8,128)(2,1)S(1)} %collective-permute-done.1.edge_ref), channel_id=1, source_target_pairs={{0,64},{1,65},{2,66},{3,67},{4,68},{5,69},{6,70},{7,71},{8,72},{9,... | collective-permute-start | bytes 2949128 | tf_op jit(solution)/shard_map/ppermute | solution.py:41
  31.9 2.5 %collective-permute-start.10 = (f32[2,512]{1,0:T(2,128)S(1)}, f32[2,512]{1,0:T(2,128)S(1)}, u32[]{:S(2)}, u32[]{:S(2)}) collective-permute-start(f32[2,512]{1,0:T(2,128)S(1)} %select_add_fusion.5), channel_id=1, source_target_pairs={{0,3},{1,0},{2,1},{3,2},{4,7},{5,4},{6,5},{7,6},{8,11},{9,8},{10,9... | collective-permute-start | bytes 12296 | tf_op jit(solution)/shard_map/ppermute | solution.py:41
  32.6 3.7 %collective-permute-start.8 = (f32[2,512]{1,0:T(2,128)S(1)}, f32[2,512]{1,0:T(2,128)S(1)}, u32[]{:S(2)}, u32[]{:S(2)}) collective-permute-start(f32[2,512]{1,0:T(2,128)S(1)} %select_add_fusion.5), channel_id=1, source_target_pairs={{0,1},{1,2},{2,3},{3,0},{4,5},{5,6},{6,7},{7,4},{8,9},{9,10},{10,1... | collective-permute-start | bytes 12296 | tf_op jit(solution)/shard_map/ppermute | solution.py:41
  33.4 4.0 %collective-permute-start.9 = (f32[2,512]{1,0:T(2,128)S(1)}, f32[2,512]{1,0:T(2,128)S(1)}, u32[]{:S(2)}, u32[]{:S(2)}) collective-permute-start(f32[2,512]{1,0:T(2,128)S(1)} %select_add_fusion.5), channel_id=1, source_target_pairs={{0,2},{1,3},{2,0},{3,1},{4,6},{5,7},{6,4},{7,5},{8,10},{9,11},{10,... | collective-permute-start | bytes 12296 | tf_op jit(solution)/shard_map/ppermute | solution.py:41
  37.5 59.6 %copy-start.1 = (bf16[512,512]{1,0:T(8,128)(2,1)S(1)}, bf16[512,512]{1,0:T(8,128)(2,1)}, u32[]{:S(2)}) copy-start(bf16[512,512]{1,0:T(8,128)(2,1)} %wq_ref.1) | copy-start | bytes 1572868
  37.5 59.6 %copy-start.2 = (bf16[512,512]{1,0:T(8,128)(2,1)S(1)}, bf16[512,512]{1,0:T(8,128)(2,1)}, u32[]{:S(2)}) copy-start(bf16[512,512]{1,0:T(8,128)(2,1)} %wk_ref.1) | copy-start | bytes 1572868
  55.2 59.8 %copy-start.3 = (bf16[512,512]{1,0:T(8,128)(2,1)S(1)}, bf16[512,512]{1,0:T(8,128)(2,1)}, u32[]{:S(2)}) copy-start(bf16[512,512]{1,0:T(8,128)(2,1)} %wv_ref.3) | copy-start | bytes 1572868
  55.2 59.7 %copy-start.4 = (bf16[512,512]{1,0:T(8,128)(2,1)S(1)}, bf16[512,512]{1,0:T(8,128)(2,1)}, u32[]{:S(2)}) copy-start(bf16[512,512]{1,0:T(8,128)(2,1)} %wo_ref.3) | copy-start | bytes 1572868
  56.8 6.2 %collective-permute-start.15 = (f32[2,512]{1,0:T(2,128)S(1)}, f32[2,512]{1,0:T(2,128)S(1)}, u32[]{:S(2)}, u32[]{:S(2)}) collective-permute-start(f32[2,512]{1,0:T(2,128)S(1)} %stats.1), channel_id=1, source_target_pairs={{0,64},{1,65},{2,66},{3,67},{4,68},{5,69},{6,70},{7,71},{8,72},{9,... | collective-permute-start | bytes 12296 | tf_op jit(solution)/shard_map/ppermute | solution.py:41
  58.6 15.5 %collective-permute-start.12 = (bf16[480,512]{1,0:T(8,128)(2,1)S(1)}, bf16[480,512]{1,0:T(8,128)(2,1)S(1)}, u32[]{:S(2)}, u32[]{:S(2)}) collective-permute-start(bf16[480,512]{1,0:T(8,128)(2,1)S(1)} %get-tuple-element.31), channel_id=1, source_target_pairs={{0,0},{1,1},{2,64},{3,65},{4,4},{5,5},{6,68},{7,69},{8,8},{9,9},{1... | collective-permute-start | bytes 1474568 | tf_op jit(solution)/shard_map/ppermute | solution.py:41
  60.7 14.8 %collective-permute-start.13 = (bf16[480,512]{1,0:T(8,128)(2,1)S(1)}, bf16[480,512]{1,0:T(8,128)(2,1)S(1)}, u32[]{:S(2)}, u32[]{:S(2)}) collective-permute-start(bf16[480,512]{1,0:T(8,128)(2,1)S(1)} %get-tuple-element.32), channel_id=1, source_target_pairs={{0,1},{1,0},{2,65},{3,64},{4,5},{5,4},{6,69},{7,68},{8,9},{9,8},{1... | collective-permute-start | bytes 1474568 | tf_op jit(solution)/shard_map/ppermute | solution.py:41
  63.1 2.8 %collective-permute-start.16 = (f32[2,512]{1,0:T(2,128)S(1)}, f32[2,512]{1,0:T(2,128)S(1)}, u32[]{:S(2)}, u32[]{:S(2)}) collective-permute-start(f32[2,512]{1,0:T(2,128)S(1)} %select_add_fusion.3), channel_id=1, source_target_pairs={{0,16},{1,17},{2,18},{3,19},{4,20},{5,21},{6,22},{7,23},{8,24},{9,... | collective-permute-start | bytes 12296 | tf_op jit(solution)/shard_map/ppermute | solution.py:41
  63.3 4.0 %collective-permute-start.17 = (f32[2,512]{1,0:T(2,128)S(1)}, f32[2,512]{1,0:T(2,128)S(1)}, u32[]{:S(2)}, u32[]{:S(2)}) collective-permute-start(f32[2,512]{1,0:T(2,128)S(1)} %select_add_fusion.3), channel_id=1, source_target_pairs={{0,32},{1,33},{2,34},{3,35},{4,36},{5,37},{6,38},{7,39},{8,40},{9,... | collective-permute-start | bytes 12296 | tf_op jit(solution)/shard_map/ppermute | solution.py:41
  65.2 2.8 %collective-permute-start.18 = (f32[2,512]{1,0:T(2,128)S(1)}, f32[2,512]{1,0:T(2,128)S(1)}, u32[]{:S(2)}, u32[]{:S(2)}) collective-permute-start(f32[2,512]{1,0:T(2,128)S(1)} %select_add_fusion.3), channel_id=1, source_target_pairs={{0,48},{1,49},{2,50},{3,51},{4,52},{5,53},{6,54},{7,55},{8,56},{9,... | collective-permute-start | bytes 12296 | tf_op jit(solution)/shard_map/ppermute | solution.py:41
  75.5 10.4 %collective-permute-start.14 = (bf16[960,512]{1,0:T(8,128)(2,1)S(1)}, bf16[960,512]{1,0:T(8,128)(2,1)S(1)}, u32[]{:S(2)}, u32[]{:S(2)}) collective-permute-start(bf16[960,512]{1,0:T(8,128)(2,1)S(1)} %constant_dynamic-update-slice_fusion.mine_ref), channel_id=1, source_target_pairs={{0,64},{1,65},{2,66},{3,67},{4,68},{5,69},{6,70},{7,71},{8,72},{9,... | collective-permute-start | bytes 2949128 | tf_op jit(solution)/shard_map/ppermute | solution.py:41
  75.7 3.7 %collective-permute-start.19 = (f32[2,512]{1,0:T(2,128)S(1)}, f32[2,512]{1,0:T(2,128)S(1)}, u32[]{:S(2)}, u32[]{:S(2)}) collective-permute-start(f32[2,512]{1,0:T(2,128)S(1)} %select_add_fusion.2), channel_id=1, source_target_pairs={{0,4},{1,5},{2,6},{3,7},{4,8},{5,9},{6,10},{7,11},{8,12},{9,13},{1... | collective-permute-start | bytes 12296 | tf_op jit(solution)/shard_map/ppermute | solution.py:41
  75.8 4.7 %collective-permute-start.20 = (f32[2,512]{1,0:T(2,128)S(1)}, f32[2,512]{1,0:T(2,128)S(1)}, u32[]{:S(2)}, u32[]{:S(2)}) collective-permute-start(f32[2,512]{1,0:T(2,128)S(1)} %select_add_fusion.2), channel_id=1, source_target_pairs={{0,8},{1,9},{2,10},{3,11},{4,12},{5,13},{6,14},{7,15},{8,0},{9,1},... | collective-permute-start | bytes 12296 | tf_op jit(solution)/shard_map/ppermute | solution.py:41
  79.4 2.5 %collective-permute-start.21 = (f32[2,512]{1,0:T(2,128)S(1)}, f32[2,512]{1,0:T(2,128)S(1)}, u32[]{:S(2)}, u32[]{:S(2)}) collective-permute-start(f32[2,512]{1,0:T(2,128)S(1)} %select_add_fusion.2), channel_id=1, source_target_pairs={{0,12},{1,13},{2,14},{3,15},{4,0},{5,1},{6,2},{7,3},{8,4},{9,5},{1... | collective-permute-start | bytes 12296 | tf_op jit(solution)/shard_map/ppermute | solution.py:41
  81.9 15.1 %collective-permute-start.26 = (bf16[960,512]{1,0:T(8,128)(2,1)S(1)}, bf16[960,512]{1,0:T(8,128)(2,1)S(1)}, u32[]{:S(2)}, u32[]{:S(2)}) collective-permute-start(bf16[960,512]{1,0:T(8,128)(2,1)S(1)} %constant_dynamic-update-slice_fusion.mine_ref), channel_id=1, source_target_pairs={{0,4},{1,5},{2,6},{3,7},{4,8},{5,9},{6,10},{7,11},{8,12},{9,13},{1... | collective-permute-start | bytes 2949128 | tf_op jit(solution)/shard_map/ppermute | solution.py:41
  85.9 5.8 %collective-permute-start.22 = (f32[2,512]{1,0:T(2,128)S(1)}, f32[2,512]{1,0:T(2,128)S(1)}, u32[]{:S(2)}, u32[]{:S(2)}) collective-permute-start(f32[2,512]{1,0:T(2,128)S(1)} %select_add_fusion.1), channel_id=1, source_target_pairs={{0,1},{1,2},{2,3},{3,0},{4,5},{5,6},{6,7},{7,4},{8,9},{9,10},{10,1... | collective-permute-start | bytes 12296 | tf_op jit(solution)/shard_map/ppermute | solution.py:41
  86.7 5.1 %collective-permute-start.23 = (f32[2,512]{1,0:T(2,128)S(1)}, f32[2,512]{1,0:T(2,128)S(1)}, u32[]{:S(2)}, u32[]{:S(2)}) collective-permute-start(f32[2,512]{1,0:T(2,128)S(1)} %select_add_fusion.1), channel_id=1, source_target_pairs={{0,2},{1,3},{2,0},{3,1},{4,6},{5,7},{6,4},{7,5},{8,10},{9,11},{10,... | collective-permute-start | bytes 12296 | tf_op jit(solution)/shard_map/ppermute | solution.py:41
  89.3 2.8 %collective-permute-start.24 = (f32[2,512]{1,0:T(2,128)S(1)}, f32[2,512]{1,0:T(2,128)S(1)}, u32[]{:S(2)}, u32[]{:S(2)}) collective-permute-start(f32[2,512]{1,0:T(2,128)S(1)} %select_add_fusion.1), channel_id=1, source_target_pairs={{0,3},{1,0},{2,1},{3,2},{4,7},{5,4},{6,5},{7,6},{8,11},{9,8},{10,9... | collective-permute-start | bytes 12296 | tf_op jit(solution)/shard_map/ppermute | solution.py:41
  89.3 18.3 %collective-permute-start.25 = (bf16[960,512]{1,0:T(8,128)(2,1)S(1)}, bf16[960,512]{1,0:T(8,128)(2,1)S(1)}, u32[]{:S(2)}, u32[]{:S(2)}) collective-permute-start(bf16[960,512]{1,0:T(8,128)(2,1)S(1)} %collective-permute-done.14.swap_ref), channel_id=1, source_target_pairs={{0,4},{1,5},{2,6},{3,7},{4,8},{5,9},{6,10},{7,11},{8,12},{9,13},{1... | collective-permute-start | bytes 2949128 | tf_op jit(solution)/shard_map/ppermute | solution.py:41
  107.6 7.4 %collective-permute-start.27 = (bf16[960,512]{1,0:T(8,128)(2,1)S(1)}, bf16[960,512]{1,0:T(8,128)(2,1)S(1)}, u32[]{:S(2)}, u32[]{:S(2)}) collective-permute-start(bf16[960,512]{1,0:T(8,128)(2,1)S(1)} %collective-permute-done.25.far_ref), channel_id=1, source_target_pairs={{0,64},{1,65},{2,66},{3,67},{4,68},{5,69},{6,70},{7,71},{8,72},{9,... | collective-permute-start | bytes 2949128 | tf_op jit(solution)/shard_map/ppermute | solution.py:41
  119.0 9.5 %collective-permute-start.29 = (bf16[480,512]{1,0:T(8,128)(2,1)S(1)}, bf16[480,512]{1,0:T(8,128)(2,1)S(1)}, u32[]{:S(2)}, u32[]{:S(2)}) collective-permute-start(bf16[480,512]{1,0:T(8,128)(2,1)S(1)} %tail1.1), channel_id=1, source_target_pairs={{0,1},{1,0},{2,65},{3,64},{4,5},{5,4},{6,69},{7,68},{8,9},{9,8},{1... | collective-permute-start | bytes 1474568 | tf_op jit(solution)/shard_map/ppermute | solution.py:41
  125.3 11.7 %collective-permute-start.28 = (bf16[480,512]{1,0:T(8,128)(2,1)S(1)}, bf16[480,512]{1,0:T(8,128)(2,1)S(1)}, u32[]{:S(2)}, u32[]{:S(2)}) collective-permute-start(bf16[480,512]{1,0:T(8,128)(2,1)S(1)} %tail0.1), channel_id=1, source_target_pairs={{0,0},{1,1},{2,64},{3,65},{4,4},{5,5},{6,68},{7,69},{8,8},{9,9},{1... | collective-permute-start | bytes 1474568 | tf_op jit(solution)/shard_map/ppermute | solution.py:41
